TPU v7x, 128 devices: a whole 4x4x4 slice. The times are simulated.
128 devices in a mesh: row: 16 (over x, y), col: 8 (over z, core).
Axes of the slice: x: 4, y: 4, z: 4, core: 2. Of those that a mesh axis runs over, the one named last changes fastest.
Arguments:
- density: bfloat16 [16384, 16384], P('row', 'col'), as said below
- block_mask: int32 [128, 128], P('row', 'col'), may hold values from 0 to 1, as said below
Outputs:
- purified_slab: float32 [1024, 16384], P('col', 'row')
Inputs may be any that keep to these rules, and one draw needn't show every extreme that they name: density is exactly symmetric. block_mask is symmetric and its diagonal is all ones.
All inputs are finite; a program needn't handle non-finite values.
Results may differ from a plain program's by a relative error of at most 0.0018.
Values may be sent and summed in bfloat16 or wider, within the bound.
No kernel may reach another device: no remote copies, remote signals or barrier semaphores. Data moves between devices by JAX's collectives and lax.ppermute only.
A program may use at most 128 MiB of HBM per device.

v0:
```python
import jax
import jax.numpy as jnp
from jax import lax
from jax.sharding import Mesh
from jax.sharding import PartitionSpec as P

BLOCK = 128
COL = ("col_0", "col_1")


def from_root(x, axes, root):
    x = jnp.where(lax.axis_index(axes) == root, x, jnp.zeros_like(x))
    for axis in axes:
        x = lax.psum(x, axis)
    return x


def local(density, block_mask):
    slab_width = density.shape[0]
    cols_local = density.shape[1]
    mask_full = jnp.repeat(jnp.repeat(block_mask.astype(jnp.bfloat16), BLOCK, 0), BLOCK, 1)
    masked = density * mask_full
    column_piece = from_root(masked[:, :slab_width], COL, 0)
    left_part = column_piece
    whole_sum = lax.psum(
        lax.dot_general(
            left_part, masked, (((0,), (0,)), ((), ())), preferred_element_type=jnp.float32
        ),
        "row",
    )
    square_slab = whole_sum.astype(jnp.bfloat16)
    ratio = cols_local // slab_width
    row_index = lax.axis_index("row")
    owner = row_index // ratio
    offset = row_index % ratio * slab_width
    own_square = lax.dynamic_slice_in_dim(whole_sum, offset, slab_width, 1)
    weight = (lax.axis_index(COL) == owner).astype(jnp.float32)
    left_part = square_slab
    return lax.psum_scatter(
        3.0 * weight * own_square
        - 2.0
        * lax.dot_general(
            left_part, masked, (((1,), (1,)), ((), ())), preferred_element_type=jnp.float32
        ),
        COL,
        scatter_dimension=0,
        tiled=True,
    )


def solution(mesh):
    torus = Mesh(mesh.devices.reshape(mesh.shape["row"], 4, 2), ("row", "col_0", "col_1"))
    in_specs = (P("row", COL), P("row", COL))
    out_specs = P(COL, "row")
    return jax.shard_map(local, mesh=torus, in_specs=in_specs, out_specs=out_specs, check_vma=False)
```

profile of v0, /device:TPU:0, one launch (start us, length us, event | category | flops | bytes accessed | tf_op | source)
XLA Modules:
  0.0 316.7 jit_solution(1278790285347594573)
XLA Ops:
  6.5 0.0 all-reduce.4.cloned.1.call-start
  6.5 0.7 convert_element_type.7
  7.2 0.0 copy-start.1
  7.3 4.5 %broadcast_in_dim.10 = bf16[1024,16,128]{2,1,0:T(8,128)(2,1)S(1)} broadcast(bf16[1024,16]{1,0:T(8,128)(2,1)S(1)} %bitcast.8), dimensions={0,1} | broadcast | bytes 4227072 | tf_op jit(solution)/shard_map/broadcast_in_dim | solution.py:21
  11.7 0.0 copy-done.1
  11.7 0.9 bitcast_multiply_fusion
  12.7 0.0 copy-start
  12.7 1.9 copy-done
  14.6 1.4 slice_select_fusion
  16.0 0.0 all-reduce.4.cloned.1.call-update
  16.1 0.0 all-reduce.6.cloned.1.call-start
  16.1 61.5 %all-reduce.4.cloned.1.call-done = bf16[1024,1024]{1,0:T(8,128)(2,1)} async-done(((bf16[1024,1024]{1,0:T(8,128)(2,1)}), bf16[1024,1024]{1,0:T(8,128)(2,1)}) %all-reduce.4.cloned.1.call-update) | async-done | bytes 2097168 | tf_op jit(solution)/shard_map/psum | solution.py:14
  77.7 0.0 all-reduce.6.cloned.1.call-update
  77.7 0.0 all-reduce.8.cloned.1.call-start
  77.7 28.9 %all-reduce.6.cloned.1.call-done = bf16[1024,1024]{1,0:T(8,128)(2,1)} async-done(((bf16[1024,1024]{1,0:T(8,128)(2,1)}), bf16[1024,1024]{1,0:T(8,128)(2,1)}) %all-reduce.6.cloned.1.call-update) | async-done | bytes 2097168 | tf_op jit(solution)/shard_map/psum | solution.py:14
  106.6 10.6 %fusion.4 = f32[1024,2048]{1,0:T(8,128)} fusion(bf16[1024,1024]{1,0:T(8,128)(2,1)} %all-reduce.6.cloned.1.call-done, bf16[1024,2048]{1,0:T(8,128)(2,1)} %copy-done), kind=kOutput, calls=%fused_computation.5 | convolution fusion | flops 4294967296 | bytes 14680064 | tf_op jit(solution)/shard_map/dot_general | solution.py:26
  117.3 0.0 all-reduce.8.cloned.1.call-update
  117.3 0.0 reduce-scatter.2.cloned.1.call-start
  117.4 143.1 %all-reduce.8.cloned.1.call-done = f32[1024,2048]{1,0:T(8,128)} async-done(((f32[1024,2048]{1,0:T(8,128)}), f32[1024,2048]{1,0:T(8,128)}) %all-reduce.8.cloned.1.call-update) | async-done | bytes 8388624 | tf_op jit(solution)/shard_map/psum | solution.py:25
  260.5 12.3 %multiply_subtract_fusion = f32[1024,1024]{1,0:T(8,128)} fusion(f32[1024,2048]{1,0:T(8,128)} %all-reduce.8.cloned.1.call-done, s32[]{:T(128)S(6)} %select_n.26, f32[]{:T(128)S(6)} %mul_shard_map.3, bf16[1024,2048]{1,0:T(8,128)(2,1)} %copy-done), kind=kOutput, calls=%fused_computation.1 | convolution fusion | flops 4300210176 | bytes 20971528 | tf_op jit(solution)/shard_map/dot_general | solution.py:42
  272.8 0.0 reduce-scatter.2.cloned.1.call-update
  272.8 37.3 %reduce-scatter.2.cloned.1.call-done = f32[128,1024]{1,0:T(8,128)} async-done(((f32[1024,1024]{1,0:T(8,128)}), f32[128,1024]{1,0:T(8,128)}) %reduce-scatter.2.cloned.1.call-update) | async-done | bytes 524304 | tf_op jit(solution)/shard_map/reduce_scatter | solution.py:39
  (1 shorter events, 0.0 us)
Async XLA Ops:
  6.5 71.1 %all-reduce.4.cloned.1.call-start = ((), (), s32[]{:S(2)}) async-start(), calls=%async_computation.1 | async-start | bytes 4194304 | tf_op jit(solution)/shard_map/psum | solution.py:14
  7.2 4.5 %copy-start.1 = (bf16[1024,2048]{1,0:T(8,128)(2,1)S(1)}, bf16[1024,2048]{1,0:T(8,128)(2,1)}, u32[]{:S(2)}) copy-start(bf16[1024,2048]{1,0:T(8,128)(2,1)} %param.2) | copy-start | bytes 12582916
  12.7 1.9 copy-start
  16.1 90.6 %all-reduce.6.cloned.1.call-start = ((), (), s32[]{:S(2)}) async-start(), calls=%async_computation.2 | async-start | bytes 4194304 | tf_op jit(solution)/shard_map/psum | solution.py:14
  77.7 182.8 %all-reduce.8.cloned.1.call-start = ((), (), s32[]{:S(2)}) async-start(), calls=%async_computation.3 | async-start | bytes 16777216 | tf_op jit(solution)/shard_map/psum | solution.py:25
  117.3 192.9 %reduce-scatter.2.cloned.1.call-start = ((), (), s32[]{:S(2)}) async-start(), calls=%async_computation.4 | async-start | bytes 4718592 | tf_op jit(solution)/shard_map/reduce_scatter | solution.py:39
Sparse Core Ops, SparseCore 0:
  16.2 61.4 all-reduce.3
  80.1 26.4 all-reduce.5
  117.4 143.0 all-reduce.7
  272.9 37.1 reduce-scatter.1
where the time goes:
time: 317 us
  waiting for transfers between devices  271 us (85%)
  matrix products  23 us (7%)
  between operations  13.2 us (4%)
  local copies, waits for them, and re-layouts  6.43 us (2%)
    psum x1, waiting for transfers between devices, local(): lax.psum(lax.dot_general(left_part, masked, (((0,), (0,)), ((), ())), pre...  143 us
    psum x2, waiting for transfers between devices, from_root(): x = lax.psum(x, axis)  90.5 us
    reduce_scatter x1, waiting for transfers between devices, local(): lax.psum_scatter(3.0 * weight * own_square - 2.0 * lax.dot_general(left_p...  37.3 us
    dot_general x1, matrix products, local(): lax.dot_general(left_part, masked, (((1,), (1,)), ((), ())), preferred_el...  12.3 us
    dot_general x1, matrix products, local(): lax.dot_general(left_part, masked, (((0,), (0,)), ((), ())), preferred_el...  10.6 us
  transfers between devices with their start and end apart: 4, of which 4 were waited for; matrix products, arithmetic and copies ran while one was open for 0% of the time, Pallas kernels for 0%

commit v1 on v0

v1 whole, which is shorter than its diff:
```python
import functools

import jax
import jax.numpy as jnp
from jax import lax
from jax.experimental import pallas as pl
from jax.experimental.pallas import tpu as pltpu
from jax.sharding import Mesh
from jax.sharding import PartitionSpec as P

BLOCK = 128
SLAB = 1024
WIDE = 2048
LANES = 128
QUARTER = SLAB // 4
PIECE = SLAB // 16
LINE = ("x", "y", "core")
F32, BF16, I16, I32 = jnp.float32, jnp.bfloat16, jnp.int16, jnp.int32

FIRST, SECOND, DEPTH, CORE, OWNER, HALF = range(6)


def shape(rows, columns, dtype):
    return jax.ShapeDtypeStruct((rows, columns), dtype)


def encode(v):
    top = jnp.max(jnp.abs(v), axis=1, keepdims=True)
    e = jnp.clip(jnp.floor(jnp.log2(top)) + 1.0, -100.0, 128.0)
    q = jnp.clip(jnp.round(v * jnp.exp2(15.0 - e)), -32767.0, 32767.0)
    tail = jnp.broadcast_to(e, (v.shape[0], LANES))
    return q.astype(I32).astype(I16), tail.astype(I32).astype(I16)


def put(ref, v):
    q, tail = encode(v)
    width = v.shape[1]
    ref[:, :width] = q
    ref[:, width:] = tail


def take(ref):
    width = ref.shape[1] - LANES
    e = ref[:, width:].astype(I32).astype(F32)
    scale = jnp.exp2(e - 15.0)[:, :1]
    return ref[:, :width].astype(I32).astype(F32) * scale


def first_kernel(d, s, own, other, top, low, out, acc):
    n = pl.program_id(0)
    dims = (((0,), (0,)), ((), ()))
    t = lax.dot_general(own[...], top[...], dims, preferred_element_type=F32)
    t += lax.dot_general(other[...], low[...], dims, preferred_element_type=F32)
    if d == 0:
        out[...] = t
    else:
        acc[:, pl.ds(pl.multiple_of(n * 512, 512), 512)] = t

        @pl.when(n == pl.num_programs(0) - 1)
        def _():
            put(out, acc[...])


def first_product(d, s, own, other, masked):
    if d == 0:
        out = shape(QUARTER, WIDE, F32)
        out_spec = pl.BlockSpec((QUARTER, 512), lambda n, s: (0, n))
    else:
        out = shape(QUARTER, WIDE + LANES, I16)
        out_spec = pl.BlockSpec((QUARTER, WIDE + LANES), lambda n, s: (0, 0))
    piece = pl.BlockSpec((512, QUARTER), lambda n, s: (0, (s[FIRST] + d) % 4))
    return pl.pallas_call(
        functools.partial(first_kernel, d),
        out_shape=out,
        grid_spec=pltpu.PrefetchScalarGridSpec(
            num_scalar_prefetch=1,
            grid=(WIDE // 512,),
            in_specs=[
                piece,
                piece,
                pl.BlockSpec((512, 512), lambda n, s: (s[CORE], n)),
                pl.BlockSpec((512, 512), lambda n, s: (1 - s[CORE], n)),
            ],
            out_specs=out_spec,
            scratch_shapes=[pltpu.VMEM((QUARTER, WIDE), F32)],
        ),
        cost_estimate=pl.CostEstimate(
            flops=2 * QUARTER * SLAB * WIDE, bytes_accessed=6 << 20, transcendentals=0
        ),
        name=f"first_{d}",
    )(s, own, other, masked, masked)


def spread_kernel(s, own, a, b, c, out0, out1, out2, out3):
    g = pl.program_id(0)
    v = own[...] + take(a) + take(b) + take(c)

    @pl.when(g == 0)
    def _():
        out0[...] = v

    for d, out in enumerate((out1, out2, out3), 1):

        @pl.when(g == d)
        def _(out=out):
            put(out, v)


def spread_sum(s, own, parts):
    index = lambda g, s: ((s[SECOND] + g) % 4, 0)
    fixed = lambda g, s: (0, 0)
    coded = WIDE + LANES
    return pl.pallas_call(
        spread_kernel,
        out_shape=[shape(PIECE, WIDE, F32)] + [shape(PIECE, coded, I16)] * 3,
        grid_spec=pltpu.PrefetchScalarGridSpec(
            num_scalar_prefetch=1,
            grid=(4,),
            in_specs=[pl.BlockSpec((PIECE, WIDE), index)]
            + [pl.BlockSpec((PIECE, coded), index)] * 3,
            out_specs=[pl.BlockSpec((PIECE, WIDE), fixed)]
            + [pl.BlockSpec((PIECE, coded), fixed)] * 3,
        ),
        cost_estimate=pl.CostEstimate(
            flops=8 << 20, bytes_accessed=6 << 20, transcendentals=0
        ),
        name="spread",
    )(s, own, *parts)


def gather_kernel(own, a, b, c, out):
    put(out, own[...] + take(a) + take(b) + take(c))


def finish_kernel(own, a, b, c, out):
    out[...] = own[...] + take(a) + take(b) + take(c)


def second_kernel(first, s, coded, block, *refs):
    mine, theirs, rounded, triple = refs if first else refs[2:]
    n = pl.program_id(0)

    @pl.when(n == 0)
    def _():
        for j in range(4):
            sub = (s[SECOND] + 4 - j) % 4
            place = ((sub // 2) ^ s[CORE]) * 128 + (sub % 2) * 64
            rows = pl.ds(pl.multiple_of(place, 64), PIECE)
            v = take(coded.at[j * PIECE : (j + 1) * PIECE])
            rounded[rows, :] = v.astype(BF16)
            for half in range(2):

                @pl.when((s[OWNER] == 1) & (s[HALF] == half))
                def _(v=v, rows=rows, half=half):
                    triple[rows, :] = 3.0 * v[:, half * SLAB : (half + 1) * SLAB]

    t = -2.0 * lax.dot_general(
        rounded[...], block[...], (((1,), (1,)), ((), ())), preferred_element_type=F32
    )

    @pl.when(s[OWNER] == 1)
    def _():
        u = t + triple[:, pl.ds(pl.multiple_of(n * 256, 256), 256)]
        mine[...] = u[:128]
        theirs[...] = u[128:]

    @pl.when(s[OWNER] == 0)
    def _():
        mine[...] = t[:128]
        theirs[...] = t[128:]


def second_product(d, s, coded, masked, kept):
    first = kept is None
    whole = pl.BlockSpec((128, 256), lambda n, s: ((s[FIRST] + 4 - d) % 4, n))
    extra = [] if first else [pl.BlockSpec(memory_space=pl.ANY)] * 2
    return pl.pallas_call(
        functools.partial(second_kernel, first),
        out_shape=[shape(512, SLAB, F32)] * 2,
        grid_spec=pltpu.PrefetchScalarGridSpec(
            num_scalar_prefetch=1,
            grid=(4,),
            in_specs=[
                pl.BlockSpec((QUARTER, WIDE + LANES), lambda n, s: (0, 0)),
                pl.BlockSpec((256, WIDE), lambda n, s: (n, 0)),
            ]
            + extra,
            out_specs=[whole, whole],
            scratch_shapes=[
                pltpu.VMEM((QUARTER, WIDE), BF16),
                pltpu.VMEM((QUARTER, SLAB), F32),
            ],
        ),
        input_output_aliases={} if first else {3: 0, 4: 1},
        cost_estimate=pl.CostEstimate(
            flops=2 * QUARTER * SLAB * WIDE, bytes_accessed=6 << 20, transcendentals=0
        ),
        name=f"second_{d}",
    )(s, coded, masked, *(() if first else kept))


def deal_kernel(s, mine, came, out0, out1, out2, out3):
    g = pl.program_id(0)
    v = mine[...] + came[...]

    @pl.when(g == 0)
    def _():
        out0[...] = v

    for d, out in enumerate((out1, out2, out3), 1):

        @pl.when(g == d)
        def _(out=out):
            put(out, v)


def deal(s, mine, came):
    index = lambda g, s: ((s[DEPTH] + g) % 4, 0)
    fixed = lambda g, s: (0, 0)
    return pl.pallas_call(
        deal_kernel,
        out_shape=[shape(128, SLAB, F32)] + [shape(128, SLAB + LANES, I16)] * 3,
        grid_spec=pltpu.PrefetchScalarGridSpec(
            num_scalar_prefetch=1,
            grid=(4,),
            in_specs=[pl.BlockSpec((128, SLAB), index)] * 2,
            out_specs=[pl.BlockSpec((128, SLAB), fixed)]
            + [pl.BlockSpec((128, SLAB + LANES), fixed)] * 3,
        ),
        cost_estimate=pl.CostEstimate(
            flops=4 << 20, bytes_accessed=5 << 20, transcendentals=0
        ),
        name="deal",
    )(s, mine, came)


def place(x, y, core):
    return (x * 4 + y) * 2 + core


def along(v, d, first):
    pairs = []
    for x in range(4):
        for y in range(4):
            for core in range(2):
                to = ((x + d) % 4, y) if (core == 0) == first else (x, (y + d) % 4)
                pairs.append((place(x, y, core), place(*to, core)))
    return lax.ppermute(v, LINE, pairs)


def swap(v):
    return lax.ppermute(v, "core", [(0, 1), (1, 0)])


def spread_column(piece, z, core):
    rows = piece.shape[0] // 2
    came = lax.ppermute(piece[rows:], "core", [(0, 1), (1, 0)])
    half = jnp.where(core == 0, piece[:rows], came)
    axes = ("z", "core")
    came = lax.ppermute(half, axes, [(0, 2), (1, 7)])
    half = jnp.where(z == 0, half, came)
    came = lax.ppermute(half, axes, [(0, 6), (1, 3), (2, 4), (7, 5)])
    late = (z == 2) | ((z == 3) & (core == 0)) | ((z == 1) & (core == 1))
    return jnp.where(late, came, half)


def local(density, block_mask):
    x, y, z, core = (lax.axis_index(a) for a in ("x", "y", "z", "core"))
    row = x * 4 + y
    first = jnp.where(core == 0, x, y)
    second = jnp.where(core == 0, y, x)
    owner = (z * 2 + core == row // 2).astype(I32)
    s = jnp.zeros((8,), I32)
    at = jnp.arange(8, dtype=I32)
    for i, v in enumerate((first, second, z, core, owner, row % 2)):
        s = jnp.where(at == i, v, s)

    wide = jnp.repeat(block_mask.astype(BF16), BLOCK, 1)
    masked = (density.reshape(8, BLOCK, WIDE) * wide[:, None, :]).reshape(SLAB, WIDE)
    own = spread_column(masked[:, :SLAB], z, core)
    other = swap(own)

    came = [along(first_product(d, s, own, other, masked), d, True) for d in (2, 1, 3)]
    mine = first_product(0, s, own, other, masked)
    mine, *parts = spread_sum(s, mine, came)
    came = [along(v, d, False) for d, v in ((2, parts[1]), (1, parts[0]), (3, parts[2]))]
    coded = pl.pallas_call(
        gather_kernel, out_shape=shape(PIECE, WIDE + LANES, I16), name="gather"
    )(mine, *came)

    near = [along(coded, d, False) for d in (1, 2, 3)]
    coded = jnp.concatenate([coded, *near], 0)
    far = {d: along(coded, d, True) for d in (1, 2, 3)}
    kept = second_product(0, s, coded, masked, None)
    for d in (1, 3, 2):
        kept = second_product(d, s, far[d], masked, kept)
    mine, *parts = deal(s, kept[0], swap(kept[1]))
    came = [
        lax.ppermute(parts[d - 1], "z", [(i, (i + d) % 4) for i in range(4)])
        for d in (2, 1, 3)
    ]
    return pl.pallas_call(finish_kernel, out_shape=shape(128, SLAB, F32), name="finish")(
        mine, *came
    )


def solution(mesh):
    torus = Mesh(mesh.devices.reshape(4, 4, 4, 2), ("x", "y", "z", "core"))
    in_specs = (P(("x", "y"), ("z", "core")),) * 2
    out_specs = P(("z", "core"), ("x", "y"))
    return jax.shard_map(local, mesh=torus, in_specs=in_specs, out_specs=out_specs, check_vma=False)
```

time: 317 us -> 209 us (0.66)
  waiting for transfers between devices: 271 us -> 89.5 us
  Pallas kernels: 0 us -> 66.4 us
  starting transfers between devices: 0.12 us -> 34 us
  matrix products: 23 us -> 0 us
  between operations: 13.2 us -> 0.18 us
  local copies, waits for them, and re-layouts: 6.43 us -> 10.2 us
  other arithmetic: 3.04 us -> 6.29 us
    psum x3 -> x0, waiting for transfers between devices: 234 us -> none  [the longest x1 143 us: local(): lax.psum(lax.dot_general(left_part, masked, (((0,), (0,)), ((), ())), pre...]
    ppermute x0 -> x20, waiting for transfers between devices: none -> 89.5 us  [the longest x12 45.7 us: along(): return lax.ppermute(v, LINE, pairs)]
    pallas_call x0 -> x12, Pallas kernels: none -> 66.4 us  [the longest x4 26.5 us: second_product(): pl.pallas_call(functools.partial(second_kernel, first), out_shape=[shape(...]
    reduce_scatter x1 -> x0, waiting for transfers between devices: 37.3 us -> none  [local(): lax.psum_scatter(3.0 * weight * own_square - 2.0 * lax.dot_general(left_p...]
    ppermute x0 -> x20, starting transfers between devices: none -> 34 us  [the longest x12 19.6 us: along(): return lax.ppermute(v, LINE, pairs)]
    dot_general x2 -> x0, matrix products: 23 us -> none  [the longest x1 12.3 us: local(): lax.dot_general(left_part, masked, (((1,), (1,)), ((), ())), preferred_el...]
    unnamed x4 -> x32, local copies, waits for them, and re-layouts: 1.93 us -> 9.89 us
    broadcast_in_dim x2 -> x0, local copies, waits for them, and re-layouts: 4.5 us -> none  [the longest x1 4.46 us: local(): jnp.repeat(jnp.repeat(block_mask.astype(jnp.bfloat16), BLOCK, 0), BLOCK, 1)]
  transfers between devices with their start and end apart: 4 -> 20, of which waited for: 4 -> 14; matrix products, arithmetic and copies ran while one was open for 0% -> 0% of each run, Pallas kernels for 0% -> 18%
where the time goes in v1:
time: 209 us; the launch traced here: 207 us
  waiting for transfers between devices  89.5 us (43%)
  Pallas kernels  66.4 us (32%)
  starting transfers between devices  34 us (16%)
  local copies, waits for them, and re-layouts  10.2 us (5%)
  other arithmetic  6.29 us (3%)
    ppermute x12, waiting for transfers between devices, along(): return lax.ppermute(v, LINE, pairs)  45.7 us
    pallas_call x4, Pallas kernels, second_product(): pl.pallas_call(functools.partial(second_kernel, first), out_shape=[shape(...  26.5 us
    pallas_call x4, Pallas kernels, first_product(): pl.pallas_call(functools.partial(first_kernel, d), out_shape=out, grid_sp...  24.5 us
    ppermute x12, starting transfers between devices, along(): return lax.ppermute(v, LINE, pairs)  19.6 us
    ppermute x1, waiting for transfers between devices, spread_column(): came = lax.ppermute(half, axes, [(0, 2), (1, 7)])  12.2 us
    ppermute x1, waiting for transfers between devices, spread_column(): came = lax.ppermute(half, axes, [(0, 6), (1, 3), (2, 4), (7, 5)])  12.2 us
    ppermute x3, waiting for transfers between devices, local(): lax.ppermute(parts[d - 1], 'z', [(i, (i + d) % 4) for i in range(4)])  10.6 us
    unnamed x32, local copies, waits for them, and re-layouts  9.89 us
  transfers between devices with their start and end apart: 20, of which 14 were waited for; matrix products, arithmetic and copies ran while one was open for 0% of the time, Pallas kernels for 18%

profile of v1, /device:TPU:0, one launch (start us, length us, event | category | flops | bytes accessed | tf_op | source)
XLA Modules:
  0.0 206.5 jit_solution(7589495165882047540)
XLA Ops:
  0.9 2.5 %bitcast_multiply_fusion.top.low.block = bf16[1024,2048]{1,0:T(8,128)(2,1)S(1)} fusion(bf16[1024,2048]{1,0:T(8,128)(2,1)} %param.2, bf16[8,2048]{1,0:T(8,128)(2,1)S(1)} %broadcast_bitcast_fusion), kind=kLoop, calls=%fused_computation | loop fusion | flops 2097152 | bytes 8421376 | tf_op jit(solution)/shard_map/mul | solution.py:279
  3.4 2.0 copy-done
  5.5 2.6 %collective-permute-done = bf16[512,1024]{1,0:T(8,128)(2,1)S(1)} collective-permute-done((bf16[512,1024]{1,0:T(8,128)(2,1)S(1)}, bf16[512,1024]{1,0:T(8,128)(2,1)S(1)}, u32[]{:S(2)}, u32[]{:S(2)}) %collective-permute-start) | collective-permute-done | bytes 1048608 | tf_op jit(solution)/shard_map/ppermute | solution.py:257
  8.2 1.3 slice_select_fusion
  9.5 4.0 %collective-permute-start.1 = (bf16[512,1024]{1,0:T(8,128)(2,1)S(1)}, bf16[512,1024]{1,0:T(8,128)(2,1)S(1)}, u32[]{:S(2)}, u32[]{:S(2)}) collective-permute-start(bf16[512,1024]{1,0:T(8,128)(2,1)S(1)} %slice_select_fusion), channel_id=1, source_target_pairs={{0,2},{1,7},{8,10},{9,15},{16,18},{17,23},{24,26},{25,31},{32,34},... | collective-permute-start | bytes 3145736 | tf_op jit(solution)/shard_map/ppermute | solution.py:260
  13.5 12.2 %collective-permute-done.1 = bf16[512,1024]{1,0:T(8,128)(2,1)S(1)} collective-permute-done((bf16[512,1024]{1,0:T(8,128)(2,1)S(1)}, bf16[512,1024]{1,0:T(8,128)(2,1)S(1)}, u32[]{:S(2)}, u32[]{:S(2)}) %collective-permute-start.1) | collective-permute-done | bytes 1048608 | tf_op jit(solution)/shard_map/ppermute | solution.py:260
  25.9 1.4 collective-permute-start.2
  27.2 12.2 %collective-permute-done.2 = bf16[512,1024]{1,0:T(8,128)(2,1)S(1)} collective-permute-done((bf16[512,1024]{1,0:T(8,128)(2,1)S(1)}, bf16[512,1024]{1,0:T(8,128)(2,1)S(1)}, u32[]{:S(2)}, u32[]{:S(2)}) %collective-permute-start.2) | collective-permute-done | bytes 1048608 | tf_op jit(solution)/shard_map/ppermute | solution.py:262
  39.6 0.9 collective-permute-start.3
  41.0 1.8 collective-permute-done.3.other
  42.8 1.0 copy-done.2
  43.7 6.2 %first_3.1 = s16[256,2176]{1,0:T(8,128)(2,1)} custom-call(s32[8]{0:T(128)} %compare_select_fusion.5.s, bf16[512,1024]{1,0:T(8,128)(2,1)} %copy-done.1, bf16[512,1024]{1,0:T(8,128)(2,1)} %copy-done.2, bf16[1024,2048]{1,0:T(8,128)(2,1)} %copy-done, bf16[1024,2048]{1,0:T(8,128)(2,1)} %copy-done), custom_call_target="tpu_custom_call" | custom-call | flops 1073741824 | bytes 6291456 | tf_op jit(solution)/shard_map/first_3/pallas_call | solution.py:72
  49.9 2.8 %collective-permute-start.6 = (s16[256,2176]{1,0:T(8,128)(2,1)}, s16[256,2176]{1,0:T(8,128)(2,1)S(1)}, u32[]{:S(2)}, u32[]{:S(2)}) collective-permute-start(s16[256,2176]{1,0:T(8,128)(2,1)} %first_3.1), channel_id=1, source_target_pairs={{0,96},{1,25},{8,104},{9,1},{16,112},{17,9},{24,120},{25,17},{32,0... | collective-permute-start | bytes 3342344 | tf_op jit(solution)/shard_map/ppermute | solution.py:248
  52.7 6.2 %first_1.1 = s16[256,2176]{1,0:T(8,128)(2,1)} custom-call(s32[8]{0:T(128)} %compare_select_fusion.5.s, bf16[512,1024]{1,0:T(8,128)(2,1)} %copy-done.1, bf16[512,1024]{1,0:T(8,128)(2,1)} %copy-done.2, bf16[1024,2048]{1,0:T(8,128)(2,1)} %copy-done, bf16[1024,2048]{1,0:T(8,128)(2,1)} %copy-done), custom_call_target="tpu_custom_call" | custom-call | flops 1073741824 | bytes 6291456 | tf_op jit(solution)/shard_map/first_1/pallas_call | solution.py:72
  58.8 6.2 %first_2.1 = s16[256,2176]{1,0:T(8,128)(2,1)} custom-call(s32[8]{0:T(128)} %compare_select_fusion.5.s, bf16[512,1024]{1,0:T(8,128)(2,1)} %copy-done.1, bf16[512,1024]{1,0:T(8,128)(2,1)} %copy-done.2, bf16[1024,2048]{1,0:T(8,128)(2,1)} %copy-done, bf16[1024,2048]{1,0:T(8,128)(2,1)} %copy-done), custom_call_target="tpu_custom_call" | custom-call | flops 1073741824 | bytes 6291456 | tf_op jit(solution)/shard_map/first_2/pallas_call | solution.py:72
  65.1 2.3 %collective-permute-start.4 = (s16[256,2176]{1,0:T(8,128)(2,1)}, s16[256,2176]{1,0:T(8,128)(2,1)S(1)}, u32[]{:S(2)}, u32[]{:S(2)}) collective-permute-start(s16[256,2176]{1,0:T(8,128)(2,1)} %first_2.1), channel_id=1, source_target_pairs={{0,64},{1,17},{8,72},{9,25},{16,80},{17,1},{24,88},{25,9},{32,96},... | collective-permute-start | bytes 3342344 | tf_op jit(solution)/shard_map/ppermute | solution.py:248
  67.4 5.9 %first_0.1.own = f32[256,2048]{1,0:T(8,128)} custom-call(s32[8]{0:T(128)} %compare_select_fusion.5.s, bf16[512,1024]{1,0:T(8,128)(2,1)} %copy-done.1, bf16[512,1024]{1,0:T(8,128)(2,1)} %copy-done.2, bf16[1024,2048]{1,0:T(8,128)(2,1)} %copy-done, bf16[1024,2048]{1,0:T(8,128)(2,1)} %copy-done), custom_call_target="tpu_custom_call" | custom-call | flops 1073741824 | bytes 6291456 | tf_op jit(solution)/shard_map/first_0/pallas_call | solution.py:72
  73.3 14.4 %collective-permute-done.5.b = s16[256,2176]{1,0:T(8,128)(2,1)S(1)} collective-permute-done((s16[256,2176]{1,0:T(8,128)(2,1)}, s16[256,2176]{1,0:T(8,128)(2,1)S(1)}, u32[]{:S(2)}, u32[]{:S(2)}) %collective-permute-start.5) | collective-permute-done | bytes 1114144 | tf_op jit(solution)/shard_map/ppermute | solution.py:248
  87.7 1.0 copy-done.8
  88.7 1.1 copy-done.9
  89.7 5.7 %spread.1 = (f32[64,2048]{1,0:T(8,128)}, s16[64,2176]{1,0:T(8,128)(2,1)}, s16[64,2176]{1,0:T(8,128)(2,1)}, s16[64,2176]{1,0:T(8,128)(2,1)}) custom-call(s32[8]{0:T(128)} %compare_select_fusion.5.s, f32[256,2048]{1,0:T(8,128)} %first_0.1.own, s16[256,2176]{1,0:T(8,128)(2,1)} %copy-done.9, s16[256,2176]{1,0:T(8,128)(2,1)} %copy-done.8, s16[256,2176]{1,0:T(8,128)(2,1)} %copy-done.7), custom_call_target="tpu_custom_call" | custom-call | flops 8388608 | bytes 6291456 | tf_op jit(solution)/shard_map/spread/pallas_call | solution.py:113
  95.5 3.2 %collective-permute-start.7 = (s16[64,2176]{1,0:T(8,128)(2,1)}, s16[64,2176]{1,0:T(8,128)(2,1)S(1)}, u32[]{:S(2)}, u32[]{:S(2)}) collective-permute-start(s16[64,2176]{1,0:T(8,128)(2,1)} %get-tuple-element.22), channel_id=1, source_target_pairs={{0,16},{1,65},{8,24},{9,73},{16,0},{17,81},{24,8},{25,89},{32,48},... | collective-permute-start | bytes 835592 | tf_op jit(solution)/shard_map/ppermute | solution.py:248
  99.3 2.6 %collective-permute-start.9 = (s16[64,2176]{1,0:T(8,128)(2,1)}, s16[64,2176]{1,0:T(8,128)(2,1)S(1)}, u32[]{:S(2)}, u32[]{:S(2)}) collective-permute-start(s16[64,2176]{1,0:T(8,128)(2,1)} %get-tuple-element.24), channel_id=1, source_target_pairs={{0,24},{1,97},{8,0},{9,105},{16,8},{17,113},{24,16},{25,121},{32,5... | collective-permute-start | bytes 835592 | tf_op jit(solution)/shard_map/ppermute | solution.py:248
  101.9 1.8 collective-permute-done.7.a
  103.7 3.0 %collective-permute-done.8.b = s16[64,2176]{1,0:T(8,128)(2,1)S(1)} collective-permute-done((s16[64,2176]{1,0:T(8,128)(2,1)}, s16[64,2176]{1,0:T(8,128)(2,1)S(1)}, u32[]{:S(2)}, u32[]{:S(2)}) %collective-permute-start.8) | collective-permute-done | bytes 278560 | tf_op jit(solution)/shard_map/ppermute | solution.py:248
  107.8 2.3 %gather.1 = s16[64,2176]{1,0:T(8,128)(2,1)} custom-call(f32[64,2048]{1,0:T(8,128)} %get-tuple-element.21.own, s16[64,2176]{1,0:T(8,128)(2,1)} %copy-done.13, s16[64,2176]{1,0:T(8,128)(2,1)} %copy-done.14, s16[64,2176]{1,0:T(8,128)(2,1)} %copy-done.15), custom_call_target="tpu_custom_call" | custom-call | tf_op jit(solution)/shard_map/gather/pallas_call | solution.py:287
  110.1 1.5 collective-permute-start.10
  111.6 2.8 %collective-permute-start.11 = (s16[64,2176]{1,0:T(8,128)(2,1)}, s16[64,2176]{1,0:T(8,128)(2,1)S(1)}, u32[]{:S(2)}, u32[]{:S(2)}) collective-permute-start(s16[64,2176]{1,0:T(8,128)(2,1)} %gather.1), channel_id=1, source_target_pairs={{0,16},{1,65},{8,24},{9,73},{16,0},{17,81},{24,8},{25,89},{32,48},... | collective-permute-start | bytes 835592 | tf_op jit(solution)/shard_map/ppermute | solution.py:248
  114.9 3.2 %collective-permute-done.10 = s16[64,2176]{1,0:T(8,128)(2,1)S(1)} collective-permute-done((s16[64,2176]{1,0:T(8,128)(2,1)}, s16[64,2176]{1,0:T(8,128)(2,1)S(1)}, u32[]{:S(2)}, u32[]{:S(2)}) %collective-permute-start.10) | collective-permute-done | bytes 278560 | tf_op jit(solution)/shard_map/ppermute | solution.py:248
  118.1 4.0 %collective-permute-done.11 = s16[64,2176]{1,0:T(8,128)(2,1)S(1)} collective-permute-done((s16[64,2176]{1,0:T(8,128)(2,1)}, s16[64,2176]{1,0:T(8,128)(2,1)S(1)}, u32[]{:S(2)}, u32[]{:S(2)}) %collective-permute-start.11) | collective-permute-done | bytes 278560 | tf_op jit(solution)/shard_map/ppermute | solution.py:248
  122.1 1.0 pad_add_fusion.coded
  123.2 3.2 %collective-permute-start.14 = (s16[256,2176]{1,0:T(8,128)(2,1)S(1)}, s16[256,2176]{1,0:T(8,128)(2,1)S(1)}, u32[]{:S(2)}, u32[]{:S(2)}) collective-permute-start(s16[256,2176]{1,0:T(8,128)(2,1)S(1)} %pad_add_fusion.coded), channel_id=1, source_target_pairs={{0,96},{1,25},{8,104},{9,1},{16,112},{17,9},{24,120},{25,17},{32,0... | collective-permute-start | bytes 3342344 | tf_op jit(solution)/shard_map/ppermute | solution.py:248
  126.5 6.6 %second_0.1 = (f32[512,1024]{1,0:T(8,128)}, f32[512,1024]{1,0:T(8,128)}) custom-call(s32[8]{0:T(128)} %compare_select_fusion.5.s, s16[256,2176]{1,0:T(8,128)(2,1)} %copy-done.3, bf16[1024,2048]{1,0:T(8,128)(2,1)} %copy-done), custom_call_target="tpu_custom_call" | custom-call | flops 1073741824 | bytes 6291456 | tf_op jit(solution)/shard_map/second_0/pallas_call | solution.py:177
  133.1 18.9 %collective-permute-done.15.coded = s16[256,2176]{1,0:T(8,128)(2,1)} collective-permute-done((s16[256,2176]{1,0:T(8,128)(2,1)S(1)}, s16[256,2176]{1,0:T(8,128)(2,1)}, u32[]{:S(2)}, u32[]{:S(2)}) %collective-permute-start.15) | collective-permute-done | bytes 1114144 | tf_op jit(solution)/shard_map/ppermute | solution.py:248
  152.0 6.7 %second_1.1 = (f32[512,1024]{1,0:T(8,128)}, f32[512,1024]{1,0:T(8,128)}) custom-call(s32[8]{0:T(128)} %compare_select_fusion.5.s, s16[256,2176]{1,0:T(8,128)(2,1)} %collective-permute-done.15.coded, bf16[1024,2048]{1,0:T(8,128)(2,1)} %copy-done, f32[512,1024]{1,0:T(8,128)} %get-tuple-element.25.refs_0_, ...), custom_call_target="tpu_custom_call", output_to_operand_aliasing={{0}: (3, {}), {1}: (4, {})} | custom-call | flops 1073741824 | bytes 6291456 | tf_op jit(solution)/shard_map/second_1/pallas_call | solution.py:177
  158.7 1.0 copy-done.6
  159.7 6.5 %second_3.1 = (f32[512,1024]{1,0:T(8,128)}, f32[512,1024]{1,0:T(8,128)}) custom-call(s32[8]{0:T(128)} %compare_select_fusion.5.s, s16[256,2176]{1,0:T(8,128)(2,1)} %copy-done.6, bf16[1024,2048]{1,0:T(8,128)(2,1)} %copy-done, f32[512,1024]{1,0:T(8,128)} %get-tuple-element.27.refs_0_, ...), custom_call_target="tpu_custom_call", output_to_operand_aliasing={{0}: (3, {}), {1}: (4, {})} | custom-call | flops 1073741824 | bytes 6291456 | tf_op jit(solution)/shard_map/second_3/pallas_call | solution.py:177
  166.3 1.0 copy-done.5
  167.3 6.6 %second_2.1 = (f32[512,1024]{1,0:T(8,128)}, f32[512,1024]{1,0:T(8,128)}) custom-call(s32[8]{0:T(128)} %compare_select_fusion.5.s, s16[256,2176]{1,0:T(8,128)(2,1)} %copy-done.5, bf16[1024,2048]{1,0:T(8,128)(2,1)} %copy-done, f32[512,1024]{1,0:T(8,128)} %get-tuple-element.29.refs_0_, ...), custom_call_target="tpu_custom_call", output_to_operand_aliasing={{0}: (3, {}), {1}: (4, {})} | custom-call | flops 1073741824 | bytes 6291456 | tf_op jit(solution)/shard_map/second_2/pallas_call | solution.py:177
  173.9 4.4 %collective-permute-done.16.came = f32[512,1024]{1,0:T(8,128)S(1)} collective-permute-done((f32[512,1024]{1,0:T(8,128)}, f32[512,1024]{1,0:T(8,128)S(1)}, u32[]{:S(2)}, u32[]{:S(2)}) %collective-permute-start.16) | collective-permute-done | bytes 2097184 | tf_op jit(solution)/shard_map/ppermute | solution.py:252
  178.3 1.4 copy-done.4
  179.6 5.1 %deal.1 = (f32[128,1024]{1,0:T(8,128)}, s16[128,1152]{1,0:T(8,128)(2,1)}, s16[128,1152]{1,0:T(8,128)(2,1)}, s16[128,1152]{1,0:T(8,128)(2,1)}) custom-call(s32[8]{0:T(128)} %compare_select_fusion.5.s, f32[512,1024]{1,0:T(8,128)} %get-tuple-element.31.mine, f32[512,1024]{1,0:T(8,128)} %copy-done.4), custom_call_target="tpu_custom_call" | custom-call | flops 4194304 | bytes 5242880 | tf_op jit(solution)/shard_map/deal/pallas_call | solution.py:220
  184.7 4.8 %collective-permute-start.17 = (s16[128,1152]{1,0:T(8,128)(2,1)}, s16[128,1152]{1,0:T(8,128)(2,1)S(1)}, u32[]{:S(2)}, u32[]{:S(2)}) collective-permute-start(s16[128,1152]{1,0:T(8,128)(2,1)} %get-tuple-element.34), channel_id=1, source_target_pairs={{0,4},{2,6},{4,0},{6,2},{1,5},{3,7},{5,1},{7,3},{8,12},{10,14},{12... | collective-permute-start | bytes 884744 | tf_op jit(solution)/shard_map/ppermute | solution.py:299
  189.5 3.2 %collective-permute-start.19 = (s16[128,1152]{1,0:T(8,128)(2,1)}, s16[128,1152]{1,0:T(8,128)(2,1)S(1)}, u32[]{:S(2)}, u32[]{:S(2)}) collective-permute-start(s16[128,1152]{1,0:T(8,128)(2,1)} %get-tuple-element.36), channel_id=1, source_target_pairs={{0,6},{2,0},{4,2},{6,4},{1,7},{3,1},{5,3},{7,5},{8,14},{10,8},{12,... | collective-permute-start | bytes 884744 | tf_op jit(solution)/shard_map/ppermute | solution.py:299
  192.7 4.9 %collective-permute-done.17.a = s16[128,1152]{1,0:T(8,128)(2,1)S(1)} collective-permute-done((s16[128,1152]{1,0:T(8,128)(2,1)}, s16[128,1152]{1,0:T(8,128)(2,1)S(1)}, u32[]{:S(2)}, u32[]{:S(2)}) %collective-permute-start.17) | collective-permute-done | bytes 294944 | tf_op jit(solution)/shard_map/ppermute | solution.py:299
  197.6 5.7 %collective-permute-done.18.b = s16[128,1152]{1,0:T(8,128)(2,1)S(1)} collective-permute-done((s16[128,1152]{1,0:T(8,128)(2,1)}, s16[128,1152]{1,0:T(8,128)(2,1)S(1)}, u32[]{:S(2)}, u32[]{:S(2)}) %collective-permute-start.18) | collective-permute-done | bytes 294944 | tf_op jit(solution)/shard_map/ppermute | solution.py:299
  203.3 0.7 copy-done.11
  204.2 2.3 %finish.1 = f32[128,1024]{1,0:T(8,128)} custom-call(f32[128,1024]{1,0:T(8,128)} %get-tuple-element.33.own, s16[128,1152]{1,0:T(8,128)(2,1)} %copy-done.10, s16[128,1152]{1,0:T(8,128)(2,1)} %copy-done.11, s16[128,1152]{1,0:T(8,128)(2,1)} %copy-done.12), custom_call_target="tpu_custom_call" | custom-call | tf_op jit(solution)/shard_map/finish/pallas_call | solution.py:302
  (46 shorter events, 4.3 us)
Async XLA Ops:
  3.4 2.0 copy-start
  5.4 2.7 %collective-permute-start = (bf16[512,1024]{1,0:T(8,128)(2,1)S(1)}, bf16[512,1024]{1,0:T(8,128)(2,1)S(1)}, u32[]{:S(2)}, u32[]{:S(2)}) collective-permute-start(bf16[512,1024]{1,0:T(8,128)(2,1)S(1)} %slice.12), channel_id=1, source_target_pairs={{0,1},{1,0},{2,3},{3,2},{4,5},{5,4},{6,7},{7,6},{8,9},{9,8},{10,11... | collective-permute-start | bytes 3145736 | tf_op jit(solution)/shard_map/ppermute | solution.py:257
  9.5 16.2 %collective-permute-start.1 = (bf16[512,1024]{1,0:T(8,128)(2,1)S(1)}, bf16[512,1024]{1,0:T(8,128)(2,1)S(1)}, u32[]{:S(2)}, u32[]{:S(2)}) collective-permute-start(bf16[512,1024]{1,0:T(8,128)(2,1)S(1)} %slice_select_fusion), channel_id=1, source_target_pairs={{0,2},{1,7},{8,10},{9,15},{16,18},{17,23},{24,26},{25,31},{32,34},... | collective-permute-start | bytes 3145736 | tf_op jit(solution)/shard_map/ppermute | solution.py:260
  25.9 13.6 %collective-permute-start.2 = (bf16[512,1024]{1,0:T(8,128)(2,1)S(1)}, bf16[512,1024]{1,0:T(8,128)(2,1)S(1)}, u32[]{:S(2)}, u32[]{:S(2)}) collective-permute-start(bf16[512,1024]{1,0:T(8,128)(2,1)S(1)} %broadcast_select_fusion), channel_id=1, source_target_pairs={{0,6},{1,3},{2,4},{7,5},{8,14},{9,11},{10,12},{15,13},{16,22},{17,... | collective-permute-start | bytes 3145736 | tf_op jit(solution)/shard_map/ppermute | solution.py:262
  39.6 3.2 %copy-start.1 = (bf16[512,1024]{1,0:T(8,128)(2,1)}, bf16[512,1024]{1,0:T(8,128)(2,1)S(1)}, u32[]{:S(2)}) copy-start(bf16[512,1024]{1,0:T(8,128)(2,1)S(1)} %broadcast_select_fusion.1.own) | copy-start | bytes 3145732
  39.6 3.2 %collective-permute-start.3 = (bf16[512,1024]{1,0:T(8,128)(2,1)S(1)}, bf16[512,1024]{1,0:T(8,128)(2,1)S(1)}, u32[]{:S(2)}, u32[]{:S(2)}) collective-permute-start(bf16[512,1024]{1,0:T(8,128)(2,1)S(1)} %broadcast_select_fusion.1.own), channel_id=1, source_target_pairs={{0,1},{1,0},{2,3},{3,2},{4,5},{5,4},{6,7},{7,6},{8,9},{9,8},{10,11... | collective-permute-start | bytes 3145736 | tf_op jit(solution)/shard_map/ppermute | solution.py:252
  42.8 1.0 copy-start.2
  49.9 23.4 %collective-permute-start.6 = (s16[256,2176]{1,0:T(8,128)(2,1)}, s16[256,2176]{1,0:T(8,128)(2,1)S(1)}, u32[]{:S(2)}, u32[]{:S(2)}) collective-permute-start(s16[256,2176]{1,0:T(8,128)(2,1)} %first_3.1), channel_id=1, source_target_pairs={{0,96},{1,25},{8,104},{9,1},{16,112},{17,9},{24,120},{25,17},{32,0... | collective-permute-start | bytes 3342344 | tf_op jit(solution)/shard_map/ppermute | solution.py:248
  58.8 28.9 %collective-permute-start.5 = (s16[256,2176]{1,0:T(8,128)(2,1)}, s16[256,2176]{1,0:T(8,128)(2,1)S(1)}, u32[]{:S(2)}, u32[]{:S(2)}) collective-permute-start(s16[256,2176]{1,0:T(8,128)(2,1)} %first_1.1), channel_id=1, source_target_pairs={{0,32},{1,9},{8,40},{9,17},{16,48},{17,25},{24,56},{25,1},{32,64},... | collective-permute-start | bytes 3342344 | tf_op jit(solution)/shard_map/ppermute | solution.py:248
  65.1 22.6 %collective-permute-start.4 = (s16[256,2176]{1,0:T(8,128)(2,1)}, s16[256,2176]{1,0:T(8,128)(2,1)S(1)}, u32[]{:S(2)}, u32[]{:S(2)}) collective-permute-start(s16[256,2176]{1,0:T(8,128)(2,1)} %first_2.1), channel_id=1, source_target_pairs={{0,64},{1,17},{8,72},{9,25},{16,80},{17,1},{24,88},{25,9},{32,96},... | collective-permute-start | bytes 3342344 | tf_op jit(solution)/shard_map/ppermute | solution.py:248
  73.3 14.4 %copy-start.7 = (s16[256,2176]{1,0:T(8,128)(2,1)}, s16[256,2176]{1,0:T(8,128)(2,1)S(1)}, u32[]{:S(2)}) copy-start(s16[256,2176]{1,0:T(8,128)(2,1)S(1)} %collective-permute-done.6.c) | copy-start | bytes 3342340
  87.7 1.0 copy-start.8
  88.7 1.1 copy-start.9
  95.5 8.3 %collective-permute-start.7 = (s16[64,2176]{1,0:T(8,128)(2,1)}, s16[64,2176]{1,0:T(8,128)(2,1)S(1)}, u32[]{:S(2)}, u32[]{:S(2)}) collective-permute-start(s16[64,2176]{1,0:T(8,128)(2,1)} %get-tuple-element.22), channel_id=1, source_target_pairs={{0,16},{1,65},{8,24},{9,73},{16,0},{17,81},{24,8},{25,89},{32,48},... | collective-permute-start | bytes 835592 | tf_op jit(solution)/shard_map/ppermute | solution.py:248
  98.7 8.1 %collective-permute-start.8 = (s16[64,2176]{1,0:T(8,128)(2,1)}, s16[64,2176]{1,0:T(8,128)(2,1)S(1)}, u32[]{:S(2)}, u32[]{:S(2)}) collective-permute-start(s16[64,2176]{1,0:T(8,128)(2,1)} %get-tuple-element.23), channel_id=1, source_target_pairs={{0,8},{1,33},{8,16},{9,41},{16,24},{17,49},{24,0},{25,57},{32,40},... | collective-permute-start | bytes 835592 | tf_op jit(solution)/shard_map/ppermute | solution.py:248
  99.3 7.7 %collective-permute-start.9 = (s16[64,2176]{1,0:T(8,128)(2,1)}, s16[64,2176]{1,0:T(8,128)(2,1)S(1)}, u32[]{:S(2)}, u32[]{:S(2)}) collective-permute-start(s16[64,2176]{1,0:T(8,128)(2,1)} %get-tuple-element.24), channel_id=1, source_target_pairs={{0,24},{1,97},{8,0},{9,105},{16,8},{17,113},{24,16},{25,121},{32,5... | collective-permute-start | bytes 835592 | tf_op jit(solution)/shard_map/ppermute | solution.py:248
  103.7 3.3 %copy-start.13 = (s16[64,2176]{1,0:T(8,128)(2,1)}, s16[64,2176]{1,0:T(8,128)(2,1)S(1)}, u32[]{:S(2)}) copy-start(s16[64,2176]{1,0:T(8,128)(2,1)S(1)} %collective-permute-done.7.a) | copy-start | bytes 835588
  106.7 0.7 copy-start.14
  107.0 0.7 copy-start.15
  110.1 8.0 %collective-permute-start.10 = (s16[64,2176]{1,0:T(8,128)(2,1)}, s16[64,2176]{1,0:T(8,128)(2,1)S(1)}, u32[]{:S(2)}, u32[]{:S(2)}) collective-permute-start(s16[64,2176]{1,0:T(8,128)(2,1)} %gather.1), channel_id=1, source_target_pairs={{0,8},{1,33},{8,16},{9,41},{16,24},{17,49},{24,0},{25,57},{32,40},... | collective-permute-start | bytes 835592 | tf_op jit(solution)/shard_map/ppermute | solution.py:248
  111.6 10.5 %collective-permute-start.11 = (s16[64,2176]{1,0:T(8,128)(2,1)}, s16[64,2176]{1,0:T(8,128)(2,1)S(1)}, u32[]{:S(2)}, u32[]{:S(2)}) collective-permute-start(s16[64,2176]{1,0:T(8,128)(2,1)} %gather.1), channel_id=1, source_target_pairs={{0,16},{1,65},{8,24},{9,73},{16,0},{17,81},{24,8},{25,89},{32,48},... | collective-permute-start | bytes 835592 | tf_op jit(solution)/shard_map/ppermute | solution.py:248
  114.4 7.7 %collective-permute-start.12 = (s16[64,2176]{1,0:T(8,128)(2,1)}, s16[64,2176]{1,0:T(8,128)(2,1)S(1)}, u32[]{:S(2)}, u32[]{:S(2)}) collective-permute-start(s16[64,2176]{1,0:T(8,128)(2,1)} %gather.1), channel_id=1, source_target_pairs={{0,24},{1,97},{8,0},{9,105},{16,8},{17,113},{24,16},{25,121},{32,5... | collective-permute-start | bytes 835592 | tf_op jit(solution)/shard_map/ppermute | solution.py:248
  123.2 3.3 %copy-start.3 = (s16[256,2176]{1,0:T(8,128)(2,1)}, s16[256,2176]{1,0:T(8,128)(2,1)S(1)}, u32[]{:S(2)}) copy-start(s16[256,2176]{1,0:T(8,128)(2,1)S(1)} %pad_add_fusion.coded) | copy-start | bytes 3342340
  123.2 28.8 %collective-permute-start.15 = (s16[256,2176]{1,0:T(8,128)(2,1)S(1)}, s16[256,2176]{1,0:T(8,128)(2,1)}, u32[]{:S(2)}, u32[]{:S(2)}) collective-permute-start(s16[256,2176]{1,0:T(8,128)(2,1)S(1)} %pad_add_fusion.coded), channel_id=1, source_target_pairs={{0,32},{1,9},{8,40},{9,17},{16,48},{17,25},{24,56},{25,1},{32,64},... | collective-permute-start | bytes 3342344 | tf_op jit(solution)/shard_map/ppermute | solution.py:248
  123.2 35.5 %collective-permute-start.14 = (s16[256,2176]{1,0:T(8,128)(2,1)S(1)}, s16[256,2176]{1,0:T(8,128)(2,1)S(1)}, u32[]{:S(2)}, u32[]{:S(2)}) collective-permute-start(s16[256,2176]{1,0:T(8,128)(2,1)S(1)} %pad_add_fusion.coded), channel_id=1, source_target_pairs={{0,96},{1,25},{8,104},{9,1},{16,112},{17,9},{24,120},{25,17},{32,0... | collective-permute-start | bytes 3342344 | tf_op jit(solution)/shard_map/ppermute | solution.py:248
  126.5 39.8 %collective-permute-start.13 = (s16[256,2176]{1,0:T(8,128)(2,1)S(1)}, s16[256,2176]{1,0:T(8,128)(2,1)S(1)}, u32[]{:S(2)}, u32[]{:S(2)}) collective-permute-start(s16[256,2176]{1,0:T(8,128)(2,1)S(1)} %pad_add_fusion.coded), channel_id=1, source_target_pairs={{0,64},{1,17},{8,72},{9,25},{16,80},{17,1},{24,88},{25,9},{32,96},... | collective-permute-start | bytes 3342344 | tf_op jit(solution)/shard_map/ppermute | solution.py:248
  158.7 1.0 copy-start.6
  166.3 1.0 copy-start.5
  173.9 4.4 %collective-permute-start.16 = (f32[512,1024]{1,0:T(8,128)}, f32[512,1024]{1,0:T(8,128)S(1)}, u32[]{:S(2)}, u32[]{:S(2)}) collective-permute-start(f32[512,1024]{1,0:T(8,128)} %get-tuple-element.32), channel_id=1, source_target_pairs={{0,1},{1,0},{2,3},{3,2},{4,5},{5,4},{6,7},{7,6},{8,9},{9,8},{10,11... | collective-permute-start | bytes 6291464 | tf_op jit(solution)/shard_map/ppermute | solution.py:252
  178.3 1.4 copy-start.4
  184.7 12.9 %collective-permute-start.17 = (s16[128,1152]{1,0:T(8,128)(2,1)}, s16[128,1152]{1,0:T(8,128)(2,1)S(1)}, u32[]{:S(2)}, u32[]{:S(2)}) collective-permute-start(s16[128,1152]{1,0:T(8,128)(2,1)} %get-tuple-element.34), channel_id=1, source_target_pairs={{0,4},{2,6},{4,0},{6,2},{1,5},{3,7},{5,1},{7,3},{8,12},{10,14},{12... | collective-permute-start | bytes 884744 | tf_op jit(solution)/shard_map/ppermute | solution.py:299
  189.5 13.8 %collective-permute-start.18 = (s16[128,1152]{1,0:T(8,128)(2,1)}, s16[128,1152]{1,0:T(8,128)(2,1)S(1)}, u32[]{:S(2)}, u32[]{:S(2)}) collective-permute-start(s16[128,1152]{1,0:T(8,128)(2,1)} %get-tuple-element.35), channel_id=1, source_target_pairs={{0,2},{2,4},{4,6},{6,0},{1,3},{3,5},{5,7},{7,1},{8,10},{10,12},{12... | collective-permute-start | bytes 884744 | tf_op jit(solution)/shard_map/ppermute | solution.py:299
  189.5 13.8 %collective-permute-start.19 = (s16[128,1152]{1,0:T(8,128)(2,1)}, s16[128,1152]{1,0:T(8,128)(2,1)S(1)}, u32[]{:S(2)}, u32[]{:S(2)}) collective-permute-start(s16[128,1152]{1,0:T(8,128)(2,1)} %get-tuple-element.36), channel_id=1, source_target_pairs={{0,6},{2,0},{4,2},{6,4},{1,7},{3,1},{5,3},{7,5},{8,14},{10,8},{12,... | collective-permute-start | bytes 884744 | tf_op jit(solution)/shard_map/ppermute | solution.py:299
  197.6 5.7 %copy-start.10 = (s16[128,1152]{1,0:T(8,128)(2,1)}, s16[128,1152]{1,0:T(8,128)(2,1)S(1)}, u32[]{:S(2)}) copy-start(s16[128,1152]{1,0:T(8,128)(2,1)S(1)} %collective-permute-done.17.a) | copy-start | bytes 884740
  203.3 0.7 copy-start.11
  203.3 0.8 copy-start.12

commit v2 on v0

v2 whole, which is shorter than its diff:
```python
import functools

import jax
import jax.numpy as jnp
from jax import lax
from jax.experimental import pallas as pl
from jax.experimental.pallas import tpu as pltpu
from jax.sharding import Mesh
from jax.sharding import PartitionSpec as P

BLOCK = 128
SLAB = 1024
WIDE = 2048
LANES = 128
QUARTER = SLAB // 4
PIECE = SLAB // 16
AXES = ("x", "y", "z", "core")
F32, BF16, I16, I32 = jnp.float32, jnp.bfloat16, jnp.int16, jnp.int32

SENT = ((1, 0, 0, 0), (2, 2, 1, 1), (3, 3, 3, 2))
SECOND, CORE, OWNER, HALF, BASE = range(4, 9)


def shape(rows, columns, dtype):
    return jax.ShapeDtypeStruct((rows, columns), dtype)


def call(kernel, out, s, *args, name, flops=1 << 22, scratch=()):
    in_vmem = pl.BlockSpec(memory_space=pltpu.VMEM)
    return pl.pallas_call(
        kernel,
        out_shape=out,
        in_specs=[pl.BlockSpec(memory_space=pltpu.SMEM)] * len(s) + [in_vmem] * len(args),
        out_specs=jax.tree.map(lambda _: in_vmem, out),
        scratch_shapes=list(scratch),
        compiler_params=pltpu.CompilerParams(vmem_limit_bytes=16 << 20),
        cost_estimate=pl.CostEstimate(flops=flops, bytes_accessed=4 << 20, transcendentals=0),
        name=name,
    )(*s, *args)


def encode(v):
    top = jnp.max(jnp.abs(v), axis=1, keepdims=True)
    e = jnp.clip(jnp.floor(jnp.log2(top)) + 1.0, -100.0, 128.0)
    q = jnp.clip(jnp.round(v * jnp.exp2(15.0 - e)), -32767.0, 32767.0)
    tail = jnp.broadcast_to(e, (v.shape[0], LANES))
    return q.astype(I32).astype(I16), tail.astype(I32).astype(I16)


def put(ref, v):
    q, tail = encode(v)
    width = v.shape[1]
    ref[:, :width] = q
    ref[:, width:] = tail


def take(ref, rows=slice(None)):
    width = ref.shape[1] - LANES
    e = ref[rows, width:].astype(I32).astype(F32)
    scale = jnp.exp2(e - 15.0)[:, :1]
    return ref[rows, :width].astype(I32).astype(F32) * scale


def at(i, size):
    return pl.ds(pl.multiple_of(i * size, size), size)


def masked_block(m, density, i, j):
    block = density[i * BLOCK : (i + 1) * BLOCK, j * BLOCK : (j + 1) * BLOCK]
    return jnp.where(m[i, j] != 0, block, jnp.zeros_like(block))


def column_kernel(s, m, density, top_a, low_a, top_b, low_b, whole):
    for i in range(8):
        for j in range(8):
            whole[i * BLOCK : (i + 1) * BLOCK, j * BLOCK : (j + 1) * BLOCK] = masked_block(m, density, i, j)
    for i, (top, low) in enumerate(((top_a, low_a), (top_b, low_b))):
        for j in range(2):
            columns = at((s[BASE] + 2 * i + j) % 4, QUARTER)
            to = slice(j * QUARTER, (j + 1) * QUARTER)
            top[:, to] = whole[:512, columns]
            low[:, to] = whole[512:, columns]


def mask_kernel(m, density, out):
    for i in range(8):
        for j in range(16):
            out[i * BLOCK : (i + 1) * BLOCK, j * BLOCK : (j + 1) * BLOCK] = masked_block(m, density, i, j)


def first_kernel(i, coded, s, *refs):
    *parts, masked, out, left, acc = refs
    for half, (own, other) in enumerate(zip(parts[::2], parts[1::2])):

        @pl.when(s[i] // 2 == half)
        def _(own=own, other=other):
            left[:512] = own[:, at(s[i] % 2, QUARTER)]
            left[512:] = other[:, at(s[i] % 2, QUARTER)]

    dims = (((0,), (0,)), ((), ()))
    to = acc if coded else out
    for n in range(4):
        columns = slice(n * 512, (n + 1) * 512)
        to[:, columns] = lax.dot_general(
            left[:512], masked[at(s[CORE], 512), columns], dims, preferred_element_type=F32
        ) + lax.dot_general(
            left[512:], masked[at(1 - s[CORE], 512), columns], dims, preferred_element_type=F32
        )
    if coded:
        put(out, acc[...])


def first_product(i, s, parts, masked, coded=True):
    out = shape(QUARTER, WIDE + LANES, I16) if coded else shape(QUARTER, WIDE, F32)
    return call(
        functools.partial(first_kernel, i, coded),
        out,
        [s],
        *parts,
        masked,
        name=f"first_{i}",
        flops=2 * QUARTER * SLAB * WIDE,
        scratch=[pltpu.VMEM((SLAB, QUARTER), BF16), pltpu.VMEM((QUARTER, WIDE), F32)],
    )


def spread_kernel(s, own, a, b, c, *outs):
    for d, out in enumerate(outs):
        rows = at((s[SECOND] + d) % 4, PIECE)
        v = own[rows, :] + take(a, rows) + take(b, rows) + take(c, rows)
        if d == 0:
            out[...] = v
        else:
            put(out, v)


def gather_kernel(own, a, b, c, out):
    put(out, own[...] + take(a) + take(b) + take(c))


def join_kernel(*refs):
    *parts, out = refs
    for i, part in enumerate(parts):
        out[i * PIECE : (i + 1) * PIECE] = part[...]


def second_kernel(s, coded, masked, mine, theirs, left):
    pieces = []
    for j in range(4):
        sub = (s[SECOND] + 4 - j) % 4
        start = ((sub // 2) ^ s[CORE]) * 128 + (sub % 2) * 64
        rows = pl.ds(pl.multiple_of(start, 64), PIECE)
        left[rows, :] = take(coded, slice(j * PIECE, (j + 1) * PIECE)).astype(BF16)
        pieces.append((j, start))
    for n in range(4):
        columns = slice(n * 256, (n + 1) * 256)
        t = -2.0 * lax.dot_general(
            left[...],
            masked[columns, :],
            (((1,), (1,)), ((), ())),
            preferred_element_type=F32,
        )
        mine[:, columns] = t[:128]
        theirs[:, columns] = t[128:]

    for half in range(2):

        @pl.when((s[OWNER] == 1) & (s[HALF] == half))
        def _(half=half):
            for j, start in pieces:
                v = take(coded, slice(j * PIECE, (j + 1) * PIECE))
                v = 3.0 * v[:, half * SLAB : (half + 1) * SLAB]

                @pl.when(start < 128)
                def _(v=v, start=start):
                    mine[pl.ds(pl.multiple_of(start, 64), PIECE), :] += v

                @pl.when(start >= 128)
                def _(v=v, start=start):
                    theirs[pl.ds(pl.multiple_of(start - 128, 64), PIECE), :] += v


def second_product(j, s, coded, masked):
    return call(
        second_kernel,
        [shape(128, SLAB, F32)] * 2,
        [s],
        coded,
        masked,
        name=f"second_{j}",
        flops=2 * QUARTER * SLAB * WIDE,
        scratch=[pltpu.VMEM((QUARTER, WIDE), BF16)],
    )


def pair_kernel(mine, came, out):
    put(out, mine[...] + came[...])


def finish_kernel(a, b, c, d, out):
    out[...] = take(a) + take(b) + take(c) + take(d)


def place(x, y, z, core):
    return ((x % 4 * 4 + y % 4) * 4 + z % 4) * 2 + core


DEVICES = [(x, y, z, c) for x in range(4) for y in range(4) for z in range(4) for c in range(2)]


def send(v, to):
    return lax.ppermute(v, AXES, [(place(*d), place(*to(*d))) for d in DEVICES])


def own_quarter(y, x, z, core):
    return (z - jnp.where(core == 0, y, x)) & 3


def along(v, shift):
    def to(x, y, z, core):
        d = shift(x if core else y, z)
        return (x, y + d, z, core) if core else (x + d, y, z, core)

    return send(v, to)


def across(v, d):
    return send(v, lambda x, y, z, core: (x + d, y, z, core) if core else (x, y + d, z, core))


def swap(v):
    return lax.ppermute(v, "core", [(0, 1), (1, 0)])


def spread_column(top, low, z, core):
    came = lax.ppermute(low, "core", [(0, 1), (1, 0)])
    half = jnp.where(core == 0, top, came)
    axes = ("z", "core")
    came = lax.ppermute(half, axes, [(0, 2), (1, 7)])
    half = jnp.where(z == 0, half, came)
    came = lax.ppermute(half, axes, [(0, 6), (1, 3), (2, 4), (7, 5)])
    late = (z == 2) | ((z == 3) & (core == 0)) | ((z == 1) & (core == 1))
    half = jnp.where(late, came, half)
    return half, swap(half)


def coordinates():
    x, y, z, core = (lax.axis_index(a) for a in AXES)
    row = x * 4 + y
    own = own_quarter(y, x, z, core)
    values = [sum((own == i).astype(I32) * b for i, b in enumerate(sent)) for sent in SENT]
    values += [own, jnp.where(core == 0, y, x), core]
    values += [(z * 2 + core == row >> 1).astype(I32), row & 1, (x + y) & 3]
    s = jnp.zeros((16,), I32)
    index = jnp.arange(16, dtype=I32)
    for i, v in enumerate(values):
        s = jnp.where(index == i, v, s)
    return s, z, core


def local(density, block_mask):
    s, z, core = coordinates()
    top_a, low_a, top_b, low_b = call(
        column_kernel,
        [shape(512, 512, BF16)] * 4,
        [s, block_mask],
        density,
        name="column",
        scratch=[pltpu.VMEM((SLAB, SLAB), BF16)],
    )
    masked = call(mask_kernel, shape(SLAB, WIDE, BF16), [block_mask], density, name="mask")
    near = spread_column(top_a, low_a, z, core)
    far = spread_column(top_b, low_b, z, core)

    came = []
    for i, parts in enumerate((near, near + far, near + far)):
        v = first_product(i, s, parts, masked)
        came.append(along(v, lambda second, z: SENT[i][(z - second) % 4] - (z - second)))
    mine = first_product(3, s, near + far, masked, False)
    wide, coded = shape(PIECE, WIDE, F32), shape(PIECE, WIDE + LANES, I16)
    mine, *parts = call(spread_kernel, [wide, coded, coded, coded], [s], mine, *came, name="spread")
    came = [across(parts[d - 1], d) for d in (2, 1, 3)]
    v = call(gather_kernel, coded, [], mine, *came, name="gather")

    parts = [across(v, d) for d in (1, 2, 3)]
    v = call(join_kernel, shape(QUARTER, WIDE + LANES, I16), [], v, *parts, name="join")
    quarters = [along(v, lambda second, z: j - second) for j in range(4)]
    came = []
    for j, v in enumerate(quarters):
        mine, theirs = second_product(j, s, v, masked)
        v = call(pair_kernel, shape(128, SLAB + LANES, I16), [], mine, swap(theirs), name="pair")
        came.append(send(v, lambda x, y, z, core: (x, y, x + y + z - j, core)))
    return call(finish_kernel, shape(128, SLAB, F32), [], *came, name="finish")


def solution(mesh):
    torus = Mesh(mesh.devices.reshape(4, 4, 4, 2), AXES)
    in_specs = (P(("x", "y"), ("z", "core")),) * 2
    out_specs = P(("z", "core"), ("x", "y"))
    return jax.shard_map(local, mesh=torus, in_specs=in_specs, out_specs=out_specs, check_vma=False)
```

time: 317 us -> 169 us (0.53)
  waiting for transfers between devices: 271 us -> 84.8 us
  starting transfers between devices: 0.12 us -> 49.4 us
  Pallas kernels: 0 us -> 26.2 us
  matrix products: 23 us -> 0 us
  between operations: 13.2 us -> 0.38 us
    psum x3 -> x0, waiting for transfers between devices: 234 us -> none  [the longest x1 143 us: local(): lax.psum(lax.dot_general(left_part, masked, (((0,), (0,)), ((), ())), pre...]
    ppermute x0 -> x29, waiting for transfers between devices: none -> 84.8 us  [the longest x17 63.4 us: send(): return lax.ppermute(v, AXES, [(place(*d), place(*to(*d))) for d in DEVICES])]
    ppermute x0 -> x29, starting transfers between devices: none -> 49.4 us  [the longest x17 39.1 us: send(): return lax.ppermute(v, AXES, [(place(*d), place(*to(*d))) for d in DEVICES])]
    reduce_scatter x1 -> x0, waiting for transfers between devices: 37.3 us -> none  [local(): lax.psum_scatter(3.0 * weight * own_square - 2.0 * lax.dot_general(left_p...]
    pallas_call x0 -> x18, Pallas kernels: none -> 26.2 us  [call(): pl.pallas_call(kernel, out_shape=out, in_specs=[pl.BlockSpec(memory_space...]
    dot_general x2 -> x0, matrix products: 23 us -> none  [the longest x1 12.3 us: local(): lax.dot_general(left_part, masked, (((1,), (1,)), ((), ())), preferred_el...]
    broadcast_in_dim x2 -> x0, local copies, waits for them, and re-layouts: 4.5 us -> none  [the longest x1 4.46 us: local(): jnp.repeat(jnp.repeat(block_mask.astype(jnp.bfloat16), BLOCK, 0), BLOCK, 1)]
  transfers between devices with their start and end apart: 4 -> 29, of which waited for: 4 -> 19; matrix products, arithmetic and copies ran while one was open for 0% -> 0% of each run, Pallas kernels for 0% -> 13%
where the time goes in v2:
time: 169 us; the launch traced here: 166 us
  waiting for transfers between devices  84.8 us (50%)
  starting transfers between devices  49.4 us (29%)
  Pallas kernels  26.2 us (16%)
  local copies, waits for them, and re-layouts  5.06 us (3%)
    ppermute x17, waiting for transfers between devices, send(): return lax.ppermute(v, AXES, [(place(*d), place(*to(*d))) for d in DEVICES])  63.4 us
    ppermute x17, starting transfers between devices, send(): return lax.ppermute(v, AXES, [(place(*d), place(*to(*d))) for d in DEVICES])  39.1 us
    pallas_call x18, Pallas kernels, call(): pl.pallas_call(kernel, out_shape=out, in_specs=[pl.BlockSpec(memory_space...  26.2 us
    ppermute x2, waiting for transfers between devices, spread_column(): came = lax.ppermute(half, axes, [(0, 2), (1, 7)])  11.9 us
    ppermute x2, waiting for transfers between devices, spread_column(): came = lax.ppermute(half, axes, [(0, 6), (1, 3), (2, 4), (7, 5)])  8.07 us
    ppermute x2, starting transfers between devices, spread_column(): came = lax.ppermute(half, axes, [(0, 2), (1, 7)])  5.29 us
    unnamed x8, local copies, waits for them, and re-layouts  5.06 us
  transfers between devices with their start and end apart: 29, of which 19 were waited for; matrix products, arithmetic and copies ran while one was open for 0% of the time, Pallas kernels for 13%

profile of v2, /device:TPU:0, one launch (start us, length us, event | category | flops | bytes accessed | tf_op | source)
XLA Modules:
  0.0 166.2 jit_solution(4660160857439429635)
XLA Ops:
  0.0 2.2 %copy-done = bf16[1024,2048]{1,0:T(8,128)(2,1)S(1)} copy-done((bf16[1024,2048]{1,0:T(8,128)(2,1)S(1)}, bf16[1024,2048]{1,0:T(8,128)(2,1)}, u32[]{:S(2)}) %copy-start) | copy-done | bytes 4194328
  2.9 1.5 column.1
  5.0 1.4 collective-permute-done
  6.4 4.0 %collective-permute-start.1 = (bf16[512,512]{1,0:T(8,128)(2,1)S(1)}, bf16[512,512]{1,0:T(8,128)(2,1)S(1)}, u32[]{:S(2)}, u32[]{:S(2)}) collective-permute-start(bf16[512,512]{1,0:T(8,128)(2,1)S(1)} %broadcast_select_fusion.1), channel_id=1, source_target_pairs={{0,2},{1,7},{8,10},{9,15},{16,18},{17,23},{24,26},{25,31},{32,34},... | collective-permute-start | bytes 1572872 | tf_op jit(solution)/shard_map/ppermute | solution.py:239
  10.5 1.3 collective-permute-start.5
  11.8 5.2 %collective-permute-done.1 = bf16[512,512]{1,0:T(8,128)(2,1)S(1)} collective-permute-done((bf16[512,512]{1,0:T(8,128)(2,1)S(1)}, bf16[512,512]{1,0:T(8,128)(2,1)S(1)}, u32[]{:S(2)}, u32[]{:S(2)}) %collective-permute-start.1) | collective-permute-done | bytes 524320 | tf_op jit(solution)/shard_map/ppermute | solution.py:239
  17.1 1.3 collective-permute-start.2
  18.4 6.7 %collective-permute-done.5 = bf16[512,512]{1,0:T(8,128)(2,1)S(1)} collective-permute-done((bf16[512,512]{1,0:T(8,128)(2,1)S(1)}, bf16[512,512]{1,0:T(8,128)(2,1)S(1)}, u32[]{:S(2)}, u32[]{:S(2)}) %collective-permute-start.5) | collective-permute-done | bytes 524320 | tf_op jit(solution)/shard_map/ppermute | solution.py:239
  25.2 1.3 collective-permute-start.6
  26.6 3.0 %collective-permute-done.2 = bf16[512,512]{1,0:T(8,128)(2,1)S(1)} collective-permute-done((bf16[512,512]{1,0:T(8,128)(2,1)S(1)}, bf16[512,512]{1,0:T(8,128)(2,1)S(1)}, u32[]{:S(2)}, u32[]{:S(2)}) %collective-permute-start.2) | collective-permute-done | bytes 524320 | tf_op jit(solution)/shard_map/ppermute | solution.py:241
  30.1 5.1 %collective-permute-done.6 = bf16[512,512]{1,0:T(8,128)(2,1)S(1)} collective-permute-done((bf16[512,512]{1,0:T(8,128)(2,1)S(1)}, bf16[512,512]{1,0:T(8,128)(2,1)S(1)}, u32[]{:S(2)}, u32[]{:S(2)}) %collective-permute-start.6) | collective-permute-done | bytes 524320 | tf_op jit(solution)/shard_map/ppermute | solution.py:241
  36.2 2.2 %copy-done.1 = bf16[1024,2048]{1,0:T(8,128)(2,1)S(1)} copy-done((bf16[1024,2048]{1,0:T(8,128)(2,1)S(1)}, bf16[1024,2048]{1,0:T(8,128)(2,1)}, u32[]{:S(2)}) %copy-start.1) | copy-done | bytes 4194328
  38.3 1.8 %mask.1.refs_4_.refs_2_.masked = bf16[1024,2048]{1,0:T(8,128)(2,1)S(1)} custom-call(s32[8,16]{1,0:T(8,128)S(1)} %copy-done.3, bf16[1024,2048]{1,0:T(8,128)(2,1)S(1)} %copy-done.1), custom_call_target="tpu_custom_call" | custom-call | flops 4194304 | bytes 4194304 | tf_op jit(solution)/shard_map/mask/pallas_call | solution.py:30
  40.2 2.2 %first_0.1 = s16[256,2176]{1,0:T(8,128)(2,1)S(1)} custom-call(s32[16]{0:T(128)S(1)} %compare_select_fusion.8.s, bf16[512,512]{1,0:T(8,128)(2,1)S(1)} %broadcast_select_fusion.5.refs_0_, bf16[512,512]{1,0:T(8,128)(2,1)S(1)} %collective-permute-done.3.refs_1_, bf16[1024,2048]{1,0:T(8,128)(2,1)S(1)} %mask.1.refs_4_.refs_2_.masked), custom_call_target="tpu_custom_call" | custom-call | flops 1073741824 | bytes 4194304 | tf_op jit(solution)/shard_map/first_0/pallas_call | solution.py:30
  42.4 1.6 collective-permute-start.8
  43.9 2.2 %first_1.1 = s16[256,2176]{1,0:T(8,128)(2,1)S(1)} custom-call(s32[16]{0:T(128)S(1)} %compare_select_fusion.8.s, bf16[512,512]{1,0:T(8,128)(2,1)S(1)} %broadcast_select_fusion.5.refs_0_, bf16[512,512]{1,0:T(8,128)(2,1)S(1)} %collective-permute-done.3.refs_1_, bf16[512,512]{1,0:T(8,128)(2,1)S(1)} %broadcast_select_fusion.4.refs_2_, ...), custom_call_target="tpu_custom_call" | custom-call | flops 1073741824 | bytes 4194304 | tf_op jit(solution)/shard_map/first_1/pallas_call | solution.py:30
  46.2 2.8 %collective-permute-start.9 = (s16[256,2176]{1,0:T(8,128)(2,1)S(1)}, s16[256,2176]{1,0:T(8,128)(2,1)S(1)}, u32[]{:S(2)}, u32[]{:S(2)}) collective-permute-start(s16[256,2176]{1,0:T(8,128)(2,1)S(1)} %first_1.1), channel_id=1, source_target_pairs={{0,64},{1,17},{2,34},{3,11},{4,100},{5,29},{6,70},{7,23},{8,72},{9... | collective-permute-start | bytes 3342344 | tf_op jit(solution)/shard_map/ppermute | solution.py:212
  49.0 2.2 %first_2.1 = s16[256,2176]{1,0:T(8,128)(2,1)S(1)} custom-call(s32[16]{0:T(128)S(1)} %compare_select_fusion.8.s, bf16[512,512]{1,0:T(8,128)(2,1)S(1)} %broadcast_select_fusion.5.refs_0_, bf16[512,512]{1,0:T(8,128)(2,1)S(1)} %collective-permute-done.3.refs_1_, bf16[512,512]{1,0:T(8,128)(2,1)S(1)} %broadcast_select_fusion.4.refs_2_, ...), custom_call_target="tpu_custom_call" | custom-call | flops 1073741824 | bytes 4194304 | tf_op jit(solution)/shard_map/first_2/pallas_call | solution.py:30
  51.2 1.5 collective-permute-start.10
  52.7 1.9 %first_3.1.own = f32[256,2048]{1,0:T(8,128)S(1)} custom-call(s32[16]{0:T(128)S(1)} %compare_select_fusion.8.s, bf16[512,512]{1,0:T(8,128)(2,1)S(1)} %broadcast_select_fusion.5.refs_0_, bf16[512,512]{1,0:T(8,128)(2,1)S(1)} %collective-permute-done.3.refs_1_, bf16[512,512]{1,0:T(8,128)(2,1)S(1)} %broadcast_select_fusion.4.refs_2_, ...), custom_call_target="tpu_custom_call" | custom-call | flops 1073741824 | bytes 4194304 | tf_op jit(solution)/shard_map/first_3/pallas_call | solution.py:30
  54.6 4.5 %collective-permute-done.8.a = s16[256,2176]{1,0:T(8,128)(2,1)S(1)} collective-permute-done((s16[256,2176]{1,0:T(8,128)(2,1)S(1)}, s16[256,2176]{1,0:T(8,128)(2,1)S(1)}, u32[]{:S(2)}, u32[]{:S(2)}) %collective-permute-start.8) | collective-permute-done | bytes 1114144 | tf_op jit(solution)/shard_map/ppermute | solution.py:212
  59.2 12.9 %collective-permute-done.9.b = s16[256,2176]{1,0:T(8,128)(2,1)S(1)} collective-permute-done((s16[256,2176]{1,0:T(8,128)(2,1)S(1)}, s16[256,2176]{1,0:T(8,128)(2,1)S(1)}, u32[]{:S(2)}, u32[]{:S(2)}) %collective-permute-start.9) | collective-permute-done | bytes 1114144 | tf_op jit(solution)/shard_map/ppermute | solution.py:212
  72.1 2.2 %collective-permute-done.10.c = s16[256,2176]{1,0:T(8,128)(2,1)S(1)} collective-permute-done((s16[256,2176]{1,0:T(8,128)(2,1)S(1)}, s16[256,2176]{1,0:T(8,128)(2,1)S(1)}, u32[]{:S(2)}, u32[]{:S(2)}) %collective-permute-start.10) | collective-permute-done | bytes 1114144 | tf_op jit(solution)/shard_map/ppermute | solution.py:212
  74.3 1.7 %spread.1 = (f32[64,2048]{1,0:T(8,128)S(1)}, s16[64,2176]{1,0:T(8,128)(2,1)S(1)}, s16[64,2176]{1,0:T(8,128)(2,1)S(1)}, s16[64,2176]{1,0:T(8,128)(2,1)S(1)}) custom-call(s32[16]{0:T(128)S(1)} %compare_select_fusion.8.s, f32[256,2048]{1,0:T(8,128)S(1)} %first_3.1.own, s16[256,2176]{1,0:T(8,128)(2,1)S(1)} %collective-permute-done.8.a, ...), custom_call_target="tpu_custom_call" | custom-call | flops 4194304 | bytes 4194304 | tf_op jit(solution)/shard_map/spread/pallas_call | solution.py:30
  76.7 5.3 %collective-permute-start.12 = (s16[64,2176]{1,0:T(8,128)(2,1)S(1)}, s16[64,2176]{1,0:T(8,128)(2,1)S(1)}, u32[]{:S(2)}, u32[]{:S(2)}) collective-permute-start(s16[64,2176]{1,0:T(8,128)(2,1)S(1)} %get-tuple-element.27), channel_id=1, source_target_pairs={{0,8},{1,33},{2,10},{3,35},{4,12},{5,37},{6,14},{7,39},{8,16},{9,4... | collective-permute-start | bytes 835592 | tf_op jit(solution)/shard_map/ppermute | solution.py:212
  82.0 2.4 %collective-permute-done.11.a = s16[64,2176]{1,0:T(8,128)(2,1)S(1)} collective-permute-done((s16[64,2176]{1,0:T(8,128)(2,1)S(1)}, s16[64,2176]{1,0:T(8,128)(2,1)S(1)}, u32[]{:S(2)}, u32[]{:S(2)}) %collective-permute-start.11) | collective-permute-done | bytes 278560 | tf_op jit(solution)/shard_map/ppermute | solution.py:212
  84.4 2.9 %collective-permute-done.12.b = s16[64,2176]{1,0:T(8,128)(2,1)S(1)} collective-permute-done((s16[64,2176]{1,0:T(8,128)(2,1)S(1)}, s16[64,2176]{1,0:T(8,128)(2,1)S(1)}, u32[]{:S(2)}, u32[]{:S(2)}) %collective-permute-start.12) | collective-permute-done | bytes 278560 | tf_op jit(solution)/shard_map/ppermute | solution.py:212
  87.3 2.2 %collective-permute-done.13.c = s16[64,2176]{1,0:T(8,128)(2,1)S(1)} collective-permute-done((s16[64,2176]{1,0:T(8,128)(2,1)S(1)}, s16[64,2176]{1,0:T(8,128)(2,1)S(1)}, u32[]{:S(2)}, u32[]{:S(2)}) %collective-permute-start.13) | collective-permute-done | bytes 278560 | tf_op jit(solution)/shard_map/ppermute | solution.py:212
  89.9 2.7 %collective-permute-start.16 = (s16[64,2176]{1,0:T(8,128)(2,1)S(1)}, s16[64,2176]{1,0:T(8,128)(2,1)S(1)}, u32[]{:S(2)}, u32[]{:S(2)}) collective-permute-start(s16[64,2176]{1,0:T(8,128)(2,1)S(1)} %gather.1.refs_0_), channel_id=1, source_target_pairs={{0,24},{1,97},{2,26},{3,99},{4,28},{5,101},{6,30},{7,103},{8,0},{9... | collective-permute-start | bytes 835592 | tf_op jit(solution)/shard_map/ppermute | solution.py:212
  92.6 0.9 collective-permute-start.14
  93.5 6.1 %collective-permute-done.16.refs_3_ = s16[64,2176]{1,0:T(8,128)(2,1)S(1)} collective-permute-done((s16[64,2176]{1,0:T(8,128)(2,1)S(1)}, s16[64,2176]{1,0:T(8,128)(2,1)S(1)}, u32[]{:S(2)}, u32[]{:S(2)}) %collective-permute-start.16) | collective-permute-done | bytes 278560 | tf_op jit(solution)/shard_map/ppermute | solution.py:212
  99.7 1.1 collective-permute-done.15.refs_2_
  100.7 2.6 %collective-permute-done.14.refs_1_ = s16[64,2176]{1,0:T(8,128)(2,1)S(1)} collective-permute-done((s16[64,2176]{1,0:T(8,128)(2,1)S(1)}, s16[64,2176]{1,0:T(8,128)(2,1)S(1)}, u32[]{:S(2)}, u32[]{:S(2)}) %collective-permute-start.14) | collective-permute-done | bytes 278560 | tf_op jit(solution)/shard_map/ppermute | solution.py:212
  103.4 1.9 %collective-permute-start.26 = (s16[256,2176]{1,0:T(8,128)(2,1)S(1)}, s16[256,2176]{1,0:T(8,128)(2,1)S(1)}, u32[]{:S(2)}, u32[]{:S(2)}) collective-permute-start(s16[256,2176]{1,0:T(8,128)(2,1)S(1)} %join.1), channel_id=1, source_target_pairs={{0,96},{1,25},{2,98},{3,27},{4,100},{5,29},{6,102},{7,31},{8,72},{... | collective-permute-start | bytes 3342344 | tf_op jit(solution)/shard_map/ppermute | solution.py:212
  105.4 2.7 %collective-permute-start.23 = (s16[256,2176]{1,0:T(8,128)(2,1)S(1)}, s16[256,2176]{1,0:T(8,128)(2,1)S(1)}, u32[]{:S(2)}, u32[]{:S(2)}) collective-permute-start(s16[256,2176]{1,0:T(8,128)(2,1)S(1)} %join.1), channel_id=1, source_target_pairs={{0,64},{1,17},{2,66},{3,19},{4,68},{5,21},{6,70},{7,23},{8,40},{9,... | collective-permute-start | bytes 3342344 | tf_op jit(solution)/shard_map/ppermute | solution.py:212
  108.1 3.1 %collective-permute-start.20 = (s16[256,2176]{1,0:T(8,128)(2,1)S(1)}, s16[256,2176]{1,0:T(8,128)(2,1)S(1)}, u32[]{:S(2)}, u32[]{:S(2)}) collective-permute-start(s16[256,2176]{1,0:T(8,128)(2,1)S(1)} %join.1), channel_id=1, source_target_pairs={{0,32},{1,9},{2,34},{3,11},{4,36},{5,13},{6,38},{7,15},{8,8},{9,17... | collective-permute-start | bytes 3342344 | tf_op jit(solution)/shard_map/ppermute | solution.py:212
  112.0 8.9 %collective-permute-done.26.coded = s16[256,2176]{1,0:T(8,128)(2,1)S(1)} collective-permute-done((s16[256,2176]{1,0:T(8,128)(2,1)S(1)}, s16[256,2176]{1,0:T(8,128)(2,1)S(1)}, u32[]{:S(2)}, u32[]{:S(2)}) %collective-permute-start.26) | collective-permute-done | bytes 1114144 | tf_op jit(solution)/shard_map/ppermute | solution.py:212
  120.8 2.6 %second_3.1 = (f32[128,1024]{1,0:T(8,128)S(1)}, f32[128,1024]{1,0:T(8,128)S(1)}) custom-call(s32[16]{0:T(128)S(1)} %compare_select_fusion.8.s, s16[256,2176]{1,0:T(8,128)(2,1)S(1)} %collective-permute-done.26.coded, bf16[1024,2048]{1,0:T(8,128)(2,1)S(1)} %mask.1.refs_4_.refs_2_.masked), custom_call_target="tpu_custom_call" | custom-call | flops 1073741824 | bytes 4194304 | tf_op jit(solution)/shard_map/second_3/pallas_call | solution.py:30
  124.3 2.6 %second_2.1 = (f32[128,1024]{1,0:T(8,128)S(1)}, f32[128,1024]{1,0:T(8,128)S(1)}) custom-call(s32[16]{0:T(128)S(1)} %compare_select_fusion.8.s, s16[256,2176]{1,0:T(8,128)(2,1)S(1)} %collective-permute-done.23.coded, bf16[1024,2048]{1,0:T(8,128)(2,1)S(1)} %mask.1.refs_4_.refs_2_.masked), custom_call_target="tpu_custom_call" | custom-call | flops 1073741824 | bytes 4194304 | tf_op jit(solution)/shard_map/second_2/pallas_call | solution.py:30
  127.1 9.1 %collective-permute-done.20.coded = s16[256,2176]{1,0:T(8,128)(2,1)S(1)} collective-permute-done((s16[256,2176]{1,0:T(8,128)(2,1)S(1)}, s16[256,2176]{1,0:T(8,128)(2,1)S(1)}, u32[]{:S(2)}, u32[]{:S(2)}) %collective-permute-start.20) | collective-permute-done | bytes 1114144 | tf_op jit(solution)/shard_map/ppermute | solution.py:212
  136.2 2.6 %second_1.1 = (f32[128,1024]{1,0:T(8,128)S(1)}, f32[128,1024]{1,0:T(8,128)S(1)}) custom-call(s32[16]{0:T(128)S(1)} %compare_select_fusion.8.s, s16[256,2176]{1,0:T(8,128)(2,1)S(1)} %collective-permute-done.20.coded, bf16[1024,2048]{1,0:T(8,128)(2,1)S(1)} %mask.1.refs_4_.refs_2_.masked), custom_call_target="tpu_custom_call" | custom-call | flops 1073741824 | bytes 4194304 | tf_op jit(solution)/shard_map/second_1/pallas_call | solution.py:30
  138.9 2.6 %second_0.1 = (f32[128,1024]{1,0:T(8,128)S(1)}, f32[128,1024]{1,0:T(8,128)S(1)}) custom-call(s32[16]{0:T(128)S(1)} %compare_select_fusion.8.s, s16[256,2176]{1,0:T(8,128)(2,1)S(1)} %collective-permute-done.17.coded, bf16[1024,2048]{1,0:T(8,128)(2,1)S(1)} %mask.1.refs_4_.refs_2_.masked), custom_call_target="tpu_custom_call" | custom-call | flops 1073741824 | bytes 4194304 | tf_op jit(solution)/shard_map/second_0/pallas_call | solution.py:30
  141.8 4.8 %collective-permute-start.28 = (s16[128,1152]{1,0:T(8,128)(2,1)S(1)}, s16[128,1152]{1,0:T(8,128)(2,1)S(1)}, u32[]{:S(2)}, u32[]{:S(2)}) collective-permute-start(s16[128,1152]{1,0:T(8,128)(2,1)S(1)} %pair.7), channel_id=1, source_target_pairs={{0,2},{1,3},{2,4},{3,5},{4,6},{5,7},{6,0},{7,1},{8,12},{9,13},{10,... | collective-permute-start | bytes 884744 | tf_op jit(solution)/shard_map/ppermute | solution.py:212
  146.9 5.1 %collective-permute-start.25 = (s16[128,1152]{1,0:T(8,128)(2,1)S(1)}, s16[128,1152]{1,0:T(8,128)(2,1)S(1)}, u32[]{:S(2)}, u32[]{:S(2)}) collective-permute-start(s16[128,1152]{1,0:T(8,128)(2,1)S(1)} %pair.6), channel_id=1, source_target_pairs={{0,4},{1,5},{2,6},{3,7},{4,0},{5,1},{6,2},{7,3},{8,14},{9,15},{10,... | collective-permute-start | bytes 884744 | tf_op jit(solution)/shard_map/ppermute | solution.py:212
  152.2 4.5 %collective-permute-start.22 = (s16[128,1152]{1,0:T(8,128)(2,1)S(1)}, s16[128,1152]{1,0:T(8,128)(2,1)S(1)}, u32[]{:S(2)}, u32[]{:S(2)}) collective-permute-start(s16[128,1152]{1,0:T(8,128)(2,1)S(1)} %pair.5), channel_id=1, source_target_pairs={{0,6},{1,7},{2,0},{3,1},{4,2},{5,3},{6,4},{7,5},{8,8},{9,9},{10,10... | collective-permute-start | bytes 884744 | tf_op jit(solution)/shard_map/ppermute | solution.py:212
  157.6 5.7 %collective-permute-done.25.c = s16[128,1152]{1,0:T(8,128)(2,1)S(1)} collective-permute-done((s16[128,1152]{1,0:T(8,128)(2,1)S(1)}, s16[128,1152]{1,0:T(8,128)(2,1)S(1)}, u32[]{:S(2)}, u32[]{:S(2)}) %collective-permute-start.25) | collective-permute-done | bytes 294944 | tf_op jit(solution)/shard_map/ppermute | solution.py:212
  163.3 1.8 %collective-permute-done.22.b = s16[128,1152]{1,0:T(8,128)(2,1)S(1)} collective-permute-done((s16[128,1152]{1,0:T(8,128)(2,1)S(1)}, s16[128,1152]{1,0:T(8,128)(2,1)S(1)}, u32[]{:S(2)}, u32[]{:S(2)}) %collective-permute-start.22) | collective-permute-done | bytes 294944 | tf_op jit(solution)/shard_map/ppermute | solution.py:212
  165.1 1.1 finish.1
  (43 shorter events, 7.5 us)
Async XLA Ops:
  0.0 2.2 %copy-start = (bf16[1024,2048]{1,0:T(8,128)(2,1)S(1)}, bf16[1024,2048]{1,0:T(8,128)(2,1)}, u32[]{:S(2)}) copy-start(bf16[1024,2048]{1,0:T(8,128)(2,1)} %density.3) | copy-start | bytes 12582916
  2.2 0.7 copy-start.2
  4.4 2.0 %collective-permute-start = (bf16[512,512]{1,0:T(8,128)(2,1)S(1)}, bf16[512,512]{1,0:T(8,128)(2,1)S(1)}, u32[]{:S(2)}, u32[]{:S(2)}) collective-permute-start(bf16[512,512]{1,0:T(8,128)(2,1)S(1)} %get-tuple-element.22), channel_id=1, source_target_pairs={{0,1},{1,0},{2,3},{3,2},{4,5},{5,4},{6,7},{7,6},{8,9},{9,8},{10,11... | collective-permute-start | bytes 1572872 | tf_op jit(solution)/shard_map/ppermute | solution.py:236
  4.5 5.9 %collective-permute-start.4 = (bf16[512,512]{1,0:T(8,128)(2,1)S(1)}, bf16[512,512]{1,0:T(8,128)(2,1)S(1)}, u32[]{:S(2)}, u32[]{:S(2)}) collective-permute-start(bf16[512,512]{1,0:T(8,128)(2,1)S(1)} %get-tuple-element.24), channel_id=1, source_target_pairs={{0,1},{1,0},{2,3},{3,2},{4,5},{5,4},{6,7},{7,6},{8,9},{9,8},{10,11... | collective-permute-start | bytes 1572872 | tf_op jit(solution)/shard_map/ppermute | solution.py:236
  6.4 10.6 %collective-permute-start.1 = (bf16[512,512]{1,0:T(8,128)(2,1)S(1)}, bf16[512,512]{1,0:T(8,128)(2,1)S(1)}, u32[]{:S(2)}, u32[]{:S(2)}) collective-permute-start(bf16[512,512]{1,0:T(8,128)(2,1)S(1)} %broadcast_select_fusion.1), channel_id=1, source_target_pairs={{0,2},{1,7},{8,10},{9,15},{16,18},{17,23},{24,26},{25,31},{32,34},... | collective-permute-start | bytes 1572872 | tf_op jit(solution)/shard_map/ppermute | solution.py:239
  10.5 14.7 %collective-permute-start.5 = (bf16[512,512]{1,0:T(8,128)(2,1)S(1)}, bf16[512,512]{1,0:T(8,128)(2,1)S(1)}, u32[]{:S(2)}, u32[]{:S(2)}) collective-permute-start(bf16[512,512]{1,0:T(8,128)(2,1)S(1)} %broadcast_select_fusion), channel_id=1, source_target_pairs={{0,2},{1,7},{8,10},{9,15},{16,18},{17,23},{24,26},{25,31},{32,34},... | collective-permute-start | bytes 1572872 | tf_op jit(solution)/shard_map/ppermute | solution.py:239
  17.1 12.5 %collective-permute-start.2 = (bf16[512,512]{1,0:T(8,128)(2,1)S(1)}, bf16[512,512]{1,0:T(8,128)(2,1)S(1)}, u32[]{:S(2)}, u32[]{:S(2)}) collective-permute-start(bf16[512,512]{1,0:T(8,128)(2,1)S(1)} %broadcast_select_fusion.3), channel_id=1, source_target_pairs={{0,6},{1,3},{2,4},{7,5},{8,14},{9,11},{10,12},{15,13},{16,22},{17,... | collective-permute-start | bytes 1572872 | tf_op jit(solution)/shard_map/ppermute | solution.py:241
  25.2 10.0 %collective-permute-start.6 = (bf16[512,512]{1,0:T(8,128)(2,1)S(1)}, bf16[512,512]{1,0:T(8,128)(2,1)S(1)}, u32[]{:S(2)}, u32[]{:S(2)}) collective-permute-start(bf16[512,512]{1,0:T(8,128)(2,1)S(1)} %broadcast_select_fusion.2), channel_id=1, source_target_pairs={{0,6},{1,3},{2,4},{7,5},{8,14},{9,11},{10,12},{15,13},{16,22},{17,... | collective-permute-start | bytes 1572872 | tf_op jit(solution)/shard_map/ppermute | solution.py:241
  29.6 6.5 %copy-start.3 = (s32[8,16]{1,0:T(8,128)S(1)}, s32[8,16]{1,0:T(8,128)}, u32[]{:S(2)}) copy-start(s32[8,16]{1,0:T(8,128)} %m.3) | copy-start | bytes 1540
  29.6 10.5 %collective-permute-start.3 = (bf16[512,512]{1,0:T(8,128)(2,1)S(1)}, bf16[512,512]{1,0:T(8,128)(2,1)S(1)}, u32[]{:S(2)}, u32[]{:S(2)}) collective-permute-start(bf16[512,512]{1,0:T(8,128)(2,1)S(1)} %broadcast_select_fusion.5.refs_0_), channel_id=1, source_target_pairs={{0,1},{1,0},{2,3},{3,2},{4,5},{5,4},{6,7},{7,6},{8,9},{9,8},{10,11... | collective-permute-start | bytes 1572872 | tf_op jit(solution)/shard_map/ppermute | solution.py:232
  35.2 8.7 %collective-permute-start.7 = (bf16[512,512]{1,0:T(8,128)(2,1)S(1)}, bf16[512,512]{1,0:T(8,128)(2,1)S(1)}, u32[]{:S(2)}, u32[]{:S(2)}) collective-permute-start(bf16[512,512]{1,0:T(8,128)(2,1)S(1)} %broadcast_select_fusion.4.refs_2_), channel_id=1, source_target_pairs={{0,1},{1,0},{2,3},{3,2},{4,5},{5,4},{6,7},{7,6},{8,9},{9,8},{10,11... | collective-permute-start | bytes 1572872 | tf_op jit(solution)/shard_map/ppermute | solution.py:232
  36.2 2.2 %copy-start.1 = (bf16[1024,2048]{1,0:T(8,128)(2,1)S(1)}, bf16[1024,2048]{1,0:T(8,128)(2,1)}, u32[]{:S(2)}) copy-start(bf16[1024,2048]{1,0:T(8,128)(2,1)} %density.3) | copy-start | bytes 12582916
  42.4 16.8 %collective-permute-start.8 = (s16[256,2176]{1,0:T(8,128)(2,1)S(1)}, s16[256,2176]{1,0:T(8,128)(2,1)S(1)}, u32[]{:S(2)}, u32[]{:S(2)}) collective-permute-start(s16[256,2176]{1,0:T(8,128)(2,1)S(1)} %first_0.1), channel_id=1, source_target_pairs={{0,32},{1,9},{2,98},{3,27},{4,68},{5,21},{6,38},{7,15},{8,40},{9,1... | collective-permute-start | bytes 3342344 | tf_op jit(solution)/shard_map/ppermute | solution.py:212
  46.2 25.9 %collective-permute-start.9 = (s16[256,2176]{1,0:T(8,128)(2,1)S(1)}, s16[256,2176]{1,0:T(8,128)(2,1)S(1)}, u32[]{:S(2)}, u32[]{:S(2)}) collective-permute-start(s16[256,2176]{1,0:T(8,128)(2,1)S(1)} %first_1.1), channel_id=1, source_target_pairs={{0,64},{1,17},{2,34},{3,11},{4,100},{5,29},{6,70},{7,23},{8,72},{9... | collective-permute-start | bytes 3342344 | tf_op jit(solution)/shard_map/ppermute | solution.py:212
  51.2 23.1 %collective-permute-start.10 = (s16[256,2176]{1,0:T(8,128)(2,1)S(1)}, s16[256,2176]{1,0:T(8,128)(2,1)S(1)}, u32[]{:S(2)}, u32[]{:S(2)}) collective-permute-start(s16[256,2176]{1,0:T(8,128)(2,1)S(1)} %first_2.1), channel_id=1, source_target_pairs={{0,96},{1,25},{2,66},{3,19},{4,36},{5,13},{6,102},{7,31},{8,104},{... | collective-permute-start | bytes 3342344 | tf_op jit(solution)/shard_map/ppermute | solution.py:212
  76.0 8.4 %collective-permute-start.11 = (s16[64,2176]{1,0:T(8,128)(2,1)S(1)}, s16[64,2176]{1,0:T(8,128)(2,1)S(1)}, u32[]{:S(2)}, u32[]{:S(2)}) collective-permute-start(s16[64,2176]{1,0:T(8,128)(2,1)S(1)} %get-tuple-element.26), channel_id=1, source_target_pairs={{0,16},{1,65},{2,18},{3,67},{4,20},{5,69},{6,22},{7,71},{8,24},{9,... | collective-permute-start | bytes 835592 | tf_op jit(solution)/shard_map/ppermute | solution.py:212
  76.7 10.6 %collective-permute-start.12 = (s16[64,2176]{1,0:T(8,128)(2,1)S(1)}, s16[64,2176]{1,0:T(8,128)(2,1)S(1)}, u32[]{:S(2)}, u32[]{:S(2)}) collective-permute-start(s16[64,2176]{1,0:T(8,128)(2,1)S(1)} %get-tuple-element.27), channel_id=1, source_target_pairs={{0,8},{1,33},{2,10},{3,35},{4,12},{5,37},{6,14},{7,39},{8,16},{9,4... | collective-permute-start | bytes 835592 | tf_op jit(solution)/shard_map/ppermute | solution.py:212
  82.0 7.5 %collective-permute-start.13 = (s16[64,2176]{1,0:T(8,128)(2,1)S(1)}, s16[64,2176]{1,0:T(8,128)(2,1)S(1)}, u32[]{:S(2)}, u32[]{:S(2)}) collective-permute-start(s16[64,2176]{1,0:T(8,128)(2,1)S(1)} %get-tuple-element.28), channel_id=1, source_target_pairs={{0,24},{1,97},{2,26},{3,99},{4,28},{5,101},{6,30},{7,103},{8,0},{9... | collective-permute-start | bytes 835592 | tf_op jit(solution)/shard_map/ppermute | solution.py:212
  89.9 9.8 %collective-permute-start.16 = (s16[64,2176]{1,0:T(8,128)(2,1)S(1)}, s16[64,2176]{1,0:T(8,128)(2,1)S(1)}, u32[]{:S(2)}, u32[]{:S(2)}) collective-permute-start(s16[64,2176]{1,0:T(8,128)(2,1)S(1)} %gather.1.refs_0_), channel_id=1, source_target_pairs={{0,24},{1,97},{2,26},{3,99},{4,28},{5,101},{6,30},{7,103},{8,0},{9... | collective-permute-start | bytes 835592 | tf_op jit(solution)/shard_map/ppermute | solution.py:212
  92.6 8.2 %collective-permute-start.15 = (s16[64,2176]{1,0:T(8,128)(2,1)S(1)}, s16[64,2176]{1,0:T(8,128)(2,1)S(1)}, u32[]{:S(2)}, u32[]{:S(2)}) collective-permute-start(s16[64,2176]{1,0:T(8,128)(2,1)S(1)} %gather.1.refs_0_), channel_id=1, source_target_pairs={{0,16},{1,65},{2,18},{3,67},{4,20},{5,69},{6,22},{7,71},{8,24},{9,... | collective-permute-start | bytes 835592 | tf_op jit(solution)/shard_map/ppermute | solution.py:212
  92.6 10.7 %collective-permute-start.14 = (s16[64,2176]{1,0:T(8,128)(2,1)S(1)}, s16[64,2176]{1,0:T(8,128)(2,1)S(1)}, u32[]{:S(2)}, u32[]{:S(2)}) collective-permute-start(s16[64,2176]{1,0:T(8,128)(2,1)S(1)} %gather.1.refs_0_), channel_id=1, source_target_pairs={{0,8},{1,33},{2,10},{3,35},{4,12},{5,37},{6,14},{7,39},{8,16},{9,4... | collective-permute-start | bytes 835592 | tf_op jit(solution)/shard_map/ppermute | solution.py:212
  103.4 17.4 %collective-permute-start.26 = (s16[256,2176]{1,0:T(8,128)(2,1)S(1)}, s16[256,2176]{1,0:T(8,128)(2,1)S(1)}, u32[]{:S(2)}, u32[]{:S(2)}) collective-permute-start(s16[256,2176]{1,0:T(8,128)(2,1)S(1)} %join.1), channel_id=1, source_target_pairs={{0,96},{1,25},{2,98},{3,27},{4,100},{5,29},{6,102},{7,31},{8,72},{... | collective-permute-start | bytes 3342344 | tf_op jit(solution)/shard_map/ppermute | solution.py:212
  105.4 19.0 %collective-permute-start.23 = (s16[256,2176]{1,0:T(8,128)(2,1)S(1)}, s16[256,2176]{1,0:T(8,128)(2,1)S(1)}, u32[]{:S(2)}, u32[]{:S(2)}) collective-permute-start(s16[256,2176]{1,0:T(8,128)(2,1)S(1)} %join.1), channel_id=1, source_target_pairs={{0,64},{1,17},{2,66},{3,19},{4,68},{5,21},{6,70},{7,23},{8,40},{9,... | collective-permute-start | bytes 3342344 | tf_op jit(solution)/shard_map/ppermute | solution.py:212
  108.1 28.1 %collective-permute-start.20 = (s16[256,2176]{1,0:T(8,128)(2,1)S(1)}, s16[256,2176]{1,0:T(8,128)(2,1)S(1)}, u32[]{:S(2)}, u32[]{:S(2)}) collective-permute-start(s16[256,2176]{1,0:T(8,128)(2,1)S(1)} %join.1), channel_id=1, source_target_pairs={{0,32},{1,9},{2,34},{3,11},{4,36},{5,13},{6,38},{7,15},{8,8},{9,17... | collective-permute-start | bytes 3342344 | tf_op jit(solution)/shard_map/ppermute | solution.py:212
  111.2 27.7 %collective-permute-start.17 = (s16[256,2176]{1,0:T(8,128)(2,1)S(1)}, s16[256,2176]{1,0:T(8,128)(2,1)S(1)}, u32[]{:S(2)}, u32[]{:S(2)}) collective-permute-start(s16[256,2176]{1,0:T(8,128)(2,1)S(1)} %join.1), channel_id=1, source_target_pairs={{0,0},{1,1},{2,2},{3,3},{4,4},{5,5},{6,6},{7,7},{8,104},{9,9},{10,... | collective-permute-start | bytes 3342344 | tf_op jit(solution)/shard_map/ppermute | solution.py:212
  123.4 18.2 %collective-permute-start.27 = (f32[128,1024]{1,0:T(8,128)S(1)}, f32[128,1024]{1,0:T(8,128)S(1)}, u32[]{:S(2)}, u32[]{:S(2)}) collective-permute-start(f32[128,1024]{1,0:T(8,128)S(1)} %get-tuple-element.36), channel_id=1, source_target_pairs={{0,1},{1,0},{2,3},{3,2},{4,5},{5,4},{6,7},{7,6},{8,9},{9,8},{10,11... | collective-permute-start | bytes 1572872 | tf_op jit(solution)/shard_map/ppermute | solution.py:232
  127.0 19.7 %collective-permute-start.24 = (f32[128,1024]{1,0:T(8,128)S(1)}, f32[128,1024]{1,0:T(8,128)S(1)}, u32[]{:S(2)}, u32[]{:S(2)}) collective-permute-start(f32[128,1024]{1,0:T(8,128)S(1)} %get-tuple-element.34), channel_id=1, source_target_pairs={{0,1},{1,0},{2,3},{3,2},{4,5},{5,4},{6,7},{7,6},{8,9},{9,8},{10,11... | collective-permute-start | bytes 1572872 | tf_op jit(solution)/shard_map/ppermute | solution.py:232
  138.8 13.2 %collective-permute-start.21 = (f32[128,1024]{1,0:T(8,128)S(1)}, f32[128,1024]{1,0:T(8,128)S(1)}, u32[]{:S(2)}, u32[]{:S(2)}) collective-permute-start(f32[128,1024]{1,0:T(8,128)S(1)} %get-tuple-element.32), channel_id=1, source_target_pairs={{0,1},{1,0},{2,3},{3,2},{4,5},{5,4},{6,7},{7,6},{8,9},{9,8},{10,11... | collective-permute-start | bytes 1572872 | tf_op jit(solution)/shard_map/ppermute | solution.py:232
  141.5 15.2 %collective-permute-start.18 = (f32[128,1024]{1,0:T(8,128)S(1)}, f32[128,1024]{1,0:T(8,128)S(1)}, u32[]{:S(2)}, u32[]{:S(2)}) collective-permute-start(f32[128,1024]{1,0:T(8,128)S(1)} %get-tuple-element.30), channel_id=1, source_target_pairs={{0,1},{1,0},{2,3},{3,2},{4,5},{5,4},{6,7},{7,6},{8,9},{9,8},{10,11... | collective-permute-start | bytes 1572872 | tf_op jit(solution)/shard_map/ppermute | solution.py:232
  141.8 15.8 %collective-permute-start.28 = (s16[128,1152]{1,0:T(8,128)(2,1)S(1)}, s16[128,1152]{1,0:T(8,128)(2,1)S(1)}, u32[]{:S(2)}, u32[]{:S(2)}) collective-permute-start(s16[128,1152]{1,0:T(8,128)(2,1)S(1)} %pair.7), channel_id=1, source_target_pairs={{0,2},{1,3},{2,4},{3,5},{4,6},{5,7},{6,0},{7,1},{8,12},{9,13},{10,... | collective-permute-start | bytes 884744 | tf_op jit(solution)/shard_map/ppermute | solution.py:212
  146.9 16.4 %collective-permute-start.25 = (s16[128,1152]{1,0:T(8,128)(2,1)S(1)}, s16[128,1152]{1,0:T(8,128)(2,1)S(1)}, u32[]{:S(2)}, u32[]{:S(2)}) collective-permute-start(s16[128,1152]{1,0:T(8,128)(2,1)S(1)} %pair.6), channel_id=1, source_target_pairs={{0,4},{1,5},{2,6},{3,7},{4,0},{5,1},{6,2},{7,3},{8,14},{9,15},{10,... | collective-permute-start | bytes 884744 | tf_op jit(solution)/shard_map/ppermute | solution.py:212
  152.2 13.0 %collective-permute-start.22 = (s16[128,1152]{1,0:T(8,128)(2,1)S(1)}, s16[128,1152]{1,0:T(8,128)(2,1)S(1)}, u32[]{:S(2)}, u32[]{:S(2)}) collective-permute-start(s16[128,1152]{1,0:T(8,128)(2,1)S(1)} %pair.5), channel_id=1, source_target_pairs={{0,6},{1,7},{2,0},{3,1},{4,2},{5,3},{6,4},{7,5},{8,8},{9,9},{10,10... | collective-permute-start | bytes 884744 | tf_op jit(solution)/shard_map/ppermute | solution.py:212
  156.9 8.2 %collective-permute-start.19 = (s16[128,1152]{1,0:T(8,128)(2,1)S(1)}, s16[128,1152]{1,0:T(8,128)(2,1)S(1)}, u32[]{:S(2)}, u32[]{:S(2)}) collective-permute-start(s16[128,1152]{1,0:T(8,128)(2,1)S(1)} %pair.4), channel_id=1, source_target_pairs={{0,0},{1,1},{2,2},{3,3},{4,4},{5,5},{6,6},{7,7},{8,10},{9,11},{10,... | collective-permute-start | bytes 884744 | tf_op jit(solution)/shard_map/ppermute | solution.py:212

commit v3 on v2

--- a/solution.py
+++ b/solution.py
@@ -25,7 +25,7 @@
     return jax.ShapeDtypeStruct((rows, columns), dtype)
 
 
-def call(kernel, out, s, *args, name, flops=1 << 22, scratch=()):
+def call(kernel, out, s, *args, flops=1 << 22, scratch=()):
     in_vmem = pl.BlockSpec(memory_space=pltpu.VMEM)
     return pl.pallas_call(
         kernel,
@@ -35,7 +35,6 @@
         scratch_shapes=list(scratch),
         compiler_params=pltpu.CompilerParams(vmem_limit_bytes=16 << 20),
         cost_estimate=pl.CostEstimate(flops=flops, bytes_accessed=4 << 20, transcendentals=0),
-        name=name,
     )(*s, *args)
 
 
@@ -118,7 +117,6 @@
         [s],
         *parts,
         masked,
-        name=f"first_{i}",
         flops=2 * QUARTER * SLAB * WIDE,
         scratch=[pltpu.VMEM((SLAB, QUARTER), BF16), pltpu.VMEM((QUARTER, WIDE), F32)],
     )
@@ -180,14 +178,13 @@
                     theirs[pl.ds(pl.multiple_of(start - 128, 64), PIECE), :] += v
 
 
-def second_product(j, s, coded, masked):
+def second_product(s, coded, masked):
     return call(
         second_kernel,
         [shape(128, SLAB, F32)] * 2,
         [s],
         coded,
         masked,
-        name=f"second_{j}",
         flops=2 * QUARTER * SLAB * WIDE,
         scratch=[pltpu.VMEM((QUARTER, WIDE), BF16)],
     )
@@ -265,10 +262,9 @@
         [shape(512, 512, BF16)] * 4,
         [s, block_mask],
         density,
-        name="column",
         scratch=[pltpu.VMEM((SLAB, SLAB), BF16)],
     )
-    masked = call(mask_kernel, shape(SLAB, WIDE, BF16), [block_mask], density, name="mask")
+    masked = call(mask_kernel, shape(SLAB, WIDE, BF16), [block_mask], density)
     near = spread_column(top_a, low_a, z, core)
     far = spread_column(top_b, low_b, z, core)
 
@@ -278,19 +274,19 @@
         came.append(along(v, lambda second, z: SENT[i][(z - second) % 4] - (z - second)))
     mine = first_product(3, s, near + far, masked, False)
     wide, coded = shape(PIECE, WIDE, F32), shape(PIECE, WIDE + LANES, I16)
-    mine, *parts = call(spread_kernel, [wide, coded, coded, coded], [s], mine, *came, name="spread")
+    mine, *parts = call(spread_kernel, [wide, coded, coded, coded], [s], mine, *came)
     came = [across(parts[d - 1], d) for d in (2, 1, 3)]
-    v = call(gather_kernel, coded, [], mine, *came, name="gather")
+    v = call(gather_kernel, coded, [], mine, *came)
 
     parts = [across(v, d) for d in (1, 2, 3)]
-    v = call(join_kernel, shape(QUARTER, WIDE + LANES, I16), [], v, *parts, name="join")
+    v = call(join_kernel, shape(QUARTER, WIDE + LANES, I16), [], v, *parts)
     quarters = [along(v, lambda second, z: j - second) for j in range(4)]
     came = []
     for j, v in enumerate(quarters):
-        mine, theirs = second_product(j, s, v, masked)
-        v = call(pair_kernel, shape(128, SLAB + LANES, I16), [], mine, swap(theirs), name="pair")
+        mine, theirs = second_product(s, v, masked)
+        v = call(pair_kernel, shape(128, SLAB + LANES, I16), [], mine, swap(theirs))
         came.append(send(v, lambda x, y, z, core: (x, y, x + y + z - j, core)))
-    return call(finish_kernel, shape(128, SLAB, F32), [], *came, name="finish")
+    return call(finish_kernel, shape(128, SLAB, F32), [], *came)
 
 
 def solution(mesh):

time: 169 us -> 169 us (level)
  no operation moved by 1% of the time
where the time goes in v3:
time: 169 us; the launch traced here: 166 us
  waiting for transfers between devices  84.8 us (50%)
  starting transfers between devices  49.4 us (29%)
  Pallas kernels  26.2 us (16%)
  local copies, waits for them, and re-layouts  5.06 us (3%)
    ppermute x17, waiting for transfers between devices, send(): return lax.ppermute(v, AXES, [(place(*d), place(*to(*d))) for d in DEVICES])  63.4 us
    ppermute x17, starting transfers between devices, send(): return lax.ppermute(v, AXES, [(place(*d), place(*to(*d))) for d in DEVICES])  39.1 us
    pallas_call x18, Pallas kernels, call(): pl.pallas_call(kernel, out_shape=out, in_specs=[pl.BlockSpec(memory_space...  26.2 us
    ppermute x2, waiting for transfers between devices, spread_column(): came = lax.ppermute(half, axes, [(0, 2), (1, 7)])  11.9 us
    ppermute x2, waiting for transfers between devices, spread_column(): came = lax.ppermute(half, axes, [(0, 6), (1, 3), (2, 4), (7, 5)])  8.07 us
    ppermute x2, starting transfers between devices, spread_column(): came = lax.ppermute(half, axes, [(0, 2), (1, 7)])  5.29 us
    unnamed x8, local copies, waits for them, and re-layouts  5.06 us
  transfers between devices with their start and end apart: 29, of which 19 were waited for; matrix products, arithmetic and copies ran while one was open for 0% of the time, Pallas kernels for 13%

profile of v3, /device:TPU:0, one launch (start us, length us, event | category | flops | bytes accessed | tf_op | source)
XLA Modules:
  0.0 166.2 jit_solution(4660160857439429635)
XLA Ops:
  0.0 2.2 %copy-done = bf16[1024,2048]{1,0:T(8,128)(2,1)S(1)} copy-done((bf16[1024,2048]{1,0:T(8,128)(2,1)S(1)}, bf16[1024,2048]{1,0:T(8,128)(2,1)}, u32[]{:S(2)}) %copy-start) | copy-done | bytes 4194328
  2.9 1.5 shard_map.28
  5.0 1.4 collective-permute-done
  6.4 4.0 %collective-permute-start.1 = (bf16[512,512]{1,0:T(8,128)(2,1)S(1)}, bf16[512,512]{1,0:T(8,128)(2,1)S(1)}, u32[]{:S(2)}, u32[]{:S(2)}) collective-permute-start(bf16[512,512]{1,0:T(8,128)(2,1)S(1)} %broadcast_select_fusion.1), channel_id=1, source_target_pairs={{0,2},{1,7},{8,10},{9,15},{16,18},{17,23},{24,26},{25,31},{32,34},... | collective-permute-start | bytes 1572872 | tf_op jit(solution)/shard_map/ppermute | solution.py:236
  10.5 1.3 collective-permute-start.5
  11.8 5.2 %collective-permute-done.1 = bf16[512,512]{1,0:T(8,128)(2,1)S(1)} collective-permute-done((bf16[512,512]{1,0:T(8,128)(2,1)S(1)}, bf16[512,512]{1,0:T(8,128)(2,1)S(1)}, u32[]{:S(2)}, u32[]{:S(2)}) %collective-permute-start.1) | collective-permute-done | bytes 524320 | tf_op jit(solution)/shard_map/ppermute | solution.py:236
  17.1 1.3 collective-permute-start.2
  18.4 6.7 %collective-permute-done.5 = bf16[512,512]{1,0:T(8,128)(2,1)S(1)} collective-permute-done((bf16[512,512]{1,0:T(8,128)(2,1)S(1)}, bf16[512,512]{1,0:T(8,128)(2,1)S(1)}, u32[]{:S(2)}, u32[]{:S(2)}) %collective-permute-start.5) | collective-permute-done | bytes 524320 | tf_op jit(solution)/shard_map/ppermute | solution.py:236
  25.2 1.3 collective-permute-start.6
  26.6 3.0 %collective-permute-done.2 = bf16[512,512]{1,0:T(8,128)(2,1)S(1)} collective-permute-done((bf16[512,512]{1,0:T(8,128)(2,1)S(1)}, bf16[512,512]{1,0:T(8,128)(2,1)S(1)}, u32[]{:S(2)}, u32[]{:S(2)}) %collective-permute-start.2) | collective-permute-done | bytes 524320 | tf_op jit(solution)/shard_map/ppermute | solution.py:238
  30.1 5.1 %collective-permute-done.6 = bf16[512,512]{1,0:T(8,128)(2,1)S(1)} collective-permute-done((bf16[512,512]{1,0:T(8,128)(2,1)S(1)}, bf16[512,512]{1,0:T(8,128)(2,1)S(1)}, u32[]{:S(2)}, u32[]{:S(2)}) %collective-permute-start.6) | collective-permute-done | bytes 524320 | tf_op jit(solution)/shard_map/ppermute | solution.py:238
  36.2 2.2 %copy-done.1 = bf16[1024,2048]{1,0:T(8,128)(2,1)S(1)} copy-done((bf16[1024,2048]{1,0:T(8,128)(2,1)S(1)}, bf16[1024,2048]{1,0:T(8,128)(2,1)}, u32[]{:S(2)}) %copy-start.1) | copy-done | bytes 4194328
  38.3 1.8 %shard_map.29.refs_4_.refs_2_.masked = bf16[1024,2048]{1,0:T(8,128)(2,1)S(1)} custom-call(s32[8,16]{1,0:T(8,128)S(1)} %copy-done.3, bf16[1024,2048]{1,0:T(8,128)(2,1)S(1)} %copy-done.1), custom_call_target="tpu_custom_call" | custom-call | flops 4194304 | bytes 4194304 | tf_op jit(solution)/shard_map/pallas_call | solution.py:30
  40.2 2.2 %shard_map.31 = s16[256,2176]{1,0:T(8,128)(2,1)S(1)} custom-call(s32[16]{0:T(128)S(1)} %compare_select_fusion.8.s, bf16[512,512]{1,0:T(8,128)(2,1)S(1)} %broadcast_select_fusion.5.refs_0_, bf16[512,512]{1,0:T(8,128)(2,1)S(1)} %collective-permute-done.3.refs_1_, bf16[1024,2048]{1,0:T(8,128)(2,1)S(1)} %shard_map.29.refs_4_.refs_2_.masked), custom_call_target="tpu_custom_call" | custom-call | flops 1073741824 | bytes 4194304 | tf_op jit(solution)/shard_map/pallas_call | solution.py:30
  42.4 1.6 collective-permute-start.8
  43.9 2.2 %shard_map.32 = s16[256,2176]{1,0:T(8,128)(2,1)S(1)} custom-call(s32[16]{0:T(128)S(1)} %compare_select_fusion.8.s, bf16[512,512]{1,0:T(8,128)(2,1)S(1)} %broadcast_select_fusion.5.refs_0_, bf16[512,512]{1,0:T(8,128)(2,1)S(1)} %collective-permute-done.3.refs_1_, bf16[512,512]{1,0:T(8,128)(2,1)S(1)} %broadcast_select_fusion.4.refs_2_, ...), custom_call_target="tpu_custom_call" | custom-call | flops 1073741824 | bytes 4194304 | tf_op jit(solution)/shard_map/pallas_call | solution.py:30
  46.2 2.8 %collective-permute-start.9 = (s16[256,2176]{1,0:T(8,128)(2,1)S(1)}, s16[256,2176]{1,0:T(8,128)(2,1)S(1)}, u32[]{:S(2)}, u32[]{:S(2)}) collective-permute-start(s16[256,2176]{1,0:T(8,128)(2,1)S(1)} %shard_map.32), channel_id=1, source_target_pairs={{0,64},{1,17},{2,34},{3,11},{4,100},{5,29},{6,70},{7,23},{8,72},{9... | collective-permute-start | bytes 3342344 | tf_op jit(solution)/shard_map/ppermute | solution.py:209
  49.0 2.2 %shard_map.33 = s16[256,2176]{1,0:T(8,128)(2,1)S(1)} custom-call(s32[16]{0:T(128)S(1)} %compare_select_fusion.8.s, bf16[512,512]{1,0:T(8,128)(2,1)S(1)} %broadcast_select_fusion.5.refs_0_, bf16[512,512]{1,0:T(8,128)(2,1)S(1)} %collective-permute-done.3.refs_1_, bf16[512,512]{1,0:T(8,128)(2,1)S(1)} %broadcast_select_fusion.4.refs_2_, ...), custom_call_target="tpu_custom_call" | custom-call | flops 1073741824 | bytes 4194304 | tf_op jit(solution)/shard_map/pallas_call | solution.py:30
  51.2 1.5 collective-permute-start.10
  52.7 1.9 %shard_map.30.own = f32[256,2048]{1,0:T(8,128)S(1)} custom-call(s32[16]{0:T(128)S(1)} %compare_select_fusion.8.s, bf16[512,512]{1,0:T(8,128)(2,1)S(1)} %broadcast_select_fusion.5.refs_0_, bf16[512,512]{1,0:T(8,128)(2,1)S(1)} %collective-permute-done.3.refs_1_, bf16[512,512]{1,0:T(8,128)(2,1)S(1)} %broadcast_select_fusion.4.refs_2_, ...), custom_call_target="tpu_custom_call" | custom-call | flops 1073741824 | bytes 4194304 | tf_op jit(solution)/shard_map/pallas_call | solution.py:30
  54.6 4.5 %collective-permute-done.8.a = s16[256,2176]{1,0:T(8,128)(2,1)S(1)} collective-permute-done((s16[256,2176]{1,0:T(8,128)(2,1)S(1)}, s16[256,2176]{1,0:T(8,128)(2,1)S(1)}, u32[]{:S(2)}, u32[]{:S(2)}) %collective-permute-start.8) | collective-permute-done | bytes 1114144 | tf_op jit(solution)/shard_map/ppermute | solution.py:209
  59.2 12.9 %collective-permute-done.9.b = s16[256,2176]{1,0:T(8,128)(2,1)S(1)} collective-permute-done((s16[256,2176]{1,0:T(8,128)(2,1)S(1)}, s16[256,2176]{1,0:T(8,128)(2,1)S(1)}, u32[]{:S(2)}, u32[]{:S(2)}) %collective-permute-start.9) | collective-permute-done | bytes 1114144 | tf_op jit(solution)/shard_map/ppermute | solution.py:209
  72.1 2.2 %collective-permute-done.10.c = s16[256,2176]{1,0:T(8,128)(2,1)S(1)} collective-permute-done((s16[256,2176]{1,0:T(8,128)(2,1)S(1)}, s16[256,2176]{1,0:T(8,128)(2,1)S(1)}, u32[]{:S(2)}, u32[]{:S(2)}) %collective-permute-start.10) | collective-permute-done | bytes 1114144 | tf_op jit(solution)/shard_map/ppermute | solution.py:209
  74.3 1.7 %shard_map.34 = (f32[64,2048]{1,0:T(8,128)S(1)}, s16[64,2176]{1,0:T(8,128)(2,1)S(1)}, s16[64,2176]{1,0:T(8,128)(2,1)S(1)}, s16[64,2176]{1,0:T(8,128)(2,1)S(1)}) custom-call(s32[16]{0:T(128)S(1)} %compare_select_fusion.8.s, f32[256,2048]{1,0:T(8,128)S(1)} %shard_map.30.own, s16[256,2176]{1,0:T(8,128)(2,1)S(1)} %collective-permute-done.8.a, ...), custom_call_target="tpu_custom_call" | custom-call | flops 4194304 | bytes 4194304 | tf_op jit(solution)/shard_map/pallas_call | solution.py:30
  76.7 5.3 %collective-permute-start.12 = (s16[64,2176]{1,0:T(8,128)(2,1)S(1)}, s16[64,2176]{1,0:T(8,128)(2,1)S(1)}, u32[]{:S(2)}, u32[]{:S(2)}) collective-permute-start(s16[64,2176]{1,0:T(8,128)(2,1)S(1)} %get-tuple-element.27), channel_id=1, source_target_pairs={{0,8},{1,33},{2,10},{3,35},{4,12},{5,37},{6,14},{7,39},{8,16},{9,4... | collective-permute-start | bytes 835592 | tf_op jit(solution)/shard_map/ppermute | solution.py:209
  82.0 2.4 %collective-permute-done.11.a = s16[64,2176]{1,0:T(8,128)(2,1)S(1)} collective-permute-done((s16[64,2176]{1,0:T(8,128)(2,1)S(1)}, s16[64,2176]{1,0:T(8,128)(2,1)S(1)}, u32[]{:S(2)}, u32[]{:S(2)}) %collective-permute-start.11) | collective-permute-done | bytes 278560 | tf_op jit(solution)/shard_map/ppermute | solution.py:209
  84.4 2.9 %collective-permute-done.12.b = s16[64,2176]{1,0:T(8,128)(2,1)S(1)} collective-permute-done((s16[64,2176]{1,0:T(8,128)(2,1)S(1)}, s16[64,2176]{1,0:T(8,128)(2,1)S(1)}, u32[]{:S(2)}, u32[]{:S(2)}) %collective-permute-start.12) | collective-permute-done | bytes 278560 | tf_op jit(solution)/shard_map/ppermute | solution.py:209
  87.3 2.2 %collective-permute-done.13.c = s16[64,2176]{1,0:T(8,128)(2,1)S(1)} collective-permute-done((s16[64,2176]{1,0:T(8,128)(2,1)S(1)}, s16[64,2176]{1,0:T(8,128)(2,1)S(1)}, u32[]{:S(2)}, u32[]{:S(2)}) %collective-permute-start.13) | collective-permute-done | bytes 278560 | tf_op jit(solution)/shard_map/ppermute | solution.py:209
  89.9 2.7 %collective-permute-start.16 = (s16[64,2176]{1,0:T(8,128)(2,1)S(1)}, s16[64,2176]{1,0:T(8,128)(2,1)S(1)}, u32[]{:S(2)}, u32[]{:S(2)}) collective-permute-start(s16[64,2176]{1,0:T(8,128)(2,1)S(1)} %shard_map.35.refs_0_), channel_id=1, source_target_pairs={{0,24},{1,97},{2,26},{3,99},{4,28},{5,101},{6,30},{7,103},{8,0},{9... | collective-permute-start | bytes 835592 | tf_op jit(solution)/shard_map/ppermute | solution.py:209
  92.6 0.9 collective-permute-start.14
  93.5 6.1 %collective-permute-done.16.refs_3_ = s16[64,2176]{1,0:T(8,128)(2,1)S(1)} collective-permute-done((s16[64,2176]{1,0:T(8,128)(2,1)S(1)}, s16[64,2176]{1,0:T(8,128)(2,1)S(1)}, u32[]{:S(2)}, u32[]{:S(2)}) %collective-permute-start.16) | collective-permute-done | bytes 278560 | tf_op jit(solution)/shard_map/ppermute | solution.py:209
  99.7 1.1 collective-permute-done.15.refs_2_
  100.7 2.6 %collective-permute-done.14.refs_1_ = s16[64,2176]{1,0:T(8,128)(2,1)S(1)} collective-permute-done((s16[64,2176]{1,0:T(8,128)(2,1)S(1)}, s16[64,2176]{1,0:T(8,128)(2,1)S(1)}, u32[]{:S(2)}, u32[]{:S(2)}) %collective-permute-start.14) | collective-permute-done | bytes 278560 | tf_op jit(solution)/shard_map/ppermute | solution.py:209
  103.4 1.9 %collective-permute-start.26 = (s16[256,2176]{1,0:T(8,128)(2,1)S(1)}, s16[256,2176]{1,0:T(8,128)(2,1)S(1)}, u32[]{:S(2)}, u32[]{:S(2)}) collective-permute-start(s16[256,2176]{1,0:T(8,128)(2,1)S(1)} %shard_map.36), channel_id=1, source_target_pairs={{0,96},{1,25},{2,98},{3,27},{4,100},{5,29},{6,102},{7,31},{8,72},{... | collective-permute-start | bytes 3342344 | tf_op jit(solution)/shard_map/ppermute | solution.py:209
  105.4 2.7 %collective-permute-start.23 = (s16[256,2176]{1,0:T(8,128)(2,1)S(1)}, s16[256,2176]{1,0:T(8,128)(2,1)S(1)}, u32[]{:S(2)}, u32[]{:S(2)}) collective-permute-start(s16[256,2176]{1,0:T(8,128)(2,1)S(1)} %shard_map.36), channel_id=1, source_target_pairs={{0,64},{1,17},{2,66},{3,19},{4,68},{5,21},{6,70},{7,23},{8,40},{9,... | collective-permute-start | bytes 3342344 | tf_op jit(solution)/shard_map/ppermute | solution.py:209
  108.1 3.1 %collective-permute-start.20 = (s16[256,2176]{1,0:T(8,128)(2,1)S(1)}, s16[256,2176]{1,0:T(8,128)(2,1)S(1)}, u32[]{:S(2)}, u32[]{:S(2)}) collective-permute-start(s16[256,2176]{1,0:T(8,128)(2,1)S(1)} %shard_map.36), channel_id=1, source_target_pairs={{0,32},{1,9},{2,34},{3,11},{4,36},{5,13},{6,38},{7,15},{8,8},{9,17... | collective-permute-start | bytes 3342344 | tf_op jit(solution)/shard_map/ppermute | solution.py:209
  112.0 8.9 %collective-permute-done.26.coded = s16[256,2176]{1,0:T(8,128)(2,1)S(1)} collective-permute-done((s16[256,2176]{1,0:T(8,128)(2,1)S(1)}, s16[256,2176]{1,0:T(8,128)(2,1)S(1)}, u32[]{:S(2)}, u32[]{:S(2)}) %collective-permute-start.26) | collective-permute-done | bytes 1114144 | tf_op jit(solution)/shard_map/ppermute | solution.py:209
  120.8 2.6 %shard_map.43 = (f32[128,1024]{1,0:T(8,128)S(1)}, f32[128,1024]{1,0:T(8,128)S(1)}) custom-call(s32[16]{0:T(128)S(1)} %compare_select_fusion.8.s, s16[256,2176]{1,0:T(8,128)(2,1)S(1)} %collective-permute-done.26.coded, bf16[1024,2048]{1,0:T(8,128)(2,1)S(1)} %shard_map.29.refs_4_.refs_2_.masked), custom_call_target="tpu_custom_call" | custom-call | flops 1073741824 | bytes 4194304 | tf_op jit(solution)/shard_map/pallas_call | solution.py:30
  124.3 2.6 %shard_map.41 = (f32[128,1024]{1,0:T(8,128)S(1)}, f32[128,1024]{1,0:T(8,128)S(1)}) custom-call(s32[16]{0:T(128)S(1)} %compare_select_fusion.8.s, s16[256,2176]{1,0:T(8,128)(2,1)S(1)} %collective-permute-done.23.coded, bf16[1024,2048]{1,0:T(8,128)(2,1)S(1)} %shard_map.29.refs_4_.refs_2_.masked), custom_call_target="tpu_custom_call" | custom-call | flops 1073741824 | bytes 4194304 | tf_op jit(solution)/shard_map/pallas_call | solution.py:30
  127.1 9.1 %collective-permute-done.20.coded = s16[256,2176]{1,0:T(8,128)(2,1)S(1)} collective-permute-done((s16[256,2176]{1,0:T(8,128)(2,1)S(1)}, s16[256,2176]{1,0:T(8,128)(2,1)S(1)}, u32[]{:S(2)}, u32[]{:S(2)}) %collective-permute-start.20) | collective-permute-done | bytes 1114144 | tf_op jit(solution)/shard_map/ppermute | solution.py:209
  136.2 2.6 %shard_map.39 = (f32[128,1024]{1,0:T(8,128)S(1)}, f32[128,1024]{1,0:T(8,128)S(1)}) custom-call(s32[16]{0:T(128)S(1)} %compare_select_fusion.8.s, s16[256,2176]{1,0:T(8,128)(2,1)S(1)} %collective-permute-done.20.coded, bf16[1024,2048]{1,0:T(8,128)(2,1)S(1)} %shard_map.29.refs_4_.refs_2_.masked), custom_call_target="tpu_custom_call" | custom-call | flops 1073741824 | bytes 4194304 | tf_op jit(solution)/shard_map/pallas_call | solution.py:30
  138.9 2.6 %shard_map.37 = (f32[128,1024]{1,0:T(8,128)S(1)}, f32[128,1024]{1,0:T(8,128)S(1)}) custom-call(s32[16]{0:T(128)S(1)} %compare_select_fusion.8.s, s16[256,2176]{1,0:T(8,128)(2,1)S(1)} %collective-permute-done.17.coded, bf16[1024,2048]{1,0:T(8,128)(2,1)S(1)} %shard_map.29.refs_4_.refs_2_.masked), custom_call_target="tpu_custom_call" | custom-call | flops 1073741824 | bytes 4194304 | tf_op jit(solution)/shard_map/pallas_call | solution.py:30
  141.8 4.8 %collective-permute-start.28 = (s16[128,1152]{1,0:T(8,128)(2,1)S(1)}, s16[128,1152]{1,0:T(8,128)(2,1)S(1)}, u32[]{:S(2)}, u32[]{:S(2)}) collective-permute-start(s16[128,1152]{1,0:T(8,128)(2,1)S(1)} %shard_map.44), channel_id=1, source_target_pairs={{0,2},{1,3},{2,4},{3,5},{4,6},{5,7},{6,0},{7,1},{8,12},{9,13},{10,... | collective-permute-start | bytes 884744 | tf_op jit(solution)/shard_map/ppermute | solution.py:209
  146.9 5.1 %collective-permute-start.25 = (s16[128,1152]{1,0:T(8,128)(2,1)S(1)}, s16[128,1152]{1,0:T(8,128)(2,1)S(1)}, u32[]{:S(2)}, u32[]{:S(2)}) collective-permute-start(s16[128,1152]{1,0:T(8,128)(2,1)S(1)} %shard_map.42), channel_id=1, source_target_pairs={{0,4},{1,5},{2,6},{3,7},{4,0},{5,1},{6,2},{7,3},{8,14},{9,15},{10,... | collective-permute-start | bytes 884744 | tf_op jit(solution)/shard_map/ppermute | solution.py:209
  152.2 4.5 %collective-permute-start.22 = (s16[128,1152]{1,0:T(8,128)(2,1)S(1)}, s16[128,1152]{1,0:T(8,128)(2,1)S(1)}, u32[]{:S(2)}, u32[]{:S(2)}) collective-permute-start(s16[128,1152]{1,0:T(8,128)(2,1)S(1)} %shard_map.40), channel_id=1, source_target_pairs={{0,6},{1,7},{2,0},{3,1},{4,2},{5,3},{6,4},{7,5},{8,8},{9,9},{10,10... | collective-permute-start | bytes 884744 | tf_op jit(solution)/shard_map/ppermute | solution.py:209
  157.6 5.7 %collective-permute-done.25.c = s16[128,1152]{1,0:T(8,128)(2,1)S(1)} collective-permute-done((s16[128,1152]{1,0:T(8,128)(2,1)S(1)}, s16[128,1152]{1,0:T(8,128)(2,1)S(1)}, u32[]{:S(2)}, u32[]{:S(2)}) %collective-permute-start.25) | collective-permute-done | bytes 294944 | tf_op jit(solution)/shard_map/ppermute | solution.py:209
  163.3 1.8 %collective-permute-done.22.b = s16[128,1152]{1,0:T(8,128)(2,1)S(1)} collective-permute-done((s16[128,1152]{1,0:T(8,128)(2,1)S(1)}, s16[128,1152]{1,0:T(8,128)(2,1)S(1)}, u32[]{:S(2)}, u32[]{:S(2)}) %collective-permute-start.22) | collective-permute-done | bytes 294944 | tf_op jit(solution)/shard_map/ppermute | solution.py:209
  165.1 1.1 shard_map.45
  (43 shorter events, 7.5 us)
Async XLA Ops:
  0.0 2.2 %copy-start = (bf16[1024,2048]{1,0:T(8,128)(2,1)S(1)}, bf16[1024,2048]{1,0:T(8,128)(2,1)}, u32[]{:S(2)}) copy-start(bf16[1024,2048]{1,0:T(8,128)(2,1)} %density.3) | copy-start | bytes 12582916
  2.2 0.7 copy-start.2
  4.4 2.0 %collective-permute-start = (bf16[512,512]{1,0:T(8,128)(2,1)S(1)}, bf16[512,512]{1,0:T(8,128)(2,1)S(1)}, u32[]{:S(2)}, u32[]{:S(2)}) collective-permute-start(bf16[512,512]{1,0:T(8,128)(2,1)S(1)} %get-tuple-element.22), channel_id=1, source_target_pairs={{0,1},{1,0},{2,3},{3,2},{4,5},{5,4},{6,7},{7,6},{8,9},{9,8},{10,11... | collective-permute-start | bytes 1572872 | tf_op jit(solution)/shard_map/ppermute | solution.py:233
  4.5 5.9 %collective-permute-start.4 = (bf16[512,512]{1,0:T(8,128)(2,1)S(1)}, bf16[512,512]{1,0:T(8,128)(2,1)S(1)}, u32[]{:S(2)}, u32[]{:S(2)}) collective-permute-start(bf16[512,512]{1,0:T(8,128)(2,1)S(1)} %get-tuple-element.24), channel_id=1, source_target_pairs={{0,1},{1,0},{2,3},{3,2},{4,5},{5,4},{6,7},{7,6},{8,9},{9,8},{10,11... | collective-permute-start | bytes 1572872 | tf_op jit(solution)/shard_map/ppermute | solution.py:233
  6.4 10.6 %collective-permute-start.1 = (bf16[512,512]{1,0:T(8,128)(2,1)S(1)}, bf16[512,512]{1,0:T(8,128)(2,1)S(1)}, u32[]{:S(2)}, u32[]{:S(2)}) collective-permute-start(bf16[512,512]{1,0:T(8,128)(2,1)S(1)} %broadcast_select_fusion.1), channel_id=1, source_target_pairs={{0,2},{1,7},{8,10},{9,15},{16,18},{17,23},{24,26},{25,31},{32,34},... | collective-permute-start | bytes 1572872 | tf_op jit(solution)/shard_map/ppermute | solution.py:236
  10.5 14.7 %collective-permute-start.5 = (bf16[512,512]{1,0:T(8,128)(2,1)S(1)}, bf16[512,512]{1,0:T(8,128)(2,1)S(1)}, u32[]{:S(2)}, u32[]{:S(2)}) collective-permute-start(bf16[512,512]{1,0:T(8,128)(2,1)S(1)} %broadcast_select_fusion), channel_id=1, source_target_pairs={{0,2},{1,7},{8,10},{9,15},{16,18},{17,23},{24,26},{25,31},{32,34},... | collective-permute-start | bytes 1572872 | tf_op jit(solution)/shard_map/ppermute | solution.py:236
  17.1 12.5 %collective-permute-start.2 = (bf16[512,512]{1,0:T(8,128)(2,1)S(1)}, bf16[512,512]{1,0:T(8,128)(2,1)S(1)}, u32[]{:S(2)}, u32[]{:S(2)}) collective-permute-start(bf16[512,512]{1,0:T(8,128)(2,1)S(1)} %broadcast_select_fusion.3), channel_id=1, source_target_pairs={{0,6},{1,3},{2,4},{7,5},{8,14},{9,11},{10,12},{15,13},{16,22},{17,... | collective-permute-start | bytes 1572872 | tf_op jit(solution)/shard_map/ppermute | solution.py:238
  25.2 10.0 %collective-permute-start.6 = (bf16[512,512]{1,0:T(8,128)(2,1)S(1)}, bf16[512,512]{1,0:T(8,128)(2,1)S(1)}, u32[]{:S(2)}, u32[]{:S(2)}) collective-permute-start(bf16[512,512]{1,0:T(8,128)(2,1)S(1)} %broadcast_select_fusion.2), channel_id=1, source_target_pairs={{0,6},{1,3},{2,4},{7,5},{8,14},{9,11},{10,12},{15,13},{16,22},{17,... | collective-permute-start | bytes 1572872 | tf_op jit(solution)/shard_map/ppermute | solution.py:238
  29.6 6.5 %copy-start.3 = (s32[8,16]{1,0:T(8,128)S(1)}, s32[8,16]{1,0:T(8,128)}, u32[]{:S(2)}) copy-start(s32[8,16]{1,0:T(8,128)} %m.3) | copy-start | bytes 1540
  29.6 10.5 %collective-permute-start.3 = (bf16[512,512]{1,0:T(8,128)(2,1)S(1)}, bf16[512,512]{1,0:T(8,128)(2,1)S(1)}, u32[]{:S(2)}, u32[]{:S(2)}) collective-permute-start(bf16[512,512]{1,0:T(8,128)(2,1)S(1)} %broadcast_select_fusion.5.refs_0_), channel_id=1, source_target_pairs={{0,1},{1,0},{2,3},{3,2},{4,5},{5,4},{6,7},{7,6},{8,9},{9,8},{10,11... | collective-permute-start | bytes 1572872 | tf_op jit(solution)/shard_map/ppermute | solution.py:229
  35.2 8.7 %collective-permute-start.7 = (bf16[512,512]{1,0:T(8,128)(2,1)S(1)}, bf16[512,512]{1,0:T(8,128)(2,1)S(1)}, u32[]{:S(2)}, u32[]{:S(2)}) collective-permute-start(bf16[512,512]{1,0:T(8,128)(2,1)S(1)} %broadcast_select_fusion.4.refs_2_), channel_id=1, source_target_pairs={{0,1},{1,0},{2,3},{3,2},{4,5},{5,4},{6,7},{7,6},{8,9},{9,8},{10,11... | collective-permute-start | bytes 1572872 | tf_op jit(solution)/shard_map/ppermute | solution.py:229
  36.2 2.2 %copy-start.1 = (bf16[1024,2048]{1,0:T(8,128)(2,1)S(1)}, bf16[1024,2048]{1,0:T(8,128)(2,1)}, u32[]{:S(2)}) copy-start(bf16[1024,2048]{1,0:T(8,128)(2,1)} %density.3) | copy-start | bytes 12582916
  42.4 16.8 %collective-permute-start.8 = (s16[256,2176]{1,0:T(8,128)(2,1)S(1)}, s16[256,2176]{1,0:T(8,128)(2,1)S(1)}, u32[]{:S(2)}, u32[]{:S(2)}) collective-permute-start(s16[256,2176]{1,0:T(8,128)(2,1)S(1)} %shard_map.31), channel_id=1, source_target_pairs={{0,32},{1,9},{2,98},{3,27},{4,68},{5,21},{6,38},{7,15},{8,40},{9,1... | collective-permute-start | bytes 3342344 | tf_op jit(solution)/shard_map/ppermute | solution.py:209
  46.2 25.9 %collective-permute-start.9 = (s16[256,2176]{1,0:T(8,128)(2,1)S(1)}, s16[256,2176]{1,0:T(8,128)(2,1)S(1)}, u32[]{:S(2)}, u32[]{:S(2)}) collective-permute-start(s16[256,2176]{1,0:T(8,128)(2,1)S(1)} %shard_map.32), channel_id=1, source_target_pairs={{0,64},{1,17},{2,34},{3,11},{4,100},{5,29},{6,70},{7,23},{8,72},{9... | collective-permute-start | bytes 3342344 | tf_op jit(solution)/shard_map/ppermute | solution.py:209
  51.2 23.1 %collective-permute-start.10 = (s16[256,2176]{1,0:T(8,128)(2,1)S(1)}, s16[256,2176]{1,0:T(8,128)(2,1)S(1)}, u32[]{:S(2)}, u32[]{:S(2)}) collective-permute-start(s16[256,2176]{1,0:T(8,128)(2,1)S(1)} %shard_map.33), channel_id=1, source_target_pairs={{0,96},{1,25},{2,66},{3,19},{4,36},{5,13},{6,102},{7,31},{8,104},{... | collective-permute-start | bytes 3342344 | tf_op jit(solution)/shard_map/ppermute | solution.py:209
  76.0 8.4 %collective-permute-start.11 = (s16[64,2176]{1,0:T(8,128)(2,1)S(1)}, s16[64,2176]{1,0:T(8,128)(2,1)S(1)}, u32[]{:S(2)}, u32[]{:S(2)}) collective-permute-start(s16[64,2176]{1,0:T(8,128)(2,1)S(1)} %get-tuple-element.26), channel_id=1, source_target_pairs={{0,16},{1,65},{2,18},{3,67},{4,20},{5,69},{6,22},{7,71},{8,24},{9,... | collective-permute-start | bytes 835592 | tf_op jit(solution)/shard_map/ppermute | solution.py:209
  76.7 10.6 %collective-permute-start.12 = (s16[64,2176]{1,0:T(8,128)(2,1)S(1)}, s16[64,2176]{1,0:T(8,128)(2,1)S(1)}, u32[]{:S(2)}, u32[]{:S(2)}) collective-permute-start(s16[64,2176]{1,0:T(8,128)(2,1)S(1)} %get-tuple-element.27), channel_id=1, source_target_pairs={{0,8},{1,33},{2,10},{3,35},{4,12},{5,37},{6,14},{7,39},{8,16},{9,4... | collective-permute-start | bytes 835592 | tf_op jit(solution)/shard_map/ppermute | solution.py:209
  82.0 7.5 %collective-permute-start.13 = (s16[64,2176]{1,0:T(8,128)(2,1)S(1)}, s16[64,2176]{1,0:T(8,128)(2,1)S(1)}, u32[]{:S(2)}, u32[]{:S(2)}) collective-permute-start(s16[64,2176]{1,0:T(8,128)(2,1)S(1)} %get-tuple-element.28), channel_id=1, source_target_pairs={{0,24},{1,97},{2,26},{3,99},{4,28},{5,101},{6,30},{7,103},{8,0},{9... | collective-permute-start | bytes 835592 | tf_op jit(solution)/shard_map/ppermute | solution.py:209
  89.9 9.8 %collective-permute-start.16 = (s16[64,2176]{1,0:T(8,128)(2,1)S(1)}, s16[64,2176]{1,0:T(8,128)(2,1)S(1)}, u32[]{:S(2)}, u32[]{:S(2)}) collective-permute-start(s16[64,2176]{1,0:T(8,128)(2,1)S(1)} %shard_map.35.refs_0_), channel_id=1, source_target_pairs={{0,24},{1,97},{2,26},{3,99},{4,28},{5,101},{6,30},{7,103},{8,0},{9... | collective-permute-start | bytes 835592 | tf_op jit(solution)/shard_map/ppermute | solution.py:209
  92.6 8.2 %collective-permute-start.15 = (s16[64,2176]{1,0:T(8,128)(2,1)S(1)}, s16[64,2176]{1,0:T(8,128)(2,1)S(1)}, u32[]{:S(2)}, u32[]{:S(2)}) collective-permute-start(s16[64,2176]{1,0:T(8,128)(2,1)S(1)} %shard_map.35.refs_0_), channel_id=1, source_target_pairs={{0,16},{1,65},{2,18},{3,67},{4,20},{5,69},{6,22},{7,71},{8,24},{9,... | collective-permute-start | bytes 835592 | tf_op jit(solution)/shard_map/ppermute | solution.py:209
  92.6 10.7 %collective-permute-start.14 = (s16[64,2176]{1,0:T(8,128)(2,1)S(1)}, s16[64,2176]{1,0:T(8,128)(2,1)S(1)}, u32[]{:S(2)}, u32[]{:S(2)}) collective-permute-start(s16[64,2176]{1,0:T(8,128)(2,1)S(1)} %shard_map.35.refs_0_), channel_id=1, source_target_pairs={{0,8},{1,33},{2,10},{3,35},{4,12},{5,37},{6,14},{7,39},{8,16},{9,4... | collective-permute-start | bytes 835592 | tf_op jit(solution)/shard_map/ppermute | solution.py:209
  103.4 17.4 %collective-permute-start.26 = (s16[256,2176]{1,0:T(8,128)(2,1)S(1)}, s16[256,2176]{1,0:T(8,128)(2,1)S(1)}, u32[]{:S(2)}, u32[]{:S(2)}) collective-permute-start(s16[256,2176]{1,0:T(8,128)(2,1)S(1)} %shard_map.36), channel_id=1, source_target_pairs={{0,96},{1,25},{2,98},{3,27},{4,100},{5,29},{6,102},{7,31},{8,72},{... | collective-permute-start | bytes 3342344 | tf_op jit(solution)/shard_map/ppermute | solution.py:209
  105.4 19.0 %collective-permute-start.23 = (s16[256,2176]{1,0:T(8,128)(2,1)S(1)}, s16[256,2176]{1,0:T(8,128)(2,1)S(1)}, u32[]{:S(2)}, u32[]{:S(2)}) collective-permute-start(s16[256,2176]{1,0:T(8,128)(2,1)S(1)} %shard_map.36), channel_id=1, source_target_pairs={{0,64},{1,17},{2,66},{3,19},{4,68},{5,21},{6,70},{7,23},{8,40},{9,... | collective-permute-start | bytes 3342344 | tf_op jit(solution)/shard_map/ppermute | solution.py:209
  108.1 28.1 %collective-permute-start.20 = (s16[256,2176]{1,0:T(8,128)(2,1)S(1)}, s16[256,2176]{1,0:T(8,128)(2,1)S(1)}, u32[]{:S(2)}, u32[]{:S(2)}) collective-permute-start(s16[256,2176]{1,0:T(8,128)(2,1)S(1)} %shard_map.36), channel_id=1, source_target_pairs={{0,32},{1,9},{2,34},{3,11},{4,36},{5,13},{6,38},{7,15},{8,8},{9,17... | collective-permute-start | bytes 3342344 | tf_op jit(solution)/shard_map/ppermute | solution.py:209
  111.2 27.7 %collective-permute-start.17 = (s16[256,2176]{1,0:T(8,128)(2,1)S(1)}, s16[256,2176]{1,0:T(8,128)(2,1)S(1)}, u32[]{:S(2)}, u32[]{:S(2)}) collective-permute-start(s16[256,2176]{1,0:T(8,128)(2,1)S(1)} %shard_map.36), channel_id=1, source_target_pairs={{0,0},{1,1},{2,2},{3,3},{4,4},{5,5},{6,6},{7,7},{8,104},{9,9},{10,... | collective-permute-start | bytes 3342344 | tf_op jit(solution)/shard_map/ppermute | solution.py:209
  123.4 18.2 %collective-permute-start.27 = (f32[128,1024]{1,0:T(8,128)S(1)}, f32[128,1024]{1,0:T(8,128)S(1)}, u32[]{:S(2)}, u32[]{:S(2)}) collective-permute-start(f32[128,1024]{1,0:T(8,128)S(1)} %get-tuple-element.36), channel_id=1, source_target_pairs={{0,1},{1,0},{2,3},{3,2},{4,5},{5,4},{6,7},{7,6},{8,9},{9,8},{10,11... | collective-permute-start | bytes 1572872 | tf_op jit(solution)/shard_map/ppermute | solution.py:229
  127.0 19.7 %collective-permute-start.24 = (f32[128,1024]{1,0:T(8,128)S(1)}, f32[128,1024]{1,0:T(8,128)S(1)}, u32[]{:S(2)}, u32[]{:S(2)}) collective-permute-start(f32[128,1024]{1,0:T(8,128)S(1)} %get-tuple-element.34), channel_id=1, source_target_pairs={{0,1},{1,0},{2,3},{3,2},{4,5},{5,4},{6,7},{7,6},{8,9},{9,8},{10,11... | collective-permute-start | bytes 1572872 | tf_op jit(solution)/shard_map/ppermute | solution.py:229
  138.8 13.2 %collective-permute-start.21 = (f32[128,1024]{1,0:T(8,128)S(1)}, f32[128,1024]{1,0:T(8,128)S(1)}, u32[]{:S(2)}, u32[]{:S(2)}) collective-permute-start(f32[128,1024]{1,0:T(8,128)S(1)} %get-tuple-element.32), channel_id=1, source_target_pairs={{0,1},{1,0},{2,3},{3,2},{4,5},{5,4},{6,7},{7,6},{8,9},{9,8},{10,11... | collective-permute-start | bytes 1572872 | tf_op jit(solution)/shard_map/ppermute | solution.py:229
  141.5 15.2 %collective-permute-start.18 = (f32[128,1024]{1,0:T(8,128)S(1)}, f32[128,1024]{1,0:T(8,128)S(1)}, u32[]{:S(2)}, u32[]{:S(2)}) collective-permute-start(f32[128,1024]{1,0:T(8,128)S(1)} %get-tuple-element.30), channel_id=1, source_target_pairs={{0,1},{1,0},{2,3},{3,2},{4,5},{5,4},{6,7},{7,6},{8,9},{9,8},{10,11... | collective-permute-start | bytes 1572872 | tf_op jit(solution)/shard_map/ppermute | solution.py:229
  141.8 15.8 %collective-permute-start.28 = (s16[128,1152]{1,0:T(8,128)(2,1)S(1)}, s16[128,1152]{1,0:T(8,128)(2,1)S(1)}, u32[]{:S(2)}, u32[]{:S(2)}) collective-permute-start(s16[128,1152]{1,0:T(8,128)(2,1)S(1)} %shard_map.44), channel_id=1, source_target_pairs={{0,2},{1,3},{2,4},{3,5},{4,6},{5,7},{6,0},{7,1},{8,12},{9,13},{10,... | collective-permute-start | bytes 884744 | tf_op jit(solution)/shard_map/ppermute | solution.py:209
  146.9 16.4 %collective-permute-start.25 = (s16[128,1152]{1,0:T(8,128)(2,1)S(1)}, s16[128,1152]{1,0:T(8,128)(2,1)S(1)}, u32[]{:S(2)}, u32[]{:S(2)}) collective-permute-start(s16[128,1152]{1,0:T(8,128)(2,1)S(1)} %shard_map.42), channel_id=1, source_target_pairs={{0,4},{1,5},{2,6},{3,7},{4,0},{5,1},{6,2},{7,3},{8,14},{9,15},{10,... | collective-permute-start | bytes 884744 | tf_op jit(solution)/shard_map/ppermute | solution.py:209
  152.2 13.0 %collective-permute-start.22 = (s16[128,1152]{1,0:T(8,128)(2,1)S(1)}, s16[128,1152]{1,0:T(8,128)(2,1)S(1)}, u32[]{:S(2)}, u32[]{:S(2)}) collective-permute-start(s16[128,1152]{1,0:T(8,128)(2,1)S(1)} %shard_map.40), channel_id=1, source_target_pairs={{0,6},{1,7},{2,0},{3,1},{4,2},{5,3},{6,4},{7,5},{8,8},{9,9},{10,10... | collective-permute-start | bytes 884744 | tf_op jit(solution)/shard_map/ppermute | solution.py:209
  156.9 8.2 %collective-permute-start.19 = (s16[128,1152]{1,0:T(8,128)(2,1)S(1)}, s16[128,1152]{1,0:T(8,128)(2,1)S(1)}, u32[]{:S(2)}, u32[]{:S(2)}) collective-permute-start(s16[128,1152]{1,0:T(8,128)(2,1)S(1)} %shard_map.38), channel_id=1, source_target_pairs={{0,0},{1,1},{2,2},{3,3},{4,4},{5,5},{6,6},{7,7},{8,10},{9,11},{10,... | collective-permute-start | bytes 884744 | tf_op jit(solution)/shard_map/ppermute | solution.py:209

commit v4 on v3

--- a/solution.py
+++ b/solution.py
@@ -17,7 +17,7 @@
 AXES = ("x", "y", "z", "core")
 F32, BF16, I16, I32 = jnp.float32, jnp.bfloat16, jnp.int16, jnp.int32
 
-SENT = ((1, 0, 0, 0), (2, 2, 1, 1), (3, 3, 3, 2))
+SENT = ((1, 0, 0, 1), (3, 2, 1, 0), (2, 3, 3, 2))
 SECOND, CORE, OWNER, HALF, BASE = range(4, 9)
 
 
@@ -69,8 +69,15 @@
     return jnp.where(m[i, j] != 0, block, jnp.zeros_like(block))
 
 
-def column_kernel(s, m, density, top_a, low_a, top_b, low_b, whole):
+def column_kernel(s, m, hbm, top_a, low_a, top_b, low_b, density, whole, sem):
+    copies = []
+    for i in range(4):
+        rows = slice(i * 256, (i + 1) * 256)
+        copies.append(pltpu.make_async_copy(hbm.at[rows, :SLAB], density.at[rows], sem.at[i]))
+        copies[i].start()
     for i in range(8):
+        if i % 2 == 0:
+            copies[i // 2].wait()
         for j in range(8):
             whole[i * BLOCK : (i + 1) * BLOCK, j * BLOCK : (j + 1) * BLOCK] = masked_block(m, density, i, j)
     for i, (top, low) in enumerate(((top_a, low_a), (top_b, low_b))):
@@ -257,13 +264,16 @@
 
 def local(density, block_mask):
     s, z, core = coordinates()
-    top_a, low_a, top_b, low_b = call(
+    in_smem = pl.BlockSpec(memory_space=pltpu.SMEM)
+    top_a, low_a, top_b, low_b = pl.pallas_call(
         column_kernel,
-        [shape(512, 512, BF16)] * 4,
-        [s, block_mask],
-        density,
-        scratch=[pltpu.VMEM((SLAB, SLAB), BF16)],
-    )
+        out_shape=[shape(512, 512, BF16)] * 4,
+        in_specs=[in_smem, in_smem, pl.BlockSpec(memory_space=pltpu.HBM)],
+        out_specs=[pl.BlockSpec(memory_space=pltpu.VMEM)] * 4,
+        scratch_shapes=[pltpu.VMEM((SLAB, SLAB), BF16)] * 2 + [pltpu.SemaphoreType.DMA((4,))],
+        compiler_params=pltpu.CompilerParams(vmem_limit_bytes=16 << 20),
+        name="column",
+    )(s, block_mask, density)
     masked = call(mask_kernel, shape(SLAB, WIDE, BF16), [block_mask], density)
     near = spread_column(top_a, low_a, z, core)
     far = spread_column(top_b, low_b, z, core)
@@ -280,11 +290,15 @@
 
     parts = [across(v, d) for d in (1, 2, 3)]
     v = call(join_kernel, shape(QUARTER, WIDE + LANES, I16), [], v, *parts)
-    quarters = [along(v, lambda second, z: j - second) for j in range(4)]
+    turns = (3, 1, 2, 0)
+    quarters = []
+    for j in turns:
+        quarters.append(along(v, lambda second, z: j - second))
     came = []
-    for j, v in enumerate(quarters):
+    for j, v in zip(turns, quarters):
         mine, theirs = second_product(s, v, masked)
-        v = call(pair_kernel, shape(128, SLAB + LANES, I16), [], mine, swap(theirs))
+        theirs = swap(theirs)
+        v = call(pair_kernel, shape(128, SLAB + LANES, I16), [], mine, theirs)
         came.append(send(v, lambda x, y, z, core: (x, y, x + y + z - j, core)))
     return call(finish_kernel, shape(128, SLAB, F32), [], *came)
 

time: 169 us -> 168 us (level)
  the two profiles are of different devices: /device:TPU:0 before, /device:TPU:24 now
where the time goes in v4:
time: 168 us; the launch traced here: 167 us
  waiting for transfers between devices  93.4 us (56%)
  starting transfers between devices  43.4 us (26%)
  Pallas kernels  24.6 us (15%)
  local copies, waits for them, and re-layouts  5.06 us (3%)
    ppermute x17, waiting for transfers between devices, send(): return lax.ppermute(v, AXES, [(place(*d), place(*to(*d))) for d in DEVICES])  72 us
    ppermute x17, starting transfers between devices, send(): return lax.ppermute(v, AXES, [(place(*d), place(*to(*d))) for d in DEVICES])  31.5 us
    pallas_call x17, Pallas kernels, call(): pl.pallas_call(kernel, out_shape=out, in_specs=[pl.BlockSpec(memory_space...  23 us
    ppermute x2, waiting for transfers between devices, spread_column(): came = lax.ppermute(half, axes, [(0, 2), (1, 7)])  11.9 us
    ppermute x2, waiting for transfers between devices, spread_column(): came = lax.ppermute(half, axes, [(0, 6), (1, 3), (2, 4), (7, 5)])  8.07 us
    ppermute x2, starting transfers between devices, spread_column(): came = lax.ppermute(half, axes, [(0, 2), (1, 7)])  5.18 us
    unnamed x8, local copies, waits for them, and re-layouts  5.06 us
    ppermute x6, starting transfers between devices, swap(): return lax.ppermute(v, 'core', [(0, 1), (1, 0)])  3.58 us
  transfers between devices with their start and end apart: 29, of which 13 were waited for; matrix products, arithmetic and copies ran while one was open for 0% of the time, Pallas kernels for 12%

profile of v4, /device:TPU:24, one launch (start us, length us, event | category | flops | bytes accessed | tf_op | source)
XLA Modules:
  0.0 167.3 jit_solution(16098831657256662530)
XLA Ops:
  0.0 2.2 %copy-done = bf16[1024,2048]{1,0:T(8,128)(2,1)S(1)} copy-done((bf16[1024,2048]{1,0:T(8,128)(2,1)S(1)}, bf16[1024,2048]{1,0:T(8,128)(2,1)}, u32[]{:S(2)}) %copy-start) | copy-done | bytes 4194328
  2.2 0.7 copy-done.2
  2.9 1.7 column.1
  5.1 1.4 collective-permute-done
  6.6 3.9 %collective-permute-start.1 = (bf16[512,512]{1,0:T(8,128)(2,1)S(1)}, bf16[512,512]{1,0:T(8,128)(2,1)S(1)}, u32[]{:S(2)}, u32[]{:S(2)}) collective-permute-start(bf16[512,512]{1,0:T(8,128)(2,1)S(1)} %broadcast_select_fusion.1), channel_id=1, source_target_pairs={{0,2},{1,7},{8,10},{9,15},{16,18},{17,23},{24,26},{25,31},{32,34},... | collective-permute-start | bytes 1572872 | tf_op jit(solution)/shard_map/ppermute | solution.py:243
  10.6 1.3 collective-permute-start.5
  11.9 5.2 %collective-permute-done.1 = bf16[512,512]{1,0:T(8,128)(2,1)S(1)} collective-permute-done((bf16[512,512]{1,0:T(8,128)(2,1)S(1)}, bf16[512,512]{1,0:T(8,128)(2,1)S(1)}, u32[]{:S(2)}, u32[]{:S(2)}) %collective-permute-start.1) | collective-permute-done | bytes 524320 | tf_op jit(solution)/shard_map/ppermute | solution.py:243
  17.2 1.3 collective-permute-start.2
  18.5 6.7 %collective-permute-done.5 = bf16[512,512]{1,0:T(8,128)(2,1)S(1)} collective-permute-done((bf16[512,512]{1,0:T(8,128)(2,1)S(1)}, bf16[512,512]{1,0:T(8,128)(2,1)S(1)}, u32[]{:S(2)}, u32[]{:S(2)}) %collective-permute-start.5) | collective-permute-done | bytes 524320 | tf_op jit(solution)/shard_map/ppermute | solution.py:243
  25.3 1.3 collective-permute-start.6
  26.6 3.0 %collective-permute-done.2 = bf16[512,512]{1,0:T(8,128)(2,1)S(1)} collective-permute-done((bf16[512,512]{1,0:T(8,128)(2,1)S(1)}, bf16[512,512]{1,0:T(8,128)(2,1)S(1)}, u32[]{:S(2)}, u32[]{:S(2)}) %collective-permute-start.2) | collective-permute-done | bytes 524320 | tf_op jit(solution)/shard_map/ppermute | solution.py:245
  30.2 5.1 %collective-permute-done.6 = bf16[512,512]{1,0:T(8,128)(2,1)S(1)} collective-permute-done((bf16[512,512]{1,0:T(8,128)(2,1)S(1)}, bf16[512,512]{1,0:T(8,128)(2,1)S(1)}, u32[]{:S(2)}, u32[]{:S(2)}) %collective-permute-start.6) | collective-permute-done | bytes 524320 | tf_op jit(solution)/shard_map/ppermute | solution.py:245
  35.3 0.9 collective-permute-start.7
  36.2 2.2 %copy-done.1 = bf16[1024,2048]{1,0:T(8,128)(2,1)S(1)} copy-done((bf16[1024,2048]{1,0:T(8,128)(2,1)S(1)}, bf16[1024,2048]{1,0:T(8,128)(2,1)}, u32[]{:S(2)}) %copy-start.1) | copy-done | bytes 4194328
  38.4 1.8 %shard_map.28.refs_4_.refs_2_.masked = bf16[1024,2048]{1,0:T(8,128)(2,1)S(1)} custom-call(s32[8,16]{1,0:T(8,128)S(1)} %copy-done.3, bf16[1024,2048]{1,0:T(8,128)(2,1)S(1)} %copy-done.1), custom_call_target="tpu_custom_call" | custom-call | flops 4194304 | bytes 4194304 | tf_op jit(solution)/shard_map/pallas_call | solution.py:30
  40.2 2.2 %shard_map.30 = s16[256,2176]{1,0:T(8,128)(2,1)S(1)} custom-call(s32[16]{0:T(128)S(1)} %compare_select_fusion.8.s, bf16[512,512]{1,0:T(8,128)(2,1)S(1)} %broadcast_select_fusion.5.refs_0_, bf16[512,512]{1,0:T(8,128)(2,1)S(1)} %collective-permute-done.3.refs_1_, bf16[1024,2048]{1,0:T(8,128)(2,1)S(1)} %shard_map.28.refs_4_.refs_2_.masked), custom_call_target="tpu_custom_call" | custom-call | flops 1073741824 | bytes 4194304 | tf_op jit(solution)/shard_map/pallas_call | solution.py:30
  42.5 2.8 %collective-permute-start.8 = (s16[256,2176]{1,0:T(8,128)(2,1)S(1)}, s16[256,2176]{1,0:T(8,128)(2,1)S(1)}, u32[]{:S(2)}, u32[]{:S(2)}) collective-permute-start(s16[256,2176]{1,0:T(8,128)(2,1)S(1)} %shard_map.30), channel_id=1, source_target_pairs={{0,32},{1,9},{2,98},{3,27},{4,68},{5,21},{6,70},{7,23},{8,72},{9,1... | collective-permute-start | bytes 3342344 | tf_op jit(solution)/shard_map/ppermute | solution.py:216
  45.3 2.2 %shard_map.31 = s16[256,2176]{1,0:T(8,128)(2,1)S(1)} custom-call(s32[16]{0:T(128)S(1)} %compare_select_fusion.8.s, bf16[512,512]{1,0:T(8,128)(2,1)S(1)} %broadcast_select_fusion.5.refs_0_, bf16[512,512]{1,0:T(8,128)(2,1)S(1)} %collective-permute-done.3.refs_1_, bf16[512,512]{1,0:T(8,128)(2,1)S(1)} %broadcast_select_fusion.4.refs_2_, ...), custom_call_target="tpu_custom_call" | custom-call | flops 1073741824 | bytes 4194304 | tf_op jit(solution)/shard_map/pallas_call | solution.py:30
  47.6 2.2 %shard_map.32 = s16[256,2176]{1,0:T(8,128)(2,1)S(1)} custom-call(s32[16]{0:T(128)S(1)} %compare_select_fusion.8.s, bf16[512,512]{1,0:T(8,128)(2,1)S(1)} %broadcast_select_fusion.5.refs_0_, bf16[512,512]{1,0:T(8,128)(2,1)S(1)} %collective-permute-done.3.refs_1_, bf16[512,512]{1,0:T(8,128)(2,1)S(1)} %broadcast_select_fusion.4.refs_2_, ...), custom_call_target="tpu_custom_call" | custom-call | flops 1073741824 | bytes 4194304 | tf_op jit(solution)/shard_map/pallas_call | solution.py:30
  49.8 2.3 %collective-permute-start.10 = (s16[256,2176]{1,0:T(8,128)(2,1)S(1)}, s16[256,2176]{1,0:T(8,128)(2,1)S(1)}, u32[]{:S(2)}, u32[]{:S(2)}) collective-permute-start(s16[256,2176]{1,0:T(8,128)(2,1)S(1)} %shard_map.32), channel_id=1, source_target_pairs={{0,64},{1,17},{2,66},{3,19},{4,36},{5,13},{6,102},{7,31},{8,104},{... | collective-permute-start | bytes 3342344 | tf_op jit(solution)/shard_map/ppermute | solution.py:216
  52.2 1.9 %shard_map.29.own = f32[256,2048]{1,0:T(8,128)S(1)} custom-call(s32[16]{0:T(128)S(1)} %compare_select_fusion.8.s, bf16[512,512]{1,0:T(8,128)(2,1)S(1)} %broadcast_select_fusion.5.refs_0_, bf16[512,512]{1,0:T(8,128)(2,1)S(1)} %collective-permute-done.3.refs_1_, bf16[512,512]{1,0:T(8,128)(2,1)S(1)} %broadcast_select_fusion.4.refs_2_, ...), custom_call_target="tpu_custom_call" | custom-call | flops 1073741824 | bytes 4194304 | tf_op jit(solution)/shard_map/pallas_call | solution.py:30
  54.1 16.2 %collective-permute-done.8.a = s16[256,2176]{1,0:T(8,128)(2,1)S(1)} collective-permute-done((s16[256,2176]{1,0:T(8,128)(2,1)S(1)}, s16[256,2176]{1,0:T(8,128)(2,1)S(1)}, u32[]{:S(2)}, u32[]{:S(2)}) %collective-permute-start.8) | collective-permute-done | bytes 1114144 | tf_op jit(solution)/shard_map/ppermute | solution.py:216
  70.3 6.0 %collective-permute-done.9.b = s16[256,2176]{1,0:T(8,128)(2,1)S(1)} collective-permute-done((s16[256,2176]{1,0:T(8,128)(2,1)S(1)}, s16[256,2176]{1,0:T(8,128)(2,1)S(1)}, u32[]{:S(2)}, u32[]{:S(2)}) %collective-permute-start.9) | collective-permute-done | bytes 1114144 | tf_op jit(solution)/shard_map/ppermute | solution.py:216
  76.2 1.7 %shard_map.33 = (f32[64,2048]{1,0:T(8,128)S(1)}, s16[64,2176]{1,0:T(8,128)(2,1)S(1)}, s16[64,2176]{1,0:T(8,128)(2,1)S(1)}, s16[64,2176]{1,0:T(8,128)(2,1)S(1)}) custom-call(s32[16]{0:T(128)S(1)} %compare_select_fusion.8.s, f32[256,2048]{1,0:T(8,128)S(1)} %shard_map.29.own, s16[256,2176]{1,0:T(8,128)(2,1)S(1)} %collective-permute-done.8.a, ...), custom_call_target="tpu_custom_call" | custom-call | flops 4194304 | bytes 4194304 | tf_op jit(solution)/shard_map/pallas_call | solution.py:30
  78.3 2.0 %collective-permute-start.13 = (s16[64,2176]{1,0:T(8,128)(2,1)S(1)}, s16[64,2176]{1,0:T(8,128)(2,1)S(1)}, u32[]{:S(2)}, u32[]{:S(2)}) collective-permute-start(s16[64,2176]{1,0:T(8,128)(2,1)S(1)} %get-tuple-element.28), channel_id=1, source_target_pairs={{0,24},{1,97},{2,26},{3,99},{4,28},{5,101},{6,30},{7,103},{8,0},{9... | collective-permute-start | bytes 835592 | tf_op jit(solution)/shard_map/ppermute | solution.py:216
  80.3 6.0 %collective-permute-done.11.a = s16[64,2176]{1,0:T(8,128)(2,1)S(1)} collective-permute-done((s16[64,2176]{1,0:T(8,128)(2,1)S(1)}, s16[64,2176]{1,0:T(8,128)(2,1)S(1)}, u32[]{:S(2)}, u32[]{:S(2)}) %collective-permute-start.11) | collective-permute-done | bytes 278560 | tf_op jit(solution)/shard_map/ppermute | solution.py:216
  86.4 2.9 %collective-permute-done.13.c = s16[64,2176]{1,0:T(8,128)(2,1)S(1)} collective-permute-done((s16[64,2176]{1,0:T(8,128)(2,1)S(1)}, s16[64,2176]{1,0:T(8,128)(2,1)S(1)}, u32[]{:S(2)}, u32[]{:S(2)}) %collective-permute-start.13) | collective-permute-done | bytes 278560 | tf_op jit(solution)/shard_map/ppermute | solution.py:216
  89.7 2.1 %collective-permute-start.15 = (s16[64,2176]{1,0:T(8,128)(2,1)S(1)}, s16[64,2176]{1,0:T(8,128)(2,1)S(1)}, u32[]{:S(2)}, u32[]{:S(2)}) collective-permute-start(s16[64,2176]{1,0:T(8,128)(2,1)S(1)} %shard_map.34.refs_0_), channel_id=1, source_target_pairs={{0,16},{1,65},{2,18},{3,67},{4,20},{5,69},{6,22},{7,71},{8,24},{9,... | collective-permute-start | bytes 835592 | tf_op jit(solution)/shard_map/ppermute | solution.py:216
  91.7 1.2 collective-permute-start.14
  92.9 7.5 %collective-permute-done.16.refs_3_ = s16[64,2176]{1,0:T(8,128)(2,1)S(1)} collective-permute-done((s16[64,2176]{1,0:T(8,128)(2,1)S(1)}, s16[64,2176]{1,0:T(8,128)(2,1)S(1)}, u32[]{:S(2)}, u32[]{:S(2)}) %collective-permute-start.16) | collective-permute-done | bytes 278560 | tf_op jit(solution)/shard_map/ppermute | solution.py:216
  100.4 0.9 collective-permute-done.14.refs_1_
  101.4 1.9 %collective-permute-start.26 = (s16[256,2176]{1,0:T(8,128)(2,1)S(1)}, s16[256,2176]{1,0:T(8,128)(2,1)S(1)}, u32[]{:S(2)}, u32[]{:S(2)}) collective-permute-start(s16[256,2176]{1,0:T(8,128)(2,1)S(1)} %shard_map.35), channel_id=1, source_target_pairs={{0,0},{1,1},{2,2},{3,3},{4,4},{5,5},{6,6},{7,7},{8,104},{9,9},{10,... | collective-permute-start | bytes 3342344 | tf_op jit(solution)/shard_map/ppermute | solution.py:216
  103.3 5.1 %collective-permute-start.23 = (s16[256,2176]{1,0:T(8,128)(2,1)S(1)}, s16[256,2176]{1,0:T(8,128)(2,1)S(1)}, u32[]{:S(2)}, u32[]{:S(2)}) collective-permute-start(s16[256,2176]{1,0:T(8,128)(2,1)S(1)} %shard_map.35), channel_id=1, source_target_pairs={{0,64},{1,17},{2,66},{3,19},{4,68},{5,21},{6,70},{7,23},{8,40},{9,... | collective-permute-start | bytes 3342344 | tf_op jit(solution)/shard_map/ppermute | solution.py:216
  108.5 1.9 %collective-permute-start.20 = (s16[256,2176]{1,0:T(8,128)(2,1)S(1)}, s16[256,2176]{1,0:T(8,128)(2,1)S(1)}, u32[]{:S(2)}, u32[]{:S(2)}) collective-permute-start(s16[256,2176]{1,0:T(8,128)(2,1)S(1)} %shard_map.35), channel_id=1, source_target_pairs={{0,32},{1,9},{2,34},{3,11},{4,36},{5,13},{6,38},{7,15},{8,8},{9,17... | collective-permute-start | bytes 3342344 | tf_op jit(solution)/shard_map/ppermute | solution.py:216
  110.4 0.7 collective-permute-start.17
  111.1 20.8 %collective-permute-done.26.coded = s16[256,2176]{1,0:T(8,128)(2,1)S(1)} collective-permute-done((s16[256,2176]{1,0:T(8,128)(2,1)S(1)}, s16[256,2176]{1,0:T(8,128)(2,1)S(1)}, u32[]{:S(2)}, u32[]{:S(2)}) %collective-permute-start.26) | collective-permute-done | bytes 1114144 | tf_op jit(solution)/shard_map/ppermute | solution.py:216
  131.9 2.2 %shard_map.42 = (f32[128,1024]{1,0:T(8,128)S(1)}, f32[128,1024]{1,0:T(8,128)S(1)}) custom-call(s32[16]{0:T(128)S(1)} %compare_select_fusion.8.s, s16[256,2176]{1,0:T(8,128)(2,1)S(1)} %collective-permute-done.26.coded, bf16[1024,2048]{1,0:T(8,128)(2,1)S(1)} %shard_map.28.refs_4_.refs_2_.masked), custom_call_target="tpu_custom_call" | custom-call | flops 1073741824 | bytes 4194304 | tf_op jit(solution)/shard_map/pallas_call | solution.py:30
  134.2 2.2 %shard_map.40 = (f32[128,1024]{1,0:T(8,128)S(1)}, f32[128,1024]{1,0:T(8,128)S(1)}) custom-call(s32[16]{0:T(128)S(1)} %compare_select_fusion.8.s, s16[256,2176]{1,0:T(8,128)(2,1)S(1)} %collective-permute-done.23.coded, bf16[1024,2048]{1,0:T(8,128)(2,1)S(1)} %shard_map.28.refs_4_.refs_2_.masked), custom_call_target="tpu_custom_call" | custom-call | flops 1073741824 | bytes 4194304 | tf_op jit(solution)/shard_map/pallas_call | solution.py:30
  136.4 1.0 collective-permute-start.24
  137.4 2.2 %shard_map.38 = (f32[128,1024]{1,0:T(8,128)S(1)}, f32[128,1024]{1,0:T(8,128)S(1)}) custom-call(s32[16]{0:T(128)S(1)} %compare_select_fusion.8.s, s16[256,2176]{1,0:T(8,128)(2,1)S(1)} %collective-permute-done.20.coded, bf16[1024,2048]{1,0:T(8,128)(2,1)S(1)} %shard_map.28.refs_4_.refs_2_.masked), custom_call_target="tpu_custom_call" | custom-call | flops 1073741824 | bytes 4194304 | tf_op jit(solution)/shard_map/pallas_call | solution.py:30
  140.1 2.2 %shard_map.36 = (f32[128,1024]{1,0:T(8,128)S(1)}, f32[128,1024]{1,0:T(8,128)S(1)}) custom-call(s32[16]{0:T(128)S(1)} %compare_select_fusion.8.s, s16[256,2176]{1,0:T(8,128)(2,1)S(1)} %collective-permute-done.17.coded, bf16[1024,2048]{1,0:T(8,128)(2,1)S(1)} %shard_map.28.refs_4_.refs_2_.masked), custom_call_target="tpu_custom_call" | custom-call | flops 1073741824 | bytes 4194304 | tf_op jit(solution)/shard_map/pallas_call | solution.py:30
  142.3 0.6 collective-permute-start.18
  143.0 4.9 %collective-permute-start.28 = (s16[128,1152]{1,0:T(8,128)(2,1)S(1)}, s16[128,1152]{1,0:T(8,128)(2,1)S(1)}, u32[]{:S(2)}, u32[]{:S(2)}) collective-permute-start(s16[128,1152]{1,0:T(8,128)(2,1)S(1)} %shard_map.43), channel_id=1, source_target_pairs={{0,0},{1,1},{2,2},{3,3},{4,4},{5,5},{6,6},{7,7},{8,10},{9,11},{10,... | collective-permute-start | bytes 884744 | tf_op jit(solution)/shard_map/ppermute | solution.py:216
  148.1 1.9 %collective-permute-start.25 = (s16[128,1152]{1,0:T(8,128)(2,1)S(1)}, s16[128,1152]{1,0:T(8,128)(2,1)S(1)}, u32[]{:S(2)}, u32[]{:S(2)}) collective-permute-start(s16[128,1152]{1,0:T(8,128)(2,1)S(1)} %shard_map.41), channel_id=1, source_target_pairs={{0,4},{1,5},{2,6},{3,7},{4,0},{5,1},{6,2},{7,3},{8,14},{9,15},{10,... | collective-permute-start | bytes 884744 | tf_op jit(solution)/shard_map/ppermute | solution.py:216
  150.2 3.4 %collective-permute-start.22 = (s16[128,1152]{1,0:T(8,128)(2,1)S(1)}, s16[128,1152]{1,0:T(8,128)(2,1)S(1)}, u32[]{:S(2)}, u32[]{:S(2)}) collective-permute-start(s16[128,1152]{1,0:T(8,128)(2,1)S(1)} %shard_map.39), channel_id=1, source_target_pairs={{0,6},{1,7},{2,0},{3,1},{4,2},{5,3},{6,4},{7,5},{8,8},{9,9},{10,10... | collective-permute-start | bytes 884744 | tf_op jit(solution)/shard_map/ppermute | solution.py:216
  153.8 0.7 collective-permute-start.19
  154.5 11.7 %collective-permute-done.25.c = s16[128,1152]{1,0:T(8,128)(2,1)S(1)} collective-permute-done((s16[128,1152]{1,0:T(8,128)(2,1)S(1)}, s16[128,1152]{1,0:T(8,128)(2,1)S(1)}, u32[]{:S(2)}, u32[]{:S(2)}) %collective-permute-start.25) | collective-permute-done | bytes 294944 | tf_op jit(solution)/shard_map/ppermute | solution.py:216
  166.2 1.1 shard_map.44
  (43 shorter events, 3.8 us)
Async XLA Ops:
  0.0 2.2 %copy-start = (bf16[1024,2048]{1,0:T(8,128)(2,1)S(1)}, bf16[1024,2048]{1,0:T(8,128)(2,1)}, u32[]{:S(2)}) copy-start(bf16[1024,2048]{1,0:T(8,128)(2,1)} %density.1) | copy-start | bytes 12582916
  2.2 0.7 copy-start.2
  4.6 2.0 %collective-permute-start = (bf16[512,512]{1,0:T(8,128)(2,1)S(1)}, bf16[512,512]{1,0:T(8,128)(2,1)S(1)}, u32[]{:S(2)}, u32[]{:S(2)}) collective-permute-start(bf16[512,512]{1,0:T(8,128)(2,1)S(1)} %get-tuple-element.22), channel_id=1, source_target_pairs={{0,1},{1,0},{2,3},{3,2},{4,5},{5,4},{6,7},{7,6},{8,9},{9,8},{10,11... | collective-permute-start | bytes 1572872 | tf_op jit(solution)/shard_map/ppermute | solution.py:240
  4.6 5.8 %collective-permute-start.4 = (bf16[512,512]{1,0:T(8,128)(2,1)S(1)}, bf16[512,512]{1,0:T(8,128)(2,1)S(1)}, u32[]{:S(2)}, u32[]{:S(2)}) collective-permute-start(bf16[512,512]{1,0:T(8,128)(2,1)S(1)} %get-tuple-element.24), channel_id=1, source_target_pairs={{0,1},{1,0},{2,3},{3,2},{4,5},{5,4},{6,7},{7,6},{8,9},{9,8},{10,11... | collective-permute-start | bytes 1572872 | tf_op jit(solution)/shard_map/ppermute | solution.py:240
  6.6 10.5 %collective-permute-start.1 = (bf16[512,512]{1,0:T(8,128)(2,1)S(1)}, bf16[512,512]{1,0:T(8,128)(2,1)S(1)}, u32[]{:S(2)}, u32[]{:S(2)}) collective-permute-start(bf16[512,512]{1,0:T(8,128)(2,1)S(1)} %broadcast_select_fusion.1), channel_id=1, source_target_pairs={{0,2},{1,7},{8,10},{9,15},{16,18},{17,23},{24,26},{25,31},{32,34},... | collective-permute-start | bytes 1572872 | tf_op jit(solution)/shard_map/ppermute | solution.py:243
  10.6 14.7 %collective-permute-start.5 = (bf16[512,512]{1,0:T(8,128)(2,1)S(1)}, bf16[512,512]{1,0:T(8,128)(2,1)S(1)}, u32[]{:S(2)}, u32[]{:S(2)}) collective-permute-start(bf16[512,512]{1,0:T(8,128)(2,1)S(1)} %broadcast_select_fusion), channel_id=1, source_target_pairs={{0,2},{1,7},{8,10},{9,15},{16,18},{17,23},{24,26},{25,31},{32,34},... | collective-permute-start | bytes 1572872 | tf_op jit(solution)/shard_map/ppermute | solution.py:243
  17.2 12.5 %collective-permute-start.2 = (bf16[512,512]{1,0:T(8,128)(2,1)S(1)}, bf16[512,512]{1,0:T(8,128)(2,1)S(1)}, u32[]{:S(2)}, u32[]{:S(2)}) collective-permute-start(bf16[512,512]{1,0:T(8,128)(2,1)S(1)} %broadcast_select_fusion.3), channel_id=1, source_target_pairs={{0,6},{1,3},{2,4},{7,5},{8,14},{9,11},{10,12},{15,13},{16,22},{17,... | collective-permute-start | bytes 1572872 | tf_op jit(solution)/shard_map/ppermute | solution.py:245
  25.3 10.0 %collective-permute-start.6 = (bf16[512,512]{1,0:T(8,128)(2,1)S(1)}, bf16[512,512]{1,0:T(8,128)(2,1)S(1)}, u32[]{:S(2)}, u32[]{:S(2)}) collective-permute-start(bf16[512,512]{1,0:T(8,128)(2,1)S(1)} %broadcast_select_fusion.2), channel_id=1, source_target_pairs={{0,6},{1,3},{2,4},{7,5},{8,14},{9,11},{10,12},{15,13},{16,22},{17,... | collective-permute-start | bytes 1572872 | tf_op jit(solution)/shard_map/ppermute | solution.py:245
  29.7 6.5 %copy-start.3 = (s32[8,16]{1,0:T(8,128)S(1)}, s32[8,16]{1,0:T(8,128)}, u32[]{:S(2)}) copy-start(s32[8,16]{1,0:T(8,128)} %m.3) | copy-start | bytes 1540
  29.7 10.5 %collective-permute-start.3 = (bf16[512,512]{1,0:T(8,128)(2,1)S(1)}, bf16[512,512]{1,0:T(8,128)(2,1)S(1)}, u32[]{:S(2)}, u32[]{:S(2)}) collective-permute-start(bf16[512,512]{1,0:T(8,128)(2,1)S(1)} %broadcast_select_fusion.5.refs_0_), channel_id=1, source_target_pairs={{0,1},{1,0},{2,3},{3,2},{4,5},{5,4},{6,7},{7,6},{8,9},{9,8},{10,11... | collective-permute-start | bytes 1572872 | tf_op jit(solution)/shard_map/ppermute | solution.py:236
  35.3 10.0 %collective-permute-start.7 = (bf16[512,512]{1,0:T(8,128)(2,1)S(1)}, bf16[512,512]{1,0:T(8,128)(2,1)S(1)}, u32[]{:S(2)}, u32[]{:S(2)}) collective-permute-start(bf16[512,512]{1,0:T(8,128)(2,1)S(1)} %broadcast_select_fusion.4.refs_2_), channel_id=1, source_target_pairs={{0,1},{1,0},{2,3},{3,2},{4,5},{5,4},{6,7},{7,6},{8,9},{9,8},{10,11... | collective-permute-start | bytes 1572872 | tf_op jit(solution)/shard_map/ppermute | solution.py:236
  36.2 2.2 %copy-start.1 = (bf16[1024,2048]{1,0:T(8,128)(2,1)S(1)}, bf16[1024,2048]{1,0:T(8,128)(2,1)}, u32[]{:S(2)}) copy-start(bf16[1024,2048]{1,0:T(8,128)(2,1)} %density.1) | copy-start | bytes 12582916
  42.5 27.8 %collective-permute-start.8 = (s16[256,2176]{1,0:T(8,128)(2,1)S(1)}, s16[256,2176]{1,0:T(8,128)(2,1)S(1)}, u32[]{:S(2)}, u32[]{:S(2)}) collective-permute-start(s16[256,2176]{1,0:T(8,128)(2,1)S(1)} %shard_map.30), channel_id=1, source_target_pairs={{0,32},{1,9},{2,98},{3,27},{4,68},{5,21},{6,70},{7,23},{8,72},{9,1... | collective-permute-start | bytes 3342344 | tf_op jit(solution)/shard_map/ppermute | solution.py:216
  47.5 28.7 %collective-permute-start.9 = (s16[256,2176]{1,0:T(8,128)(2,1)S(1)}, s16[256,2176]{1,0:T(8,128)(2,1)S(1)}, u32[]{:S(2)}, u32[]{:S(2)}) collective-permute-start(s16[256,2176]{1,0:T(8,128)(2,1)S(1)} %shard_map.31), channel_id=1, source_target_pairs={{0,96},{1,25},{2,34},{3,11},{4,100},{5,29},{6,38},{7,15},{8,40},{9... | collective-permute-start | bytes 3342344 | tf_op jit(solution)/shard_map/ppermute | solution.py:216
  49.8 26.4 %collective-permute-start.10 = (s16[256,2176]{1,0:T(8,128)(2,1)S(1)}, s16[256,2176]{1,0:T(8,128)(2,1)S(1)}, u32[]{:S(2)}, u32[]{:S(2)}) collective-permute-start(s16[256,2176]{1,0:T(8,128)(2,1)S(1)} %shard_map.32), channel_id=1, source_target_pairs={{0,64},{1,17},{2,66},{3,19},{4,36},{5,13},{6,102},{7,31},{8,104},{... | collective-permute-start | bytes 3342344 | tf_op jit(solution)/shard_map/ppermute | solution.py:216
  77.9 8.4 %collective-permute-start.11 = (s16[64,2176]{1,0:T(8,128)(2,1)S(1)}, s16[64,2176]{1,0:T(8,128)(2,1)S(1)}, u32[]{:S(2)}, u32[]{:S(2)}) collective-permute-start(s16[64,2176]{1,0:T(8,128)(2,1)S(1)} %get-tuple-element.26), channel_id=1, source_target_pairs={{0,16},{1,65},{2,18},{3,67},{4,20},{5,69},{6,22},{7,71},{8,24},{9,... | collective-permute-start | bytes 835592 | tf_op jit(solution)/shard_map/ppermute | solution.py:216
  78.2 8.1 %collective-permute-start.12 = (s16[64,2176]{1,0:T(8,128)(2,1)S(1)}, s16[64,2176]{1,0:T(8,128)(2,1)S(1)}, u32[]{:S(2)}, u32[]{:S(2)}) collective-permute-start(s16[64,2176]{1,0:T(8,128)(2,1)S(1)} %get-tuple-element.27), channel_id=1, source_target_pairs={{0,8},{1,33},{2,10},{3,35},{4,12},{5,37},{6,14},{7,39},{8,16},{9,4... | collective-permute-start | bytes 835592 | tf_op jit(solution)/shard_map/ppermute | solution.py:216
  78.3 10.9 %collective-permute-start.13 = (s16[64,2176]{1,0:T(8,128)(2,1)S(1)}, s16[64,2176]{1,0:T(8,128)(2,1)S(1)}, u32[]{:S(2)}, u32[]{:S(2)}) collective-permute-start(s16[64,2176]{1,0:T(8,128)(2,1)S(1)} %get-tuple-element.28), channel_id=1, source_target_pairs={{0,24},{1,97},{2,26},{3,99},{4,28},{5,101},{6,30},{7,103},{8,0},{9... | collective-permute-start | bytes 835592 | tf_op jit(solution)/shard_map/ppermute | solution.py:216
  89.6 10.8 %collective-permute-start.16 = (s16[64,2176]{1,0:T(8,128)(2,1)S(1)}, s16[64,2176]{1,0:T(8,128)(2,1)S(1)}, u32[]{:S(2)}, u32[]{:S(2)}) collective-permute-start(s16[64,2176]{1,0:T(8,128)(2,1)S(1)} %shard_map.34.refs_0_), channel_id=1, source_target_pairs={{0,24},{1,97},{2,26},{3,99},{4,28},{5,101},{6,30},{7,103},{8,0},{9... | collective-permute-start | bytes 835592 | tf_op jit(solution)/shard_map/ppermute | solution.py:216
  89.7 10.7 %collective-permute-start.15 = (s16[64,2176]{1,0:T(8,128)(2,1)S(1)}, s16[64,2176]{1,0:T(8,128)(2,1)S(1)}, u32[]{:S(2)}, u32[]{:S(2)}) collective-permute-start(s16[64,2176]{1,0:T(8,128)(2,1)S(1)} %shard_map.34.refs_0_), channel_id=1, source_target_pairs={{0,16},{1,65},{2,18},{3,67},{4,20},{5,69},{6,22},{7,71},{8,24},{9,... | collective-permute-start | bytes 835592 | tf_op jit(solution)/shard_map/ppermute | solution.py:216
  91.7 9.6 %collective-permute-start.14 = (s16[64,2176]{1,0:T(8,128)(2,1)S(1)}, s16[64,2176]{1,0:T(8,128)(2,1)S(1)}, u32[]{:S(2)}, u32[]{:S(2)}) collective-permute-start(s16[64,2176]{1,0:T(8,128)(2,1)S(1)} %shard_map.34.refs_0_), channel_id=1, source_target_pairs={{0,8},{1,33},{2,10},{3,35},{4,12},{5,37},{6,14},{7,39},{8,16},{9,4... | collective-permute-start | bytes 835592 | tf_op jit(solution)/shard_map/ppermute | solution.py:216
  101.4 30.5 %collective-permute-start.26 = (s16[256,2176]{1,0:T(8,128)(2,1)S(1)}, s16[256,2176]{1,0:T(8,128)(2,1)S(1)}, u32[]{:S(2)}, u32[]{:S(2)}) collective-permute-start(s16[256,2176]{1,0:T(8,128)(2,1)S(1)} %shard_map.35), channel_id=1, source_target_pairs={{0,0},{1,1},{2,2},{3,3},{4,4},{5,5},{6,6},{7,7},{8,104},{9,9},{10,... | collective-permute-start | bytes 3342344 | tf_op jit(solution)/shard_map/ppermute | solution.py:216
  103.3 30.9 %collective-permute-start.23 = (s16[256,2176]{1,0:T(8,128)(2,1)S(1)}, s16[256,2176]{1,0:T(8,128)(2,1)S(1)}, u32[]{:S(2)}, u32[]{:S(2)}) collective-permute-start(s16[256,2176]{1,0:T(8,128)(2,1)S(1)} %shard_map.35), channel_id=1, source_target_pairs={{0,64},{1,17},{2,66},{3,19},{4,68},{5,21},{6,70},{7,23},{8,40},{9,... | collective-permute-start | bytes 3342344 | tf_op jit(solution)/shard_map/ppermute | solution.py:216
  108.5 28.9 %collective-permute-start.20 = (s16[256,2176]{1,0:T(8,128)(2,1)S(1)}, s16[256,2176]{1,0:T(8,128)(2,1)S(1)}, u32[]{:S(2)}, u32[]{:S(2)}) collective-permute-start(s16[256,2176]{1,0:T(8,128)(2,1)S(1)} %shard_map.35), channel_id=1, source_target_pairs={{0,32},{1,9},{2,34},{3,11},{4,36},{5,13},{6,38},{7,15},{8,8},{9,17... | collective-permute-start | bytes 3342344 | tf_op jit(solution)/shard_map/ppermute | solution.py:216
  110.4 29.7 %collective-permute-start.17 = (s16[256,2176]{1,0:T(8,128)(2,1)S(1)}, s16[256,2176]{1,0:T(8,128)(2,1)S(1)}, u32[]{:S(2)}, u32[]{:S(2)}) collective-permute-start(s16[256,2176]{1,0:T(8,128)(2,1)S(1)} %shard_map.35), channel_id=1, source_target_pairs={{0,96},{1,25},{2,98},{3,27},{4,100},{5,29},{6,102},{7,31},{8,72},{... | collective-permute-start | bytes 3342344 | tf_op jit(solution)/shard_map/ppermute | solution.py:216
  134.1 8.7 %collective-permute-start.27 = (f32[128,1024]{1,0:T(8,128)S(1)}, f32[128,1024]{1,0:T(8,128)S(1)}, u32[]{:S(2)}, u32[]{:S(2)}) collective-permute-start(f32[128,1024]{1,0:T(8,128)S(1)} %get-tuple-element.36), channel_id=1, source_target_pairs={{0,1},{1,0},{2,3},{3,2},{4,5},{5,4},{6,7},{7,6},{8,9},{9,8},{10,11... | collective-permute-start | bytes 1572872 | tf_op jit(solution)/shard_map/ppermute | solution.py:236
  136.4 11.5 %collective-permute-start.24 = (f32[128,1024]{1,0:T(8,128)S(1)}, f32[128,1024]{1,0:T(8,128)S(1)}, u32[]{:S(2)}, u32[]{:S(2)}) collective-permute-start(f32[128,1024]{1,0:T(8,128)S(1)} %get-tuple-element.34), channel_id=1, source_target_pairs={{0,1},{1,0},{2,3},{3,2},{4,5},{5,4},{6,7},{7,6},{8,9},{9,8},{10,11... | collective-permute-start | bytes 1572872 | tf_op jit(solution)/shard_map/ppermute | solution.py:236
  139.5 10.5 %collective-permute-start.21 = (f32[128,1024]{1,0:T(8,128)S(1)}, f32[128,1024]{1,0:T(8,128)S(1)}, u32[]{:S(2)}, u32[]{:S(2)}) collective-permute-start(f32[128,1024]{1,0:T(8,128)S(1)} %get-tuple-element.32), channel_id=1, source_target_pairs={{0,1},{1,0},{2,3},{3,2},{4,5},{5,4},{6,7},{7,6},{8,9},{9,8},{10,11... | collective-permute-start | bytes 1572872 | tf_op jit(solution)/shard_map/ppermute | solution.py:236
  142.3 11.4 %collective-permute-start.18 = (f32[128,1024]{1,0:T(8,128)S(1)}, f32[128,1024]{1,0:T(8,128)S(1)}, u32[]{:S(2)}, u32[]{:S(2)}) collective-permute-start(f32[128,1024]{1,0:T(8,128)S(1)} %get-tuple-element.30), channel_id=1, source_target_pairs={{0,1},{1,0},{2,3},{3,2},{4,5},{5,4},{6,7},{7,6},{8,9},{9,8},{10,11... | collective-permute-start | bytes 1572872 | tf_op jit(solution)/shard_map/ppermute | solution.py:236
  143.0 11.5 %collective-permute-start.28 = (s16[128,1152]{1,0:T(8,128)(2,1)S(1)}, s16[128,1152]{1,0:T(8,128)(2,1)S(1)}, u32[]{:S(2)}, u32[]{:S(2)}) collective-permute-start(s16[128,1152]{1,0:T(8,128)(2,1)S(1)} %shard_map.43), channel_id=1, source_target_pairs={{0,0},{1,1},{2,2},{3,3},{4,4},{5,5},{6,6},{7,7},{8,10},{9,11},{10,... | collective-permute-start | bytes 884744 | tf_op jit(solution)/shard_map/ppermute | solution.py:216
  148.1 18.1 %collective-permute-start.25 = (s16[128,1152]{1,0:T(8,128)(2,1)S(1)}, s16[128,1152]{1,0:T(8,128)(2,1)S(1)}, u32[]{:S(2)}, u32[]{:S(2)}) collective-permute-start(s16[128,1152]{1,0:T(8,128)(2,1)S(1)} %shard_map.41), channel_id=1, source_target_pairs={{0,4},{1,5},{2,6},{3,7},{4,0},{5,1},{6,2},{7,3},{8,14},{9,15},{10,... | collective-permute-start | bytes 884744 | tf_op jit(solution)/shard_map/ppermute | solution.py:216
  150.2 16.0 %collective-permute-start.22 = (s16[128,1152]{1,0:T(8,128)(2,1)S(1)}, s16[128,1152]{1,0:T(8,128)(2,1)S(1)}, u32[]{:S(2)}, u32[]{:S(2)}) collective-permute-start(s16[128,1152]{1,0:T(8,128)(2,1)S(1)} %shard_map.39), channel_id=1, source_target_pairs={{0,6},{1,7},{2,0},{3,1},{4,2},{5,3},{6,4},{7,5},{8,8},{9,9},{10,10... | collective-permute-start | bytes 884744 | tf_op jit(solution)/shard_map/ppermute | solution.py:216
  153.8 12.4 %collective-permute-start.19 = (s16[128,1152]{1,0:T(8,128)(2,1)S(1)}, s16[128,1152]{1,0:T(8,128)(2,1)S(1)}, u32[]{:S(2)}, u32[]{:S(2)}) collective-permute-start(s16[128,1152]{1,0:T(8,128)(2,1)S(1)} %shard_map.37), channel_id=1, source_target_pairs={{0,2},{1,3},{2,4},{3,5},{4,6},{5,7},{6,0},{7,1},{8,12},{9,13},{10,... | collective-permute-start | bytes 884744 | tf_op jit(solution)/shard_map/ppermute | solution.py:216
